TPU v7x, 32 devices: a whole 2x2x4 slice. The times are simulated.
32 devices in a mesh: sub: 8 (over y, x, core), coarse: 4 (over z).
Axes of the slice: x: 2, y: 2, z: 4, core: 2. Of those that a mesh axis runs over, the one named last changes fastest.
Arguments:
- right_side: float32 [8, 4, 128, 128], P('sub', 'coarse'), may hold values from -150 to 150
- diagonal: float32 [8, 4, 128, 128], P('sub', 'coarse'), may hold values from 2 to 8
- cell_link: float32 [8, 4, 128, 128], P('sub', 'coarse'), may hold values from 0.2 to 0.9
- block_inverse: float32 [8, 4, 128, 128, 128], P('sub', 'coarse'), may hold values from -1 to 1
- coupling: float32 [8, 4, 4, 128, 128], P('sub', 'coarse'), may hold values from -0.26516503 to 0.26516503
- coarse_basis: float32 [8, 4, 128, 128], P('sub', 'coarse'), may hold values from -6 to 6
- coarse_inverse: float32 [512, 512], P('coarse'), may hold values from -0.25 to 0.25
- partner: int32 [8, 4], P('sub'), may hold values from 0 to 7, as said below
- margin_width: int32 [8, 4], P('sub'), may hold values from 4 to 8, as said below
- margin_blocks: int32 [8, 4, 4, 8], P('sub', 'coarse'), may hold values from 0 to 127
- aggregate: int32 [8, 4, 128], P('sub', 'coarse'), may hold values from 0 to 511, as said below
Outputs:
- solution: float32 [8, 4, 128, 128], P('sub', 'coarse')
Inputs may be any that keep to these rules, and one draw needn't show every extreme that they name: partner[s, r] differs from s, partner[partner[s, r], r] = s, and the 4 partners of one subdomain are distinct. margin_width[partner[s, r], r] = margin_width[s, r]; every colour round has a pair with width 8. `margin_blocks`: entries with w >= margin_width[s, r] are not used. aggregate[s, c, b] lies in (s * 4 + c) * 16 to (s * 4 + c + 1) * 16 - 1, and every one of these 16 aggregates has a block of part [s, c].
All inputs are finite; a program needn't handle non-finite values.
Results may differ from a plain program's by a relative error of at most 0.0003.
Values sent between devices are 32-bit elements; how exact they have to be, the bound alone decides.
No kernel may reach another device: no remote copies, remote signals or barrier semaphores. Data moves between devices by JAX's collectives and lax.ppermute only.
A program may use at most 64 MiB of HBM per device.

v0:
```python
import jax
import jax.numpy as jnp
from jax import lax
from jax.sharding import PartitionSpec as P

BS = 128
BPD = 128
AGG_DEV = 16
ITERS = 4


def givens_solve(columns, beta):
    steps_count = len(columns)
    cosines = []
    sines = []
    side_terms = [beta] + [jnp.zeros_like(beta) for unused in range(steps_count)]
    triangle = []
    for column_id in range(steps_count):
        column = list(columns[column_id])
        for row_id in range(column_id):
            upper = column[row_id]
            lower = column[row_id + 1]
            column[row_id] = cosines[row_id] * upper + sines[row_id] * lower
            column[row_id + 1] = cosines[row_id] * lower - sines[row_id] * upper
        upper = column[column_id]
        lower = column[column_id + 1]
        radius = jnp.sqrt(upper * upper + lower * lower)
        cosine = upper / radius
        sine_value = lower / radius
        column[column_id] = radius
        cosines.append(cosine)
        sines.append(sine_value)
        side_terms[column_id + 1] = -sine_value * side_terms[column_id]
        side_terms[column_id] = cosine * side_terms[column_id]
        triangle.append(column)
    weights = [None] * steps_count
    for column_id in reversed(range(steps_count)):
        running = side_terms[column_id]
        for later_col in range(column_id + 1, steps_count):
            running = running - triangle[later_col][column_id] * weights[later_col]
        weights[column_id] = running / triangle[column_id][column_id]
    return weights


def on_device(
    right_side,
    diagonal,
    cell_link,
    block_inverse,
    coupling,
    coarse_basis,
    coarse_inverse,
    partner,
    margin_width,
    margin_blocks,
    aggregate,
):
    highest = lax.Precision.HIGHEST
    block_count = right_side.shape[2]
    unknowns = right_side.shape[3]
    factor = (BS * BPD / AGG_DEV) ** (-0.5)
    inverse_blocks = block_inverse[0, 0]
    couplings = coupling[0, 0]
    basis_local = coarse_basis[0, 0]
    diagonal_local = diagonal[0, 0]
    link_local = cell_link[0, 0]
    paired = partner[0]
    widths = margin_width[0]
    blocks = margin_blocks[0, 0]
    member_of = aggregate[0, 0]
    aggregate_count = coarse_inverse.shape[1]
    member_table = (member_of[:, None] == jnp.arange(aggregate_count)[None, :]).astype(jnp.float32)
    rounds = blocks.shape[0]
    widest = blocks.shape[1]
    target = (blocks.reshape(-1)[:, None] == jnp.arange(block_count)[None, :]).astype(jnp.float32)
    live_mask = (jnp.arange(widest)[None, :] < widths[:, None]).astype(jnp.float32)

    def margin(values):
        outgoing = jnp.take(values, blocks.reshape(-1), axis=0).reshape(rounds, widest, unknowns)
        pieces = []
        for round_id in range(rounds):
            gathered = lax.all_gather(outgoing[round_id], "sub", axis=0, tiled=True)
            pieces.append(lax.dynamic_slice_in_dim(gathered, paired[round_id] * widest, widest, 0))
        incoming = jnp.stack(pieces)
        mapped = (
            jnp.einsum("rij,rwj->rwi", couplings, incoming, precision=highest)
            * live_mask[:, :, None]
        )
        return jnp.einsum(
            "kb,ki->bi", target, mapped.reshape(rounds * widest, unknowns), precision=highest
        )

    def squared_norm(values):
        return lax.psum(jnp.sum(values * values), ("sub", "coarse"))

    start_vector = right_side[0, 0]
    directions = []
    columns = []
    beta = jnp.sqrt(squared_norm(start_vector))
    basis_list = [start_vector / beta]
    for krylov_step in range(ITERS):
        current = basis_list[-1]
        inner = jnp.sum(basis_local * current, axis=1)
        restricted = lax.psum(
            jnp.dot(inner, member_table, precision=highest) * factor, ("sub", "coarse")
        )
        local_part = jnp.einsum(
            "bij,bj->bi", inverse_blocks, current + margin(current), precision=highest
        )
        coarse_part = jnp.dot(coarse_inverse, restricted, precision=highest)
        coarse_full = lax.all_gather(coarse_part, "coarse", axis=0, tiled=True)
        prolonged = jnp.dot(member_table, coarse_full, precision=highest)
        direction = local_part + prolonged[:, None] * basis_local
        directions.append(direction)
        flat_line = direction.reshape(-1)
        link_line = link_local.reshape(-1)
        zero_pad = jnp.zeros((1,), jnp.float32)
        ahead_terms = jnp.concatenate([flat_line[1:], zero_pad]) * link_line
        behind_terms = jnp.concatenate([zero_pad, (link_line * flat_line)[:-1]])
        product = (
            diagonal_local * direction
            - (ahead_terms + behind_terms).reshape(direction.shape)
            - margin(direction)
        )
        projected = lax.psum(
            jnp.stack([jnp.sum(vector * product) for vector in basis_list]), ("sub", "coarse")
        )
        for position in range(len(basis_list)):
            product = product - projected[position] * basis_list[position]
        norm_new = jnp.sqrt(squared_norm(product))
        columns.append([projected[position] for position in range(len(basis_list))] + [norm_new])
        basis_list.append(product / norm_new)
    weights = givens_solve(columns, beta)
    solution = weights[0] * directions[0]
    for position in range(1, ITERS):
        solution = solution + weights[position] * directions[position]
    return solution.reshape(right_side.shape)


def solution(mesh):
    placed = (
        P("sub", "coarse", None, None),
        P("sub", "coarse", None, None),
        P("sub", "coarse", None, None),
        P("sub", "coarse", None, None, None),
        P("sub", "coarse", None, None, None),
        P("sub", "coarse", None, None),
        P("coarse", None),
        P("sub", None),
        P("sub", None),
        P("sub", "coarse", None, None),
        P("sub", "coarse", None),
    )
    return jax.shard_map(
        on_device,
        mesh=mesh,
        in_specs=placed,
        out_specs=P("sub", "coarse", None, None),
        check_vma=False,
    )
```

profile of v0, /device:TPU:0, one launch (start us, length us, event | category | flops | bytes accessed | tf_op | source)
XLA Modules:
  0.0 959.3 jit_solution(15861982066872133460)
XLA Ops:
  2.3 42.2 %psum.91 = f32[]{:T(128)} all-reduce(f32[]{:T(128)} %multiply_reduce_fusion.14), channel_id=1, replica_groups=mesh['sub'=8,'coarse'=4] {'sub','coarse'}, use_global_device_ids=true, to_apply=%region_1.0 | all-reduce | flops 1 | bytes 8 | tf_op jit(solution)/shard_map/psum | solution.py:94
  46.9 10.0 %all_gather.108 = f32[64,128]{1,0:T(8,128)S(1)} all-gather(f32[8,128]{1,0:T(8,128)S(1)} %get-tuple-element.63), channel_id=1, replica_groups=mesh['sub'=8,'coarse'=4] {'sub'}, dimensions={0}, use_global_device_ids=true | all-gather | bytes 36864 | tf_op jit(solution)/shard_map/all_gather | solution.py:82
  87.8 15.4 %fusion.6 = f32[128,1,128]{2,1,0:T(1,128)S(1)} fusion(f32[128,128,1]{1,2,0:T(1,128)S(1)} %bitcast.355, f32[1,1,128,128,128]{4,3,2,1,0:T(8,128)} %param.16), kind=kOutput, calls=%fused_computation.14 | convolution fusion | flops 25165824 | bytes 8519680 | tf_op jit(solution)/shard_map/bij,bj->bi/dot_general | solution.py:107
  103.5 39.4 %psum.92 = f32[512]{0:T(512)S(1)} all-reduce(f32[512]{0:T(512)S(1)} %broadcast_multiply_fusion.3), channel_id=1, replica_groups=mesh['sub'=8,'coarse'=4] {'sub','coarse'}, use_global_device_ids=true, to_apply=%region_3.5 | all-reduce | flops 512 | bytes 4096 | tf_op jit(solution)/shard_map/psum | solution.py:104
  153.9 9.8 %all_gather.113 = f32[64,128]{1,0:T(8,128)S(1)} all-gather(f32[8,128]{1,0:T(8,128)S(1)} %get-tuple-element.59), channel_id=1, replica_groups=mesh['sub'=8,'coarse'=4] {'sub'}, dimensions={0}, use_global_device_ids=true | all-gather | bytes 36864 | tf_op jit(solution)/shard_map/all_gather | solution.py:82
  191.5 38.1 %psum.93 = f32[]{:T(128)} all-reduce(f32[]{:T(128)} %get-tuple-element.80), channel_id=1, replica_groups=mesh['sub'=8,'coarse'=4] {'sub','coarse'}, use_global_device_ids=true, to_apply=%region_5.7 | all-reduce | flops 1 | bytes 8 | tf_op jit(solution)/shard_map/psum | solution.py:125
  230.9 41.2 %psum.94 = f32[]{:T(128)} all-reduce(f32[]{:T(128)} %multiply_reduce_fusion.12), channel_id=1, replica_groups=mesh['sub'=8,'coarse'=4] {'sub','coarse'}, use_global_device_ids=true, to_apply=%region_7.9 | all-reduce | flops 1 | bytes 8 | tf_op jit(solution)/shard_map/psum | solution.py:94
  274.3 10.1 %all_gather.117 = f32[64,128]{1,0:T(8,128)S(1)} all-gather(f32[8,128]{1,0:T(8,128)S(1)} %get-tuple-element.55), channel_id=1, replica_groups=mesh['sub'=8,'coarse'=4] {'sub'}, dimensions={0}, use_global_device_ids=true | all-gather | bytes 36864 | tf_op jit(solution)/shard_map/all_gather | solution.py:82
  311.4 15.4 %fusion.4 = f32[128,1,128]{2,1,0:T(1,128)S(1)} fusion(f32[128,128,1]{1,2,0:T(1,128)S(1)} %bitcast.356, f32[1,1,128,128,128]{4,3,2,1,0:T(8,128)} %param.16), kind=kOutput, calls=%fused_computation.12 | convolution fusion | flops 25165824 | bytes 8519680 | tf_op jit(solution)/shard_map/bij,bj->bi/dot_general | solution.py:107
  327.1 37.7 %psum.95 = f32[512]{0:T(512)S(1)} all-reduce(f32[512]{0:T(512)S(1)} %broadcast_multiply_fusion.2), channel_id=1, replica_groups=mesh['sub'=8,'coarse'=4] {'sub','coarse'}, use_global_device_ids=true, to_apply=%region_9.11 | all-reduce | flops 512 | bytes 4096 | tf_op jit(solution)/shard_map/psum | solution.py:104
  375.7 9.8 %all_gather.122 = f32[64,128]{1,0:T(8,128)S(1)} all-gather(f32[8,128]{1,0:T(8,128)S(1)} %get-tuple-element.51), channel_id=1, replica_groups=mesh['sub'=8,'coarse'=4] {'sub'}, dimensions={0}, use_global_device_ids=true | all-gather | bytes 36864 | tf_op jit(solution)/shard_map/all_gather | solution.py:82
  413.8 37.6 %psum.96 = f32[2]{0:T(128)S(1)} all-reduce(f32[2]{0:T(128)S(1)} %pad_maximum_fusion.8), channel_id=1, replica_groups=mesh['sub'=8,'coarse'=4] {'sub','coarse'}, use_global_device_ids=true, to_apply=%region_12.14 | all-reduce | flops 2 | bytes 16 | tf_op jit(solution)/shard_map/psum | solution.py:125
  453.9 41.7 %psum.97 = f32[]{:T(128)} all-reduce(f32[]{:T(128)} %get-tuple-element.21), channel_id=1, replica_groups=mesh['sub'=8,'coarse'=4] {'sub','coarse'}, use_global_device_ids=true, to_apply=%region_14.16 | all-reduce | flops 1 | bytes 8 | tf_op jit(solution)/shard_map/psum | solution.py:94
  497.1 10.1 %all_gather.126 = f32[64,128]{1,0:T(8,128)S(1)} all-gather(f32[8,128]{1,0:T(8,128)S(1)} %get-tuple-element.47), channel_id=1, replica_groups=mesh['sub'=8,'coarse'=4] {'sub'}, dimensions={0}, use_global_device_ids=true | all-gather | bytes 36864 | tf_op jit(solution)/shard_map/all_gather | solution.py:82
  533.2 15.4 %fusion.2 = f32[128,1,128]{2,1,0:T(1,128)S(1)} fusion(f32[128,128,1]{1,2,0:T(1,128)S(1)} %bitcast.357, f32[1,1,128,128,128]{4,3,2,1,0:T(8,128)} %param.16), kind=kOutput, calls=%fused_computation.10 | convolution fusion | flops 25165824 | bytes 8519680 | tf_op jit(solution)/shard_map/bij,bj->bi/dot_general | solution.py:107
  548.9 37.7 %psum.98 = f32[512]{0:T(512)S(1)} all-reduce(f32[512]{0:T(512)S(1)} %broadcast_multiply_fusion.1), channel_id=1, replica_groups=mesh['sub'=8,'coarse'=4] {'sub','coarse'}, use_global_device_ids=true, to_apply=%region_16.18 | all-reduce | flops 512 | bytes 4096 | tf_op jit(solution)/shard_map/psum | solution.py:104
  597.5 9.8 %all_gather.131 = f32[64,128]{1,0:T(8,128)S(1)} all-gather(f32[8,128]{1,0:T(8,128)S(1)} %get-tuple-element.43), channel_id=1, replica_groups=mesh['sub'=8,'coarse'=4] {'sub'}, dimensions={0}, use_global_device_ids=true | all-gather | bytes 36864 | tf_op jit(solution)/shard_map/all_gather | solution.py:82
  637.2 37.6 %psum.99 = f32[3]{0:T(128)S(1)} all-reduce(f32[3]{0:T(128)S(1)} %pad_maximum_fusion.9), channel_id=1, replica_groups=mesh['sub'=8,'coarse'=4] {'sub','coarse'}, use_global_device_ids=true, to_apply=%region_20.22 | all-reduce | flops 3 | bytes 24 | tf_op jit(solution)/shard_map/psum | solution.py:125
  678.0 40.7 %psum.100 = f32[]{:T(128)} all-reduce(f32[]{:T(128)} %get-tuple-element.17), channel_id=1, replica_groups=mesh['sub'=8,'coarse'=4] {'sub','coarse'}, use_global_device_ids=true, to_apply=%region_22.24 | all-reduce | flops 1 | bytes 8 | tf_op jit(solution)/shard_map/psum | solution.py:94
  720.1 10.0 %all_gather.135 = f32[64,128]{1,0:T(8,128)S(1)} all-gather(f32[8,128]{1,0:T(8,128)S(1)} %get-tuple-element.39), channel_id=1, replica_groups=mesh['sub'=8,'coarse'=4] {'sub'}, dimensions={0}, use_global_device_ids=true | all-gather | bytes 36864 | tf_op jit(solution)/shard_map/all_gather | solution.py:82
  757.1 15.4 %fusion = f32[128,1,128]{2,1,0:T(1,128)S(1)} fusion(f32[128,128,1]{1,2,0:T(1,128)S(1)} %bitcast.358, f32[1,1,128,128,128]{4,3,2,1,0:T(8,128)} %param.16), kind=kOutput, calls=%fused_computation.8 | convolution fusion | flops 25165824 | bytes 8519680 | tf_op jit(solution)/shard_map/bij,bj->bi/dot_general | solution.py:107
  772.8 37.7 %psum.101 = f32[512]{0:T(512)S(1)} all-reduce(f32[512]{0:T(512)S(1)} %broadcast_multiply_fusion), channel_id=1, replica_groups=mesh['sub'=8,'coarse'=4] {'sub','coarse'}, use_global_device_ids=true, to_apply=%region_24.26 | all-reduce | flops 512 | bytes 4096 | tf_op jit(solution)/shard_map/psum | solution.py:104
  860.8 37.6 %psum.102 = f32[4]{0:T(128)S(1)} all-reduce(f32[4]{0:T(128)S(1)} %pad_maximum_fusion.10), channel_id=1, replica_groups=mesh['sub'=8,'coarse'=4] {'sub','coarse'}, use_global_device_ids=true, to_apply=%region_29.31 | all-reduce | flops 4 | bytes 32 | tf_op jit(solution)/shard_map/psum | solution.py:125
  908.7 41.8 %psum.103 = f32[]{:T(128)} all-reduce(f32[]{:T(128)} %multiply_reduce_fusion), channel_id=1, replica_groups=mesh['sub'=8,'coarse'=4] {'sub','coarse'}, use_global_device_ids=true, to_apply=%region_31.33 | all-reduce | flops 1 | bytes 8 | tf_op jit(solution)/shard_map/psum | solution.py:94
  (159 shorter events, 296.9 us)
Async XLA Ops:
  0.0 87.0 %copy-start = (f32[1,1,4,128,128]{4,3,2,1,0:T(8,128)S(1)}, f32[1,1,4,128,128]{4,3,2,1,0:T(8,128)}, u32[]{:S(2)}) copy-start(f32[1,1,4,128,128]{4,3,2,1,0:T(8,128)} %param.17) | copy-start | bytes 786436
  0.0 153.1 %copy-start.1 = (f32[1,1,128,128]{3,2,1,0:T(8,128)S(1)}, f32[1,1,128,128]{3,2,1,0:T(8,128)}, u32[]{:S(2)}) copy-start(f32[1,1,128,128]{3,2,1,0:T(8,128)} %param.18) | copy-start | bytes 196612
  0.0 103.2 %copy-start.5 = (s32[1,1,128]{2,1,0:T(1,128)S(1)}, s32[1,1,128]{2,1,0:T(1,128)}, u32[]{:S(2)}) copy-start(s32[1,1,128]{2,1,0:T(1,128)} %param.23) | copy-start | bytes 1540
  0.0 142.9 %copy-start.2 = (f32[128,512]{1,0:T(8,128)S(1)}, f32[128,512]{1,0:T(8,128)}, u32[]{:S(2)}) copy-start(f32[128,512]{1,0:T(8,128)} %param.19) | copy-start | bytes 786436
  0.0 190.4 %copy-start.3 = (f32[1,1,128,128]{3,2,1,0:T(8,128)S(1)}, f32[1,1,128,128]{3,2,1,0:T(8,128)}, u32[]{:S(2)}) copy-start(f32[1,1,128,128]{3,2,1,0:T(8,128)} %param.15) | copy-start | bytes 196612
  0.0 190.5 %copy-start.4 = (f32[1,1,128,128]{3,2,1,0:T(8,128)S(1)}, f32[1,1,128,128]{3,2,1,0:T(8,128)}, u32[]{:S(2)}) copy-start(f32[1,1,128,128]{3,2,1,0:T(8,128)} %param.14) | copy-start | bytes 196612
where the time goes:
time: 971 us; the launch traced here: 959 us
  blocking collectives  835 us (86%)
  matrix products  73.9 us (8%)
  other arithmetic  21.1 us (2%)
  between operations  20.4 us (2%)
    all_gather x32, blocking collectives, margin(): gathered = lax.all_gather(outgoing[round_id], 'sub', axis=0, tiled=True)  286 us
    psum x5, blocking collectives, squared_norm(): return lax.psum(jnp.sum(values * values), ('sub', 'coarse'))  208 us
    psum x4, blocking collectives, on_device(): lax.psum(jnp.dot(inner, member_table, precision=highest) * factor, ('sub'...  152 us
    psum x4, blocking collectives, on_device(): lax.psum(jnp.stack([jnp.sum(vector * product) for vector in basis_list]),...  151 us
    dot_general x4, matrix products, on_device(): jnp.einsum('bij,bj->bi', inverse_blocks, current + margin(current), preci...  61.5 us
    all_gather x4, blocking collectives, on_device(): coarse_full = lax.all_gather(coarse_part, 'coarse', axis=0, tiled=True)  38.7 us

commit v1 on v0

v1 whole, which is shorter than its diff:
```python
import jax
import jax.numpy as jnp
from jax import lax
from jax.experimental import pallas as pl
from jax.experimental.pallas import tpu as pltpu
from jax.sharding import PartitionSpec as P

BS = 128
BPD = 128
AGG_DEV = 16
ITERS = 4
LANES = 128
ROWS = 8
BF16 = jnp.bfloat16
F32 = jnp.float32


def split(values):
    high = values.astype(BF16)
    low = (values - high.astype(F32)).astype(BF16)
    return high, low


def dot_rows(left, right):
    return lax.dot_general(left, right, (((1,), (1,)), ((), ())), preferred_element_type=F32)


def dot_plain(left, right):
    return lax.dot_general(left, right, (((1,), (0,)), ((), ())), preferred_element_type=F32)


def paired_rows(values):
    high, low = split(values)
    return jnp.concatenate(
        [
            jnp.concatenate([high, high], axis=1),
            jnp.concatenate([low, jnp.zeros_like(low)], axis=1),
        ],
        axis=0,
    )


def pick(selector, values):
    high, low = split(values)
    return dot_plain(selector, jnp.concatenate([high, low], axis=0))


def couple(arrived, coupling_ref, target_ref):
    count = arrived.shape[0]
    left = paired_rows(arrived)
    highs = []
    lows = []
    for round_id in range(coupling_ref.shape[0]):
        both = dot_rows(left, coupling_ref[round_id])
        high, low = split(both[:count] + both[count:])
        highs.append(high)
        lows.append(low)
    return dot_plain(target_ref[...], jnp.concatenate(highs + lows, axis=0))


def column_sum(values):
    return jnp.sum(values, axis=0, keepdims=True)


def line_product(values, diagonal, link):
    rows = values.shape[0]
    lanes = values.shape[1]
    row = lax.broadcasted_iota(jnp.int32, values.shape, 0)
    lane = lax.broadcasted_iota(jnp.int32, values.shape, 1)
    next_lane = pltpu.roll(values, lanes - 1, 1)
    next_row = pltpu.roll(next_lane, rows - 1, 0)
    ahead = jnp.where(lane < lanes - 1, next_lane, jnp.where(row < rows - 1, next_row, 0.0))
    scaled = link * values
    last_lane = pltpu.roll(scaled, 1, 1)
    last_row = pltpu.roll(last_lane, 1, 0)
    behind = jnp.where(lane > 0, last_lane, jnp.where(row > 0, last_row, 0.0))
    return diagonal * values - (ahead * link + behind)


def restriction_rows(vector, basis, member, own_row, factor):
    inner = jnp.sum(basis * vector, axis=1, keepdims=True)
    return own_row * (column_sum(inner * member) * factor)


def vmem(shape, dtype=F32):
    return pltpu.VMEM(shape, dtype)


def call(kernel, outs, *args, name):
    spec = pl.BlockSpec(memory_space=pltpu.VMEM)
    return pl.pallas_call(
        kernel,
        out_shape=outs,
        in_specs=[spec] * len(args),
        out_specs=[spec] * len(outs),
        name=name,
        compiler_params=pltpu.CompilerParams(vmem_limit_bytes=48 * 1024 * 1024),
    )(*args)


def on_device(
    right_side,
    diagonal,
    cell_link,
    block_inverse,
    coupling,
    coarse_basis,
    coarse_inverse,
    partner,
    margin_width,
    margin_blocks,
    aggregate,
):
    subs = lax.axis_size("sub")
    parts = lax.axis_size("coarse")
    devices = subs * parts
    own_sub = lax.axis_index("sub")
    own_part = lax.axis_index("coarse")
    block_count = right_side.shape[2]
    unknowns = right_side.shape[3]
    rounds = margin_blocks.shape[2]
    widest = margin_blocks.shape[3]
    aggregates = coarse_inverse.shape[1]
    own_aggregates = aggregates // devices
    sub_aggregates = subs * own_aggregates
    factor = (BS * BPD / AGG_DEV) ** (-0.5)
    coarse_rows = aggregates // LANES
    stat_rows = -(-(coarse_rows + ITERS) // ROWS) * ROWS
    slot_rows = subs * widest
    full = (block_count, unknowns)

    basis = coarse_basis[0, 0]
    diagonal_local = diagonal[0, 0]
    link_local = cell_link[0, 0]
    start_vector = right_side[0, 0]
    paired = partner[0]
    widths = margin_width[0]
    blocks = margin_blocks[0, 0]
    member_of = aggregate[0, 0]

    block_ids = jnp.arange(block_count)
    meets = paired[:, None] == jnp.arange(subs)[None, :]
    at_block = blocks[:, :, None] == block_ids[None, None, :]
    selector = jnp.sum(
        (meets[:, :, None, None] & at_block[:, None, :, :]).astype(F32), axis=0
    ).reshape(slot_rows, block_count)
    selector = jnp.concatenate([selector, selector], axis=1).astype(BF16)
    live = jnp.arange(widest)[None, :] < widths[:, None]
    wanted = jnp.where(
        meets[:, :, None] & live[:, None, :], blocks[:, None, :], -1
    ).reshape(rounds * slot_rows)
    target = (block_ids[:, None] == wanted[None, :]).astype(BF16)
    target = jnp.concatenate([target, target], axis=1)
    own_first = (own_sub * parts + own_part) * own_aggregates
    lanes = jnp.arange(LANES)
    member = ((member_of % LANES)[:, None] == lanes[None, :]).astype(F32)
    own_row = jnp.broadcast_to(
        (jnp.arange(coarse_rows) == own_first // LANES)[:, None], (coarse_rows, LANES)
    ).astype(F32)
    sub_lane = member_of - own_first + own_sub * own_aggregates
    sub_member = (sub_lane[:, None] == jnp.arange(sub_aggregates)[None, :]).astype(F32)
    sub_member_lane = ((sub_lane % LANES)[:, None] == lanes[None, :]).astype(F32)
    part_mask = jnp.broadcast_to(
        (jnp.arange(parts) == own_part)[:, None, None], (parts, widest, LANES)
    ).astype(F32)

    sent_rows = coarse_inverse.reshape(subs // parts, parts, own_aggregates, aggregates)
    sent_rows = sent_rows.transpose(1, 0, 2, 3).reshape(parts, -1, aggregates)
    coarse_block = lax.all_to_all(sent_rows, "coarse", 0, 0).reshape(sub_aggregates, aggregates)

    def prepare(inverse_ref, coupling_ref, weight_ref, coupling_pair_ref):
        def step(position, carry):
            for offset in range(2):
                high, low = split(inverse_ref[position * 2 + offset])
                rows = pl.ds(offset * unknowns, unknowns)
                weight_ref[position, rows, 0:unknowns] = high
                weight_ref[position, rows, unknowns : 2 * unknowns] = low
            return carry

        lax.fori_loop(0, block_count // 2, step, 0, unroll=2)
        for round_id in range(rounds):
            high, low = split(coupling_ref[round_id])
            coupling_pair_ref[round_id, :, 0:unknowns] = high
            coupling_pair_ref[round_id, :, unknowns : 2 * unknowns] = low

    weights, coupling_pairs = call(
        prepare,
        [
            vmem((block_count // 2, 2 * unknowns, 2 * unknowns), BF16),
            vmem((rounds, unknowns, 2 * unknowns), BF16),
        ],
        block_inverse[0, 0],
        coupling[0, 0],
        name="prepare",
    )

    def write_statistics(stat_ref, vector, basis_value, member_value, own_row_value, dots):
        stat_ref[...] = jnp.zeros_like(stat_ref)
        stat_ref[0:coarse_rows, :] = restriction_rows(
            vector, basis_value, member_value, own_row_value, factor
        )
        for position, other in enumerate(dots):
            stat_ref[coarse_rows + position : coarse_rows + position + 1, :] = column_sum(
                other * vector
            )

    def begin(start_ref, basis_ref, member_ref, row_ref, lane_ref, selector_ref, out_ref, stat_ref):
        start = start_ref[...]
        basis_value = basis_ref[...]
        table = selector_ref[...]
        out_ref[:, 0:widest, :] = pick(table, start).reshape(subs, widest, unknowns)
        out_ref[:, widest : 2 * widest, :] = pick(table, basis_value).reshape(
            subs, widest, unknowns
        )
        out_ref[:, 2 * widest : 3 * widest, :] = pick(table, lane_ref[...]).reshape(
            subs, widest, LANES
        )
        write_statistics(stat_ref, start, basis_value, member_ref[...], row_ref[...], [start])

    outgoing, statistics = call(
        begin,
        [vmem((subs, 3 * widest, unknowns)), vmem((stat_rows, LANES))],
        start_vector,
        basis,
        member,
        own_row,
        sub_member_lane,
        selector,
        name="begin",
    )

    def smooth(arrived, vector_ref, stat_ref, weight_ref, pair_ref, target_ref, selector_ref, mask_ref, out_ref, slot_ref):
        shifted = vector_ref[...] + couple(arrived, pair_ref, target_ref)
        out_ref[...] = shifted
        row = lax.broadcasted_iota(jnp.int32, (ROWS, unknowns), 0)

        def step(group, carry):
            rows = pl.ds(pl.multiple_of(group * ROWS, ROWS), ROWS)
            left = paired_rows(out_ref[rows, :])
            total = jnp.zeros((ROWS, unknowns), F32)
            for offset in range(ROWS // 2):
                both = dot_rows(left, weight_ref[group * (ROWS // 2) + offset])
                both = both[:ROWS] + both[ROWS:]
                total = jnp.where(row == 2 * offset, both[:, :unknowns], total)
                total = jnp.where(row == 2 * offset + 1, both[:, unknowns:], total)
            out_ref[rows, :] = total
            return carry

        lax.fori_loop(0, block_count // ROWS, step, 0, unroll=2)
        margin_rows = pick(selector_ref[...], out_ref[...]).reshape(subs, widest, unknowns)
        statistic = stat_ref[...]
        for sub_id in range(subs):
            for part_id in range(parts):
                slot = sub_id * parts + part_id
                slot_ref[slot, 0:widest, :] = margin_rows[sub_id] * mask_ref[part_id]
                slot_ref[slot, widest:, :] = statistic

    def smooth_first(arrived_ref, *refs):
        *rest, basis_ref, lane_ref = refs
        smooth(arrived_ref[:, 0:widest, :].reshape(slot_rows, unknowns), *rest)
        basis_ref[...] = arrived_ref[:, widest : 2 * widest, :].reshape(slot_rows, unknowns)
        lane_ref[...] = arrived_ref[:, 2 * widest : 3 * widest, :].reshape(slot_rows, LANES)

    def smooth_later(arrived_ref, *refs):
        smooth(arrived_ref[...].reshape(slot_rows, unknowns), *refs)

    def advance(step_id):
        last = step_id == ITERS - 1

        def kernel(*refs):
            (
                arrived_ref,
                smoothed_ref,
                vector_ref,
                coarse_ref,
                sub_member_ref,
                member_ref,
                row_ref,
                basis_ref,
                margin_basis_ref,
                margin_lane_ref,
                pair_ref,
                target_ref,
                selector_ref,
                diagonal_ref,
                link_ref,
            ) = refs[:15]
            earlier = refs[15 : 15 + 3 * step_id]
            v_refs = earlier[:step_id]
            z_refs = earlier[step_id : 2 * step_id]
            m_refs = earlier[2 * step_id :]
            outs = refs[15 + 3 * step_id :]
            total = arrived_ref[0, widest:, :]
            for slot in range(1, devices):
                total = total + arrived_ref[slot, widest:, :]
            products = jnp.sum(total[coarse_rows : coarse_rows + step_id + 1], axis=1, keepdims=True)
            heads = [products[i : i + 1] for i in range(step_id)]
            square = products[step_id : step_id + 1]
            remaining = square
            for head in heads:
                remaining = remaining - head * head
            length = jnp.sqrt(jnp.maximum(remaining, square * 1e-12))
            scale = 1.0 / length
            gathered = coarse_ref[:, 0:LANES] * total[0:1]
            for chunk in range(1, coarse_rows):
                gathered = gathered + (
                    coarse_ref[:, chunk * LANES : (chunk + 1) * LANES] * total[chunk : chunk + 1]
                )
            column = jnp.sum(gathered, axis=1, keepdims=True)
            same = lax.broadcasted_iota(jnp.int32, (LANES, LANES), 0) == lax.broadcasted_iota(
                jnp.int32, (LANES, LANES), 1
            )
            coarse_lines = [
                column_sum(jnp.where(same, column[start : start + LANES], 0.0))
                for start in range(0, sub_aggregates, LANES)
            ]
            own_coarse = jnp.zeros((block_count, LANES), F32)
            for chunk, line in enumerate(coarse_lines):
                own_coarse = own_coarse + (
                    sub_member_ref[:, chunk * LANES : (chunk + 1) * LANES] * line
                )
            own_coarse = jnp.sum(own_coarse, axis=1, keepdims=True)
            basis_value = basis_ref[...]
            direction = smoothed_ref[...] + own_coarse * basis_value
            for head, z_ref in zip(heads, z_refs):
                direction = direction - head * z_ref[...]
            direction = direction * scale
            pieces = []
            for sub_id in range(subs):
                piece = arrived_ref[sub_id * parts, 0:widest, :]
                for part_id in range(1, parts):
                    piece = piece + arrived_ref[sub_id * parts + part_id, 0:widest, :]
                line = coarse_lines[sub_id * own_aggregates // LANES]
                rows = pl.ds(sub_id * widest, widest)
                weight = jnp.sum(margin_lane_ref[rows, :] * line, axis=1, keepdims=True)
                pieces.append(piece + weight * margin_basis_ref[rows, :])
            margin_rows = jnp.concatenate(pieces, axis=0)
            for head, m_ref in zip(heads, m_refs):
                margin_rows = margin_rows - head * m_ref[...]
            margin_rows = margin_rows * scale
            vector = vector_ref[...]
            for head, v_ref in zip(heads, v_refs):
                vector = vector - head * v_ref[...]
            vector = vector * scale
            product = line_product(direction, diagonal_ref[...], link_ref[...]) - couple(
                margin_rows, pair_ref, target_ref
            )
            against = [v_ref[...] for v_ref in v_refs] + [vector, product]
            if last:
                direction_ref, head_ref, out_ref = outs
                block = jnp.concatenate(
                    [column_sum(other * product) for other in against]
                    + [jnp.zeros((ROWS - len(against), LANES), F32)],
                    axis=0,
                )
                for slot in range(devices):
                    out_ref[slot] = block
            else:
                direction_ref, head_ref, new_v_ref, margin_ref, product_ref, out_ref, stat_ref = outs
                new_v_ref[...] = vector
                margin_ref[...] = margin_rows
                product_ref[...] = product
                out_ref[...] = pick(selector_ref[...], product).reshape(subs, widest, unknowns)
                write_statistics(
                    stat_ref, product, basis_value, member_ref[...], row_ref[...], against
                )
            direction_ref[...] = direction
            head_ref[...] = jnp.broadcast_to(
                jnp.concatenate(
                    heads + [length] + [jnp.zeros((ROWS - step_id - 1, 1), F32)], axis=0
                ),
                (ROWS, LANES),
            )

        return kernel

    v_list = []
    z_list = []
    m_list = []
    head_list = []
    vector = start_vector
    margin_basis = margin_lane = None
    for step_id in range(ITERS):
        arrived = lax.all_to_all(outgoing, "sub", 0, 0)
        outs = [vmem(full), vmem((devices, widest + stat_rows, unknowns))]
        if step_id == 0:
            outs += [vmem((slot_rows, unknowns)), vmem((slot_rows, LANES))]
        made = call(
            smooth_first if step_id == 0 else smooth_later,
            outs,
            arrived,
            vector,
            statistics,
            weights,
            coupling_pairs,
            target,
            selector,
            part_mask,
            name=f"smooth{step_id}",
        )
        smoothed, slots = made[:2]
        if step_id == 0:
            margin_basis, margin_lane = made[2:]
        arrived = lax.all_to_all(slots, ("sub", "coarse"), 0, 0)
        outs = [vmem(full), vmem((ROWS, LANES))]
        if step_id == ITERS - 1:
            outs += [vmem((devices, ROWS, LANES))]
        else:
            outs += [
                vmem(full),
                vmem((slot_rows, unknowns)),
                vmem(full),
                vmem((subs, widest, unknowns)),
                vmem((stat_rows, LANES)),
            ]
        made = call(
            advance(step_id),
            outs,
            arrived,
            smoothed,
            vector,
            coarse_block,
            sub_member,
            member,
            own_row,
            basis,
            margin_basis,
            margin_lane,
            coupling_pairs,
            target,
            selector,
            diagonal_local,
            link_local,
            *v_list,
            *z_list,
            *m_list,
            name=f"advance{step_id}",
        )
        z_list.append(made[0])
        head_list.append(made[1])
        if step_id < ITERS - 1:
            v_list.append(made[2])
            m_list.append(made[3])
            vector, outgoing, statistics = made[4:]
        else:
            slots = made[2]
    arrived = lax.all_to_all(slots, ("sub", "coarse"), 0, 0)

    def finish(arrived_ref, *refs):
        head_refs = refs[:ITERS]
        z_refs = refs[ITERS : 2 * ITERS]
        out_ref = refs[2 * ITERS]
        total = arrived_ref[0]
        for slot in range(1, devices):
            total = total + arrived_ref[slot]
        products = jnp.sum(total, axis=1, keepdims=True)
        heads = [products[i : i + 1] for i in range(ITERS)]
        square = products[ITERS : ITERS + 1]
        remaining = square
        for head in heads:
            remaining = remaining - head * head
        length = jnp.sqrt(jnp.maximum(remaining, square * 1e-12))
        beta = head_refs[0][0:1, 0:1]
        columns = []
        for column_id in range(1, ITERS):
            columns.append([head_refs[column_id][i : i + 1, 0:1] for i in range(column_id + 1)])
        columns.append(heads + [length])
        weights_found = givens_solve(columns, beta)
        result = weights_found[0] * z_refs[0][...]
        for position in range(1, ITERS):
            result = result + weights_found[position] * z_refs[position][...]
        out_ref[...] = result

    (answer,) = call(
        finish, [jax.ShapeDtypeStruct(full, F32)], arrived, *head_list, *z_list, name="finish"
    )
    return answer.reshape(right_side.shape)


def givens_solve(columns, beta):
    steps_count = len(columns)
    cosines = []
    sines = []
    side_terms = [beta] + [jnp.zeros_like(beta) for unused in range(steps_count)]
    triangle = []
    for column_id in range(steps_count):
        column = list(columns[column_id])
        for row_id in range(column_id):
            upper = column[row_id]
            lower = column[row_id + 1]
            column[row_id] = cosines[row_id] * upper + sines[row_id] * lower
            column[row_id + 1] = cosines[row_id] * lower - sines[row_id] * upper
        upper = column[column_id]
        lower = column[column_id + 1]
        radius = jnp.sqrt(upper * upper + lower * lower)
        cosine = upper / radius
        sine_value = lower / radius
        column[column_id] = radius
        cosines.append(cosine)
        sines.append(sine_value)
        side_terms[column_id + 1] = -sine_value * side_terms[column_id]
        side_terms[column_id] = cosine * side_terms[column_id]
        triangle.append(column)
    weights = [None] * steps_count
    for column_id in reversed(range(steps_count)):
        running = side_terms[column_id]
        for later_col in range(column_id + 1, steps_count):
            running = running - triangle[later_col][column_id] * weights[later_col]
        weights[column_id] = running / triangle[column_id][column_id]
    return weights


def solution(mesh):
    placed = (
        P("sub", "coarse", None, None),
        P("sub", "coarse", None, None),
        P("sub", "coarse", None, None),
        P("sub", "coarse", None, None, None),
        P("sub", "coarse", None, None, None),
        P("sub", "coarse", None, None),
        P("coarse", None),
        P("sub", None),
        P("sub", None),
        P("sub", "coarse", None, None),
        P("sub", "coarse", None),
    )
    return jax.shard_map(
        on_device,
        mesh=mesh,
        in_specs=placed,
        out_specs=P("sub", "coarse", None, None),
        check_vma=False,
    )
```

time: 971 us -> 146 us (0.15); the launches traced: 959 us -> 145 us
  blocking collectives: 835 us -> 69 us
  matrix products: 73.9 us -> 0 us
  Pallas kernels: 0 us -> 38.4 us
  between operations: 20.4 us -> 0.15 us
  other arithmetic: 21.1 us -> 3.35 us
  starting transfers between devices: 0 us -> 14.2 us
  waiting for transfers between devices: 0 us -> 12.9 us
    psum x13 -> x0, blocking collectives: 511 us -> none  [the longest x5 208 us: squared_norm(): return lax.psum(jnp.sum(values * values), ('sub', 'coarse'))]
    all_gather x36 -> x0, blocking collectives: 324 us -> none  [the longest x32 286 us: margin(): gathered = lax.all_gather(outgoing[round_id], 'sub', axis=0, tiled=True)]
    dot_general x32 -> x0, matrix products: 73.9 us -> none  [the longest x4 61.5 us: on_device(): jnp.einsum('bij,bj->bi', inverse_blocks, current + margin(current), preci...]
    all_to_all x0 -> x7, blocking collectives: none -> 69 us  [the longest x4 47.3 us: on_device(): arrived = lax.all_to_all(slots, ('sub', 'coarse'), 0, 0)]
    pallas_call x0 -> x11, Pallas kernels: none -> 38.4 us  [call(): pl.pallas_call(kernel, out_shape=outs, in_specs=[spec] * len(args), out_s...]
    all_to_all x0 -> x3, starting transfers between devices: none -> 14.2 us  [the longest x1 5.18 us: on_device(): arrived = lax.all_to_all(outgoing, 'sub', 0, 0)]
    all_to_all x0 -> x3, waiting for transfers between devices: none -> 12.9 us  [the longest x1 10.1 us: on_device(): arrived = lax.all_to_all(slots, ('sub', 'coarse'), 0, 0)]
    reduce_sum x9 -> x1, other arithmetic: 12.2 us -> 0.1 us  [on_device(): jnp.sum((meets[:, :, None, None] & at_block[:, None, :, :]).astype(F32),...]
  transfers between devices with their start and end apart: 0 -> 3, of which waited for: 0 -> 2; matrix products, arithmetic and copies ran while one was open for 0% -> 2% of each run, Pallas kernels for 0% -> 9%
where the time goes in v1:
time: 146 us; the launch traced here: 145 us
  blocking collectives  69 us (47%)
  Pallas kernels  38.4 us (26%)
  starting transfers between devices  14.2 us (10%)
  waiting for transfers between devices  12.9 us (9%)
  local copies, waits for them, and re-layouts  6.86 us (5%)
  other arithmetic  3.35 us (2%)
    all_to_all x4, blocking collectives, on_device(): arrived = lax.all_to_all(slots, ('sub', 'coarse'), 0, 0)  47.3 us
    pallas_call x11, Pallas kernels, call(): pl.pallas_call(kernel, out_shape=outs, in_specs=[spec] * len(args), out_s...  38.4 us
    all_to_all x3, blocking collectives, on_device(): arrived = lax.all_to_all(outgoing, 'sub', 0, 0)  21.6 us
    all_to_all x1, waiting for transfers between devices, on_device(): arrived = lax.all_to_all(slots, ('sub', 'coarse'), 0, 0)  10.1 us
    all_to_all x1, starting transfers between devices, on_device(): arrived = lax.all_to_all(outgoing, 'sub', 0, 0)  5.18 us
    unnamed x14, local copies, waits for them, and re-layouts  4.95 us
    all_to_all x1, starting transfers between devices, on_device(): lax.all_to_all(sent_rows, 'coarse', 0, 0)  4.87 us
    all_to_all x1, starting transfers between devices, on_device(): arrived = lax.all_to_all(slots, ('sub', 'coarse'), 0, 0)  4.19 us
  transfers between devices with their start and end apart: 3, of which 2 were waited for; matrix products, arithmetic and copies ran while one was open for 2% of the time, Pallas kernels for 9%

profile of v1, /device:TPU:0, one launch (start us, length us, event | category | flops | bytes accessed | tf_op | source)
XLA Modules:
  0.0 144.8 jit_solution(12349282839838435026)
XLA Ops:
  0.0 0.8 iota_compare_fusion.4
  2.6 0.8 copy-done.1
  3.4 0.8 copy-done.5
  4.3 0.8 begin.1
  5.1 5.2 %all-to-all-start = ((f32[8,24,128]{2,1,0:T(8,128)}), f32[8,24,128]{2,1,0:T(8,128)S(1)}, u32[]{:S(2)}, u32[]{:S(2)}) async-start(f32[8,24,128]{2,1,0:T(8,128)} %get-tuple-element.43), calls=%async_computation | async-start | bytes 196608 | tf_op jit(solution)/shard_map/all_to_all | solution.py:384
  11.0 1.7 %copy.13 = f32[4,2,16,512]{3,2,1,0:T(8,128)} copy(f32[4,2,16,512]{3,2,0,1:T(8,128)} %bitcast.46) | data formatting | bytes 524288 | tf_op jit(solution)/shard_map/transpose | solution.py:168
  12.7 2.8 %all-to-all-done.arrived_ref = f32[8,24,128]{2,1,0:T(8,128)S(1)} async-done(((f32[8,24,128]{2,1,0:T(8,128)}), f32[8,24,128]{2,1,0:T(8,128)S(1)}, u32[]{:S(2)}, u32[]{:S(2)}) %all-to-all-start) | async-done | bytes 98336 | tf_op jit(solution)/shard_map/all_to_all | solution.py:384
  15.4 4.9 %all-to-all-start.2 = ((f32[4,32,512]{2,1,0:T(8,128)}), f32[4,32,512]{2,1,0:T(8,128)S(1)}, u32[]{:S(2)}, u32[]{:S(2)}) async-start(f32[4,32,512]{2,1,0:T(8,128)} %bitcast.11), calls=%async_computation.2 | async-start | bytes 524288 | tf_op jit(solution)/shard_map/all_to_all | solution.py:169
  20.4 4.9 %prepare.1 = (bf16[64,256,256]{2,1,0:T(8,128)(2,1)S(1)}, bf16[4,128,256]{2,1,0:T(8,128)(2,1)S(1)}) custom-call(f32[128,128,128]{2,1,0:T(8,128)} %bitcast.44, f32[4,128,128]{2,1,0:T(8,128)} %bitcast.45), custom_call_target="tpu_custom_call" | custom-call | tf_op jit(solution)/shard_map/prepare/pallas_call | solution.py:91
  25.4 3.2 %copy-done = bf16[64,256,256]{2,1,0:T(8,128)(2,1)} copy-done((bf16[64,256,256]{2,1,0:T(8,128)(2,1)}, bf16[64,256,256]{2,1,0:T(8,128)(2,1)S(1)}, u32[]{:S(2)}) %copy-start) | copy-done | bytes 8388632
  28.7 7.8 %smooth0.1 = (f32[128,128]{1,0:T(8,128)S(1)}, f32[32,16,128]{2,1,0:T(8,128)}, f32[64,128]{1,0:T(8,128)S(1)}, f32[64,128]{1,0:T(8,128)S(1)}) custom-call(f32[8,24,128]{2,1,0:T(8,128)S(1)} %all-to-all-done.arrived_ref, f32[128,128]{1,0:T(8,128)S(1)} %bitcast.42, f32[8,128]{1,0:T(8,128)S(1)} %get-tuple-element.44.refs_1_, bf16[64,256,256]{2,1,0:T(8,128)(2,1)} %copy-done, ...), custom_call_target="tpu_custom_call" | custom-call | tf_op jit(solution)/shard_map/smooth0/pallas_call | solution.py:91
  36.5 4.2 %all-to-all-start.1 = ((f32[32,16,128]{2,1,0:T(8,128)}), f32[32,16,128]{2,1,0:T(8,128)S(1)}, u32[]{:S(2)}, u32[]{:S(2)}) async-start(f32[32,16,128]{2,1,0:T(8,128)} %get-tuple-element.47), calls=%async_computation.1 | async-start | bytes 524288 | tf_op jit(solution)/shard_map/all_to_all | solution.py:404
  40.8 10.1 %all-to-all-done.1.refs_0_ = f32[32,16,128]{2,1,0:T(8,128)S(1)} async-done(((f32[32,16,128]{2,1,0:T(8,128)}), f32[32,16,128]{2,1,0:T(8,128)S(1)}, u32[]{:S(2)}, u32[]{:S(2)}) %all-to-all-start.1) | async-done | bytes 262176 | tf_op jit(solution)/shard_map/all_to_all | solution.py:404
  51.7 7.2 %all_to_all.50.arrived_ref = f32[8,8,128]{2,1,0:T(8,128)S(1)} all-to-all(f32[8,8,128]{2,1,0:T(8,128)S(1)} %get-tuple-element.51), channel_id=1, replica_groups=mesh['sub'=8,'coarse'=4] {'sub'}, dimensions={0} | all-to-all | bytes 65536 | tf_op jit(solution)/shard_map/all_to_all | solution.py:384
  58.9 7.0 %smooth1.1 = (f32[128,128]{1,0:T(8,128)S(1)}, f32[32,16,128]{2,1,0:T(8,128)S(1)}) custom-call(f32[8,8,128]{2,1,0:T(8,128)S(1)} %all_to_all.50.arrived_ref, f32[128,128]{1,0:T(8,128)S(1)} %get-tuple-element.52.refs_0_.refs_2_, f32[8,128]{1,0:T(8,128)S(1)} %get-tuple-element.53.refs_1_, bf16[64,256,256]{2,1,0:T(8,128)(2,1)} %copy-done, ...), custom_call_target="tpu_custom_call" | custom-call | tf_op jit(solution)/shard_map/smooth1/pallas_call | solution.py:91
  66.0 12.1 %all_to_all.51.refs_0_ = f32[32,16,128]{2,1,0:T(8,128)S(1)} all-to-all(f32[32,16,128]{2,1,0:T(8,128)S(1)} %get-tuple-element.54), channel_id=1, replica_groups=mesh['sub'=8,'coarse'=4] {'sub','coarse'}, dimensions={0} | all-to-all | bytes 524288 | tf_op jit(solution)/shard_map/all_to_all | solution.py:404
  78.8 7.2 %all_to_all.52.arrived_ref = f32[8,8,128]{2,1,0:T(8,128)S(1)} all-to-all(f32[8,8,128]{2,1,0:T(8,128)S(1)} %get-tuple-element.59), channel_id=1, replica_groups=mesh['sub'=8,'coarse'=4] {'sub'}, dimensions={0} | all-to-all | bytes 65536 | tf_op jit(solution)/shard_map/all_to_all | solution.py:384
  86.0 7.1 %smooth2.1 = (f32[128,128]{1,0:T(8,128)S(1)}, f32[32,16,128]{2,1,0:T(8,128)S(1)}) custom-call(f32[8,8,128]{2,1,0:T(8,128)S(1)} %all_to_all.52.arrived_ref, f32[128,128]{1,0:T(8,128)S(1)} %get-tuple-element.60.refs_0_.refs_2_, f32[8,128]{1,0:T(8,128)S(1)} %get-tuple-element.61.refs_1_, bf16[64,256,256]{2,1,0:T(8,128)(2,1)} %copy-done, ...), custom_call_target="tpu_custom_call" | custom-call | tf_op jit(solution)/shard_map/smooth2/pallas_call | solution.py:91
  93.1 12.1 %all_to_all.53.refs_0_ = f32[32,16,128]{2,1,0:T(8,128)S(1)} all-to-all(f32[32,16,128]{2,1,0:T(8,128)S(1)} %get-tuple-element.62), channel_id=1, replica_groups=mesh['sub'=8,'coarse'=4] {'sub','coarse'}, dimensions={0} | all-to-all | bytes 524288 | tf_op jit(solution)/shard_map/all_to_all | solution.py:404
  106.0 7.2 %all_to_all.54.arrived_ref = f32[8,8,128]{2,1,0:T(8,128)S(1)} all-to-all(f32[8,8,128]{2,1,0:T(8,128)S(1)} %get-tuple-element.67), channel_id=1, replica_groups=mesh['sub'=8,'coarse'=4] {'sub'}, dimensions={0} | all-to-all | bytes 65536 | tf_op jit(solution)/shard_map/all_to_all | solution.py:384
  113.2 7.1 %smooth3.1 = (f32[128,128]{1,0:T(8,128)S(1)}, f32[32,16,128]{2,1,0:T(8,128)S(1)}) custom-call(f32[8,8,128]{2,1,0:T(8,128)S(1)} %all_to_all.54.arrived_ref, f32[128,128]{1,0:T(8,128)S(1)} %get-tuple-element.68.refs_0_.refs_2_, f32[8,128]{1,0:T(8,128)S(1)} %get-tuple-element.69.refs_1_, bf16[64,256,256]{2,1,0:T(8,128)(2,1)} %copy-done, ...), custom_call_target="tpu_custom_call" | custom-call | tf_op jit(solution)/shard_map/smooth3/pallas_call | solution.py:91
  120.3 12.1 %all_to_all.55.refs_0_ = f32[32,16,128]{2,1,0:T(8,128)S(1)} all-to-all(f32[32,16,128]{2,1,0:T(8,128)S(1)} %get-tuple-element.70), channel_id=1, replica_groups=mesh['sub'=8,'coarse'=4] {'sub','coarse'}, dimensions={0} | all-to-all | bytes 524288 | tf_op jit(solution)/shard_map/all_to_all | solution.py:404
  133.1 10.9 %all_to_all.56.arrived_ref = f32[32,8,128]{2,1,0:T(8,128)S(1)} all-to-all(f32[32,8,128]{2,1,0:T(8,128)S(1)} %get-tuple-element.75), channel_id=1, replica_groups=mesh['sub'=8,'coarse'=4] {'sub','coarse'}, dimensions={0} | all-to-all | bytes 262144 | tf_op jit(solution)/shard_map/all_to_all | solution.py:447
  144.0 0.8 finish.1
  (31 shorter events, 5.7 us)
Async XLA Ops:
  0.0 28.7 %copy-start.6 = (f32[1,1,128,128]{3,2,1,0:T(8,128)S(1)}, f32[1,1,128,128]{3,2,1,0:T(8,128)}, u32[]{:S(2)}) copy-start(f32[1,1,128,128]{3,2,1,0:T(8,128)} %param.11) | copy-start | bytes 196612
  2.6 0.8 copy-start.1
  3.4 0.8 copy-start.5
  5.1 10.4 %all-to-all-start = ((f32[8,24,128]{2,1,0:T(8,128)}), f32[8,24,128]{2,1,0:T(8,128)S(1)}, u32[]{:S(2)}, u32[]{:S(2)}) async-start(f32[8,24,128]{2,1,0:T(8,128)} %get-tuple-element.43), calls=%async_computation | async-start | bytes 196608 | tf_op jit(solution)/shard_map/all_to_all | solution.py:384
  15.4 21.1 %all-to-all-start.2 = ((f32[4,32,512]{2,1,0:T(8,128)}), f32[4,32,512]{2,1,0:T(8,128)S(1)}, u32[]{:S(2)}, u32[]{:S(2)}) async-start(f32[4,32,512]{2,1,0:T(8,128)} %bitcast.11), calls=%async_computation.2 | async-start | bytes 524288 | tf_op jit(solution)/shard_map/all_to_all | solution.py:169
  20.4 30.5 %copy-start.2 = (f32[1,1,128,128]{3,2,1,0:T(8,128)S(1)}, f32[1,1,128,128]{3,2,1,0:T(8,128)}, u32[]{:S(2)}) copy-start(f32[1,1,128,128]{3,2,1,0:T(8,128)} %param.16) | copy-start | bytes 196612
  20.4 30.5 %copy-start.3 = (f32[1,1,128,128]{3,2,1,0:T(8,128)S(1)}, f32[1,1,128,128]{3,2,1,0:T(8,128)}, u32[]{:S(2)}) copy-start(f32[1,1,128,128]{3,2,1,0:T(8,128)} %param.12) | copy-start | bytes 196612
  20.4 30.5 %copy-start.4 = (f32[1,1,128,128]{3,2,1,0:T(8,128)S(1)}, f32[1,1,128,128]{3,2,1,0:T(8,128)}, u32[]{:S(2)}) copy-start(f32[1,1,128,128]{3,2,1,0:T(8,128)} %param.13) | copy-start | bytes 196612
  25.4 3.3 %copy-start = (bf16[64,256,256]{2,1,0:T(8,128)(2,1)}, bf16[64,256,256]{2,1,0:T(8,128)(2,1)S(1)}, u32[]{:S(2)}) copy-start(bf16[64,256,256]{2,1,0:T(8,128)(2,1)S(1)} %get-tuple-element.45.refs_2_) | copy-start | bytes 25165828
  36.5 14.4 %all-to-all-start.1 = ((f32[32,16,128]{2,1,0:T(8,128)}), f32[32,16,128]{2,1,0:T(8,128)S(1)}, u32[]{:S(2)}, u32[]{:S(2)}) async-start(f32[32,16,128]{2,1,0:T(8,128)} %get-tuple-element.47), calls=%async_computation.1 | async-start | bytes 524288 | tf_op jit(solution)/shard_map/all_to_all | solution.py:404

commit v2 on v1

v2 whole, which is shorter than its diff:
```python
import jax
import jax.numpy as jnp
from jax import lax
from jax.experimental import pallas as pl
from jax.experimental.pallas import tpu as pltpu
from jax.sharding import PartitionSpec as P

BS = 128
BPD = 128
AGG_DEV = 16
ITERS = 4
LANES = 128
ROWS = 8
BF16 = jnp.bfloat16
F32 = jnp.float32


def split(values):
    high = values.astype(BF16)
    low = (values - high.astype(F32)).astype(BF16)
    return high, low


def dot_rows(left, right):
    return lax.dot_general(left, right, (((1,), (1,)), ((), ())), preferred_element_type=F32)


def dot_plain(left, right):
    return lax.dot_general(left, right, (((1,), (0,)), ((), ())), preferred_element_type=F32)


def paired_rows(values):
    high, low = split(values)
    return jnp.concatenate(
        [
            jnp.concatenate([high, high], axis=1),
            jnp.concatenate([low, jnp.zeros_like(low)], axis=1),
        ],
        axis=0,
    )


def pick(selector, values):
    high, low = split(values)
    return dot_plain(selector, jnp.concatenate([high, low], axis=0))


def column_sum(values):
    return jnp.sum(values, axis=0, keepdims=True)


def line_product(values, diagonal, link):
    rows = values.shape[0]
    lanes = values.shape[1]
    row = lax.broadcasted_iota(jnp.int32, values.shape, 0)
    lane = lax.broadcasted_iota(jnp.int32, values.shape, 1)
    next_lane = pltpu.roll(values, lanes - 1, 1)
    next_row = pltpu.roll(next_lane, rows - 1, 0)
    ahead = jnp.where(lane < lanes - 1, next_lane, jnp.where(row < rows - 1, next_row, 0.0))
    scaled = link * values
    last_lane = pltpu.roll(scaled, 1, 1)
    last_row = pltpu.roll(last_lane, 1, 0)
    behind = jnp.where(lane > 0, last_lane, jnp.where(row > 0, last_row, 0.0))
    return diagonal * values - (ahead * link + behind)


def couple(arrived, pair_ref, live):
    rounds = pair_ref.shape[0]
    widest = arrived.shape[0] // rounds
    pieces = []
    for round_id in range(rounds):
        left = paired_rows(arrived[round_id * widest : (round_id + 1) * widest])
        both = dot_rows(left, pair_ref[round_id])
        pieces.append(both[:widest] + both[widest:])
    return jnp.concatenate(pieces, axis=0) * live


def gather_rounds(slots, route, rounds):
    pieces = []
    for round_id in range(rounds):
        total = None
        for sub_id, piece in enumerate(slots):
            at = round_id * len(slots) + sub_id
            term = route[at : at + 1] * piece
            total = term if total is None else total + term
        pieces.append(total)
    return jnp.concatenate(pieces, axis=0)


def spread_rounds(values, route, subs, rounds):
    widest = values.shape[0] // rounds
    slots = []
    for sub_id in range(subs):
        total = None
        for round_id in range(rounds):
            at = round_id * subs + sub_id
            term = route[at : at + 1] * values[round_id * widest : (round_id + 1) * widest]
            total = term if total is None else total + term
        slots.append(total)
    return slots


def vmem(shape, dtype=F32):
    return pltpu.VMEM(shape, dtype)


def call(kernel, outs, *args, name, scalars=0):
    spec = pl.BlockSpec(memory_space=pltpu.VMEM)
    scalar_spec = pl.BlockSpec(memory_space=pltpu.SMEM)
    return pl.pallas_call(
        kernel,
        out_shape=outs,
        in_specs=[scalar_spec] * scalars + [spec] * (len(args) - scalars),
        out_specs=[spec] * len(outs),
        name=name,
        compiler_params=pltpu.CompilerParams(vmem_limit_bytes=16 * 1024 * 1024),
    )(*args)


def on_device(
    right_side,
    diagonal,
    cell_link,
    block_inverse,
    coupling,
    coarse_basis,
    coarse_inverse,
    partner,
    margin_width,
    margin_blocks,
    aggregate,
):
    subs = lax.axis_size("sub")
    parts = lax.axis_size("coarse")
    devices = subs * parts
    block_count = right_side.shape[2]
    unknowns = right_side.shape[3]
    rounds = margin_blocks.shape[2]
    widest = margin_blocks.shape[3]
    aggregates = coarse_inverse.shape[1]
    held_rows = coarse_inverse.shape[0]
    own_aggregates = aggregates // devices
    sub_aggregates = subs * own_aggregates
    sub_chunks = sub_aggregates // LANES
    piece_rows = own_aggregates // parts
    factor = (BS * BPD / AGG_DEV) ** (-0.5)
    coarse_rows = aggregates // LANES
    stat_rows = -(-(coarse_rows + ITERS) // ROWS) * ROWS
    slot_rows = max(widest, stat_rows)
    extra_rows = -(-piece_rows * coarse_rows // ROWS) * ROWS
    margin_rows = rounds * widest
    table_rows = -(-2 * margin_rows // LANES) * LANES
    full = (block_count, unknowns)

    basis = coarse_basis[0, 0]
    diagonal_local = diagonal[0, 0]
    link_local = cell_link[0, 0]
    start_vector = right_side[0, 0]
    inverse_blocks = block_inverse[0, 0]
    blocks = margin_blocks[0, 0]
    member_of = aggregate[0]
    own_bits = own_aggregates.bit_length() - 1
    part_bits = parts.bit_length() - 1
    piece_bits = piece_rows.bit_length() - 1
    lane_bits = LANES.bit_length() - 1
    assert own_aggregates == 1 << own_bits and parts == 1 << part_bits
    assert piece_rows == 1 << piece_bits

    def iota(shape, dim):
        return lax.broadcasted_iota(jnp.int32, shape, dim)

    def hot(condition):
        return jnp.where(condition, 1.0, 0.0).astype(F32)

    def statistics_block(vector, basis_value, member_value, home, dots, rows, count):
        inner = jnp.sum(basis_value * vector, axis=1, keepdims=True)
        line = column_sum(inner * member_value) * factor
        lines = [home[chunk : chunk + 1] * line for chunk in range(count)]
        lines += [column_sum(other * vector) for other in dots]
        if len(lines) < rows:
            lines.append(jnp.zeros((rows - len(lines), LANES), F32))
        return jnp.concatenate(lines, axis=0)

    def begin(
        blocks_ref,
        partner_ref,
        width_ref,
        start_ref,
        basis_ref,
        member_of_ref,
        slot_ref,
        selector_ref,
        route_ref,
        live_ref,
        member_ref,
        home_ref,
    ):
        start = start_ref[...]
        basis_value = basis_ref[...]
        numbers = member_of_ref[...]
        row = iota((widest, LANES), 0)
        lane = iota((widest, LANES), 1)
        tables = []
        for round_id in range(rounds):
            wanted = jnp.zeros((widest, LANES), jnp.int32)
            for position in range(widest):
                wanted = jnp.where(row == position, blocks_ref[round_id, position], wanted)
            tables.append(hot(lane == wanted))
            live_ref[round_id * widest : (round_id + 1) * widest, :] = hot(
                row < width_ref[0, round_id]
            )
            sub_row = iota((subs, LANES), 0)
            route_ref[round_id * subs : (round_id + 1) * subs, :] = hot(
                sub_row == partner_ref[0, round_id]
            )
        table = jnp.concatenate(tables, axis=0)
        table = jnp.concatenate([table, table], axis=1).astype(BF16)
        selector_ref[...] = table
        route = route_ref[...]
        member = hot((numbers & (LANES - 1)) == iota((LANES, block_count), 0)).T
        member_ref[...] = member
        home = hot((numbers >> lane_bits) == iota((coarse_rows, LANES), 0))
        home_ref[...] = home
        own_sub = numbers >> (own_bits + part_bits)
        sub_lane = own_sub * own_aggregates + (numbers & (own_aggregates - 1))
        sub_table = hot((sub_lane & (LANES - 1)) == iota((LANES, block_count), 0)).astype(BF16)
        rows_start = spread_rounds(pick(table, start), route, subs, rounds)
        rows_basis = spread_rounds(pick(table, basis_value), route, subs, rounds)
        rows_lane = spread_rounds(
            dot_rows(table[:, :block_count], sub_table), route, subs, rounds
        )
        statistic = statistics_block(
            start, basis_value, member, home, [start], stat_rows, coarse_rows
        )
        for sub_id in range(subs):
            slot_ref[sub_id, 0:widest, :] = rows_start[sub_id]
            slot_ref[sub_id, widest : widest + stat_rows, :] = statistic
            at = widest + stat_rows
            slot_ref[sub_id, at : at + widest, :] = rows_basis[sub_id]
            slot_ref[sub_id, at + widest : at + 2 * widest, :] = rows_lane[sub_id]

    (outgoing, selector, route, live, member, home) = call(
        begin,
        [
            vmem((subs, 3 * widest + stat_rows, unknowns)),
            vmem((margin_rows, 2 * block_count), BF16),
            vmem((rounds * subs, LANES)),
            vmem((margin_rows, LANES)),
            vmem((block_count, LANES)),
            vmem((coarse_rows, LANES)),
        ],
        blocks,
        partner,
        margin_width,
        start_vector,
        basis,
        member_of,
        name="begin",
        scalars=3,
    )

    def prepare(
        blocks_ref,
        inverse_ref,
        coupling_ref,
        selector_ref,
        member_of_ref,
        weight_ref,
        pair_ref,
        target_ref,
        sub_member_ref,
        part_ref,
        piece_ref,
    ):
        for round_id in range(rounds):
            high, low = split(coupling_ref[round_id])
            pair_ref[round_id, :, 0:unknowns] = high
            pair_ref[round_id, :, unknowns : 2 * unknowns] = low
            for position in range(widest):
                at = round_id * widest + position
                high, low = split(inverse_ref[blocks_ref[round_id, position]])
                rows = slice((at % 2) * unknowns, (at % 2 + 1) * unknowns)
                weight_ref[at // 2, rows, 0:unknowns] = high
                weight_ref[at // 2, rows, unknowns : 2 * unknowns] = low
        table = selector_ref[:, 0:block_count].astype(F32)
        pieces = [table, table]
        if table_rows > 2 * margin_rows:
            pieces.append(jnp.zeros((table_rows - 2 * margin_rows, block_count), F32))
        table = jnp.concatenate(pieces, axis=0)
        target_ref[...] = jnp.concatenate(
            [table[start : start + LANES].T for start in range(0, table_rows, LANES)], axis=1
        ).astype(BF16)
        numbers = member_of_ref[...]
        own_device = numbers >> own_bits
        own_part = own_device & (parts - 1)
        own_sub = own_device >> part_bits
        sub_lane = own_sub * own_aggregates + (numbers & (own_aggregates - 1))
        for chunk in range(sub_chunks):
            sub_member_ref[:, chunk * LANES : (chunk + 1) * LANES] = hot(
                sub_lane == iota((LANES, block_count), 0) + chunk * LANES
            ).T
        part_ref[...] = hot(own_part == iota((ROWS, LANES), 0))
        order = iota((parts * piece_rows, LANES), 0)
        first = (
            ((own_sub >> part_bits) << (part_bits + own_bits))
            + ((order >> piece_bits) << own_bits)
            + ((own_sub & (parts - 1)) << piece_bits)
            + (order & (piece_rows - 1))
        )
        for chunk in range(held_rows // LANES):
            at_row = hot(first == iota((parts * piece_rows, LANES), 1) + chunk * LANES)
            at_row = at_row.astype(BF16)
            piece_ref[:, chunk * LANES : (chunk + 1) * LANES] = at_row
            piece_ref[:, held_rows + chunk * LANES : held_rows + (chunk + 1) * LANES] = at_row

    weights, pairs, target, sub_member, part_table, piece_table = call(
        prepare,
        [
            vmem((margin_rows // 2, 2 * unknowns, 2 * unknowns), BF16),
            vmem((rounds, unknowns, 2 * unknowns), BF16),
            vmem((block_count, table_rows), BF16),
            vmem((block_count, sub_aggregates)),
            vmem((ROWS, LANES)),
            vmem((parts * piece_rows, 2 * held_rows), BF16),
        ],
        blocks,
        inverse_blocks,
        coupling[0, 0],
        selector,
        member_of,
        name="prepare",
        scalars=1,
    )

    def put(target_value, values):
        high, low = split(values)
        pieces = [high, low]
        if table_rows > 2 * margin_rows:
            pieces.append(jnp.zeros((table_rows - 2 * margin_rows, unknowns), BF16))
        return dot_plain(target_value, jnp.concatenate(pieces, axis=0))

    def solve(vector_ref, inverse_ref, out_ref):
        def step(group, carry):
            rows = pl.ds(pl.multiple_of(group * ROWS, ROWS), ROWS)
            values = vector_ref[rows, :]
            lines = []
            for offset in range(ROWS):
                scaled = inverse_ref[group * ROWS + offset] * values[offset : offset + 1, :]
                lines.append(jnp.sum(scaled, axis=1)[None, :])
            out_ref[rows, :] = jnp.concatenate(lines, axis=0)
            return carry

        lax.fori_loop(0, block_count // ROWS, step, 0)

    def smooth(first):
        def kernel(
            arrived_ref,
            solved_ref,
            weight_ref,
            pair_ref,
            target_ref,
            selector_ref,
            route_ref,
            live_ref,
            part_ref,
            stat_ref,
            *refs,
        ):
            if first:
                coarse_ref, piece_ref, out_ref, slot_ref, sum_ref, basis_rows_ref, lane_rows_ref = refs
            else:
                out_ref, slot_ref, sum_ref = refs
            route = route_ref[...]
            arrived = gather_rounds(
                [arrived_ref[sub_id, 0:widest, :] for sub_id in range(subs)], route, rounds
            )
            mapped = couple(arrived, pair_ref, live_ref[...])
            row = iota((widest, unknowns), 0)
            pieces = []
            for round_id in range(rounds):
                left = paired_rows(mapped[round_id * widest : (round_id + 1) * widest])
                total = jnp.zeros((widest, unknowns), F32)
                for offset in range(widest // 2):
                    both = dot_rows(left, weight_ref[round_id * (widest // 2) + offset])
                    both = both[:widest] + both[widest:]
                    total = jnp.where(row == 2 * offset, both[:, :unknowns], total)
                    total = jnp.where(row == 2 * offset + 1, both[:, unknowns:], total)
                pieces.append(total)
            out = solved_ref[...] + put(target_ref[...], jnp.concatenate(pieces, axis=0))
            out_ref[...] = out
            slots = spread_rounds(pick(selector_ref[...], out), route, subs, rounds)
            statistic = stat_ref[0, widest : widest + stat_rows, :]
            if stat_rows < slot_rows:
                statistic = jnp.concatenate(
                    [statistic, jnp.zeros((slot_rows - stat_rows, LANES), F32)], axis=0
                )
            if first:
                passed = pick(piece_ref[...], coarse_ref[...])
            for sub_id in range(subs):
                piece = slots[sub_id]
                if widest < slot_rows:
                    piece = jnp.concatenate(
                        [piece, jnp.zeros((slot_rows - widest, unknowns), F32)], axis=0
                    )
                for part_id in range(parts):
                    slot = sub_id * parts + part_id
                    slot_ref[slot, 0:slot_rows, :] = jnp.where(
                        part_ref[part_id : part_id + 1, :] > 0.5, piece, statistic
                    )
                    if first:
                        for chunk in range(coarse_rows):
                            at = slot_rows + chunk * piece_rows
                            slot_ref[slot, at : at + piece_rows, :] = passed[
                                part_id * piece_rows : (part_id + 1) * piece_rows,
                                chunk * LANES : (chunk + 1) * LANES,
                            ]
            total = arrived_ref[0, widest : widest + stat_rows, :]
            for sub_id in range(1, subs):
                total = total + arrived_ref[sub_id, widest : widest + stat_rows, :]
            sum_ref[...] = total
            if first:
                at = widest + stat_rows
                basis_rows_ref[...] = gather_rounds(
                    [arrived_ref[sub_id, at : at + widest, :] for sub_id in range(subs)],
                    route,
                    rounds,
                )
                at = at + widest
                for chunk in range(sub_chunks):
                    lo = chunk * subs // sub_chunks
                    hi = (chunk + 1) * subs // sub_chunks
                    lane_rows_ref[chunk] = gather_rounds(
                        [
                            arrived_ref[sub_id, at : at + widest, :]
                            if lo <= sub_id < hi
                            else jnp.zeros((widest, LANES), F32)
                            for sub_id in range(subs)
                        ],
                        route,
                        rounds,
                    )

        return kernel

    def advance(step_id):
        first = step_id == 0
        last = step_id == ITERS - 1

        def kernel(*refs):
            (
                arrived_ref,
                sum_ref,
                smoothed_ref,
                vector_ref,
                sub_member_ref,
                member_ref,
                home_ref,
                basis_ref,
                basis_rows_ref,
                lane_rows_ref,
                pair_ref,
                target_ref,
                selector_ref,
                route_ref,
                live_ref,
                part_ref,
                diagonal_ref,
                link_ref,
            ) = refs[:18]
            refs = refs[18:]
            v_refs = refs[:step_id]
            z_refs = refs[step_id : 2 * step_id]
            m_refs = refs[2 * step_id : 3 * step_id]
            outs = list(refs[3 * step_id :])
            if first:
                coarse_ref = outs.pop()
                for sub_id in range(subs):
                    for part_id in range(parts):
                        row = (part_id * subs + sub_id) * piece_rows
                        for chunk in range(coarse_rows):
                            at = slot_rows + chunk * piece_rows
                            coarse_ref[
                                row : row + piece_rows, chunk * LANES : (chunk + 1) * LANES
                            ] = arrived_ref[sub_id * parts + part_id, at : at + piece_rows, :]
            else:
                coarse_ref = outs.pop(0)
            total = sum_ref[...]
            pieces = []
            for sub_id in range(subs):
                piece = jnp.zeros((widest, unknowns), F32)
                for part_id in range(parts):
                    slot = sub_id * parts + part_id
                    own = part_ref[part_id : part_id + 1, :] > 0.5
                    total = total + jnp.where(own, 0.0, arrived_ref[slot, 0:stat_rows, :])
                    piece = piece + jnp.where(own, arrived_ref[slot, 0:widest, :], 0.0)
                pieces.append(piece)
            products = jnp.sum(total[coarse_rows : coarse_rows + step_id + 1], axis=1, keepdims=True)
            heads = [products[i : i + 1] for i in range(step_id)]
            square = products[step_id : step_id + 1]
            remaining = square
            for head in heads:
                remaining = remaining - head * head
            length = jnp.sqrt(jnp.maximum(remaining, square * 1e-12))
            scale = 1.0 / length
            gathered = coarse_ref[:, 0:LANES] * total[0:1]
            for chunk in range(1, coarse_rows):
                gathered = gathered + (
                    coarse_ref[:, chunk * LANES : (chunk + 1) * LANES] * total[chunk : chunk + 1]
                )
            column = jnp.sum(gathered, axis=1, keepdims=True)
            same = iota((LANES, LANES), 0) == iota((LANES, LANES), 1)
            lines = [
                column_sum(jnp.where(same, column[start : start + LANES], 0.0))
                for start in range(0, sub_aggregates, LANES)
            ]
            own_coarse = sub_member_ref[:, 0:LANES] * lines[0]
            row_coarse = lane_rows_ref[0] * lines[0]
            for chunk in range(1, sub_chunks):
                own_coarse = own_coarse + (
                    sub_member_ref[:, chunk * LANES : (chunk + 1) * LANES] * lines[chunk]
                )
                row_coarse = row_coarse + lane_rows_ref[chunk] * lines[chunk]
            own_coarse = jnp.sum(own_coarse, axis=1, keepdims=True)
            row_coarse = jnp.sum(row_coarse, axis=1, keepdims=True)
            basis_value = basis_ref[...]
            direction = smoothed_ref[...] + own_coarse * basis_value
            for head, z_ref in zip(heads, z_refs):
                direction = direction - head * z_ref[...]
            direction = direction * scale
            route = route_ref[...]
            rows = gather_rounds(pieces, route, rounds) + row_coarse * basis_rows_ref[...]
            for head, m_ref in zip(heads, m_refs):
                rows = rows - head * m_ref[...]
            rows = rows * scale
            vector = vector_ref[...]
            for head, v_ref in zip(heads, v_refs):
                vector = vector - head * v_ref[...]
            vector = vector * scale
            product = line_product(direction, diagonal_ref[...], link_ref[...]) - put(
                target_ref[...], couple(rows, pair_ref, live_ref[...])
            )
            against = [v_ref[...] for v_ref in v_refs] + [vector, product]
            if last:
                direction_ref, head_ref, slot_ref = outs
                block = statistics_block(
                    product, basis_value, member_ref[...], home_ref[...], against, ROWS, 0
                )
                for slot in range(devices):
                    slot_ref[slot] = block
            else:
                direction_ref, head_ref, new_v_ref, margin_ref, product_ref, slot_ref = outs
                new_v_ref[...] = vector
                margin_ref[...] = rows
                product_ref[...] = product
                slots = spread_rounds(pick(selector_ref[...], product), route, subs, rounds)
                block = statistics_block(
                    product,
                    basis_value,
                    member_ref[...],
                    home_ref[...],
                    against,
                    stat_rows,
                    coarse_rows,
                )
                for sub_id in range(subs):
                    slot_ref[sub_id, 0:widest, :] = slots[sub_id]
                    slot_ref[sub_id, widest:, :] = block
            direction_ref[...] = direction
            head_ref[...] = jnp.broadcast_to(
                jnp.concatenate(
                    heads + [length] + [jnp.zeros((ROWS - step_id - 1, 1), F32)], axis=0
                ),
                (ROWS, LANES),
            )

        return kernel

    v_list = []
    z_list = []
    m_list = []
    head_list = []
    vector = start_vector
    basis_rows = lane_rows = coarse_block = None
    for step_id in range(ITERS):
        first = step_id == 0
        last = step_id == ITERS - 1
        arrived = lax.all_to_all(outgoing, "sub", 0, 0)
        (solved,) = call(solve, [vmem(full)], vector, inverse_blocks, name=f"solve{step_id}")
        outs = [
            vmem(full),
            vmem((devices, slot_rows + (extra_rows if first else 0), unknowns)),
            vmem((stat_rows, LANES)),
        ]
        if first:
            outs += [vmem((margin_rows, unknowns)), vmem((sub_chunks, margin_rows, LANES))]
        made = call(
            smooth(first),
            outs,
            arrived,
            solved,
            weights,
            pairs,
            target,
            selector,
            route,
            live,
            part_table,
            outgoing,
            *([coarse_inverse, piece_table] if first else []),
            name=f"smooth{step_id}",
        )
        smoothed, slots, sums = made[:3]
        if first:
            basis_rows, lane_rows = made[3:]
        arrived = lax.all_to_all(slots, ("sub", "coarse"), 0, 0)
        outs = [vmem(full), vmem((ROWS, LANES))]
        if last:
            outs += [vmem((devices, ROWS, LANES))]
        else:
            outs += [
                vmem(full),
                vmem((margin_rows, unknowns)),
                vmem(full),
                vmem((subs, widest + stat_rows, unknowns)),
            ]
        if first:
            outs += [vmem((sub_aggregates, aggregates))]
        made = call(
            advance(step_id),
            outs,
            arrived,
            sums,
            smoothed,
            vector,
            sub_member,
            member,
            home,
            basis,
            basis_rows,
            lane_rows,
            pairs,
            target,
            selector,
            route,
            live,
            part_table,
            diagonal_local,
            link_local,
            *v_list,
            *z_list,
            *m_list,
            *([] if first else [coarse_block]),
            name=f"advance{step_id}",
        )
        if first:
            *made, coarse_block = made
        z_list.append(made[0])
        head_list.append(made[1])
        if last:
            slots = made[2]
        else:
            v_list.append(made[2])
            m_list.append(made[3])
            vector, outgoing = made[4:]
    arrived = lax.all_to_all(slots, ("sub", "coarse"), 0, 0)

    def finish(arrived_ref, *refs):
        head_refs = refs[:ITERS]
        z_refs = refs[ITERS : 2 * ITERS]
        out_ref = refs[2 * ITERS]
        total = arrived_ref[0]
        for slot in range(1, devices):
            total = total + arrived_ref[slot]
        products = jnp.sum(total, axis=1, keepdims=True)
        heads = [products[i : i + 1] for i in range(ITERS)]
        square = products[ITERS : ITERS + 1]
        remaining = square
        for head in heads:
            remaining = remaining - head * head
        length = jnp.sqrt(jnp.maximum(remaining, square * 1e-12))
        beta = head_refs[0][0:1, 0:1]
        columns = []
        for column_id in range(1, ITERS):
            columns.append([head_refs[column_id][i : i + 1, 0:1] for i in range(column_id + 1)])
        columns.append(heads + [length])
        weights_found = givens_solve(columns, beta)
        result = weights_found[0] * z_refs[0][...]
        for position in range(1, ITERS):
            result = result + weights_found[position] * z_refs[position][...]
        out_ref[...] = result

    (answer,) = call(
        finish, [jax.ShapeDtypeStruct(full, F32)], arrived, *head_list, *z_list, name="finish"
    )
    return answer.reshape(right_side.shape)


def givens_solve(columns, beta):
    steps_count = len(columns)
    cosines = []
    sines = []
    side_terms = [beta] + [jnp.zeros_like(beta) for unused in range(steps_count)]
    triangle = []
    for column_id in range(steps_count):
        column = list(columns[column_id])
        for row_id in range(column_id):
            upper = column[row_id]
            lower = column[row_id + 1]
            column[row_id] = cosines[row_id] * upper + sines[row_id] * lower
            column[row_id + 1] = cosines[row_id] * lower - sines[row_id] * upper
        upper = column[column_id]
        lower = column[column_id + 1]
        radius = jnp.sqrt(upper * upper + lower * lower)
        cosine = upper / radius
        sine_value = lower / radius
        column[column_id] = radius
        cosines.append(cosine)
        sines.append(sine_value)
        side_terms[column_id + 1] = -sine_value * side_terms[column_id]
        side_terms[column_id] = cosine * side_terms[column_id]
        triangle.append(column)
    weights = [None] * steps_count
    for column_id in reversed(range(steps_count)):
        running = side_terms[column_id]
        for later_col in range(column_id + 1, steps_count):
            running = running - triangle[later_col][column_id] * weights[later_col]
        weights[column_id] = running / triangle[column_id][column_id]
    return weights


def solution(mesh):
    placed = (
        P("sub", "coarse", None, None),
        P("sub", "coarse", None, None),
        P("sub", "coarse", None, None),
        P("sub", "coarse", None, None, None),
        P("sub", "coarse", None, None, None),
        P("sub", "coarse", None, None),
        P("coarse", None),
        P("sub", None),
        P("sub", None),
        P("sub", "coarse", None, None),
        P("sub", "coarse", None),
    )
    return jax.shard_map(
        on_device,
        mesh=mesh,
        in_specs=placed,
        out_specs=P("sub", "coarse", None, None),
        check_vma=False,
    )
```

time: 146 us -> 139 us (0.952)
  local copies, waits for them, and re-layouts: 6.86 us -> 27.2 us
  waiting for transfers between devices: 12.9 us -> 0.01 us
  Pallas kernels: 38.4 us -> 29 us
  other arithmetic: 3.35 us -> 0 us
  blocking collectives: 69 us -> 65.7 us
    unnamed x14 -> x62, local copies, waits for them, and re-layouts: 4.95 us -> 27.2 us
    all_to_all x3 -> x0, blocking collectives: 21.6 us -> none  [on_device(): arrived = lax.all_to_all(outgoing, 'sub', 0, 0)]
    all_to_all x4 -> x5, blocking collectives: 47.3 us -> 65.7 us  [on_device(): arrived = lax.all_to_all(slots, ('sub', 'coarse'), 0, 0)]
    all_to_all x2 -> x0, waiting for transfers between devices: 10.1 us -> none  [the longest x1 10.1 us: on_device(): arrived = lax.all_to_all(slots, ('sub', 'coarse'), 0, 0)]
    all_to_all x1 -> x4, starting transfers between devices: 5.18 us -> 15.2 us  [on_device(): arrived = lax.all_to_all(outgoing, 'sub', 0, 0)]
    pallas_call x11 -> x15, Pallas kernels: 38.4 us -> 29 us  [call(): pl.pallas_call(kernel, out_shape=outs, in_specs=[scalar_spec] * scalars +...]
    all_to_all x2 -> x0, starting transfers between devices: 9.06 us -> none  [the longest x1 4.87 us: on_device(): lax.all_to_all(sent_rows, 'coarse', 0, 0)]
    all_to_all x1 -> x4, waiting for transfers between devices: 2.76 us -> 0.01 us  [on_device(): arrived = lax.all_to_all(outgoing, 'sub', 0, 0)]
  transfers between devices with their start and end apart: 3 -> 4, of which waited for: 2 -> 0; matrix products, arithmetic and copies ran while one was open for 2% -> 0% of each run, Pallas kernels for 9% -> 11%
where the time goes in v2:
time: 139 us; the launch traced here: 137 us
  blocking collectives  65.7 us (47%)
  Pallas kernels  29 us (21%)
  local copies, waits for them, and re-layouts  27.2 us (20%)
  starting transfers between devices  15.2 us (11%)
    all_to_all x5, blocking collectives, on_device(): arrived = lax.all_to_all(slots, ('sub', 'coarse'), 0, 0)  65.7 us
    pallas_call x15, Pallas kernels, call(): pl.pallas_call(kernel, out_shape=outs, in_specs=[scalar_spec] * scalars +...  29 us
    unnamed x62, local copies, waits for them, and re-layouts  27.2 us
    all_to_all x4, starting transfers between devices, on_device(): arrived = lax.all_to_all(outgoing, 'sub', 0, 0)  15.2 us
  transfers between devices with their start and end apart: 4, of which 0 were waited for; matrix products, arithmetic and copies ran while one was open for 0% of the time, Pallas kernels for 11%

profile of v2, /device:TPU:0, one launch (start us, length us, event | category | flops | bytes accessed | tf_op | source)
XLA Modules:
  0.0 137.4 jit_solution(16792017178070826802)
XLA Ops:
  4.4 1.4 %begin.1 = (f32[8,32,128]{2,1,0:T(8,128)}, bf16[32,256]{1,0:T(8,128)(2,1)S(1)}, f32[32,128]{1,0:T(8,128)S(1)}, f32[32,128]{1,0:T(8,128)S(1)}, f32[128,128]{1,0:T(8,128)S(1)}, /*index=5*/f32[4,128]{1,0:T(4,128)S(1)}) custom-call(s32[4,8]{1,0:T(4,128)S(1)} %bitcast.31, s32[1,4]{1,0:T(1,128)S(1)} %copy-done.29, s32[1,4]{1,0:T(1,128)S(1)} %copy-done.30, ...), custom_call_target="tpu_custom_call" | custom-call | tf_op jit(solution)/shard_map/begin/pallas_call | solution.py:110
  5.8 5.2 %all-to-all-start = ((f32[8,32,128]{2,1,0:T(8,128)}), f32[8,32,128]{2,1,0:T(8,128)S(1)}, u32[]{:S(2)}, u32[]{:S(2)}) async-start(f32[8,32,128]{2,1,0:T(8,128)} %get-tuple-element.53.stat_ref), calls=%async_computation | async-start | bytes 262144 | tf_op jit(solution)/shard_map/all_to_all | solution.py:587
  11.0 3.4 %copy-done = f32[1,1,128,128,128]{4,3,2,1,0:T(8,128)S(1)} copy-done((f32[1,1,128,128,128]{4,3,2,1,0:T(8,128)S(1)}, f32[1,1,128,128,128]{4,3,2,1,0:T(8,128)}, u32[]{:S(2)}) %copy-start) | copy-done | bytes 8388632
  15.2 3.4 %solve0.1.solved_ref = f32[128,128]{1,0:T(8,128)S(1)} custom-call(f32[128,128]{1,0:T(8,128)S(1)} %bitcast.28, f32[128,128,128]{2,1,0:T(8,128)S(1)} %bitcast.9), custom_call_target="tpu_custom_call" | custom-call | tf_op jit(solution)/shard_map/solve0/pallas_call | solution.py:110
  20.7 2.0 %smooth0.1 = (f32[128,128]{1,0:T(8,128)S(1)}, f32[32,24,128]{2,1,0:T(8,128)S(1)}, f32[8,128]{1,0:T(8,128)S(1)}, f32[32,128]{1,0:T(8,128)S(1)}, f32[1,32,128]{2,1,0:T(8,128)S(1)}) custom-call(f32[8,32,128]{2,1,0:T(8,128)S(1)} %all-to-all-done.arrived_ref, f32[128,128]{1,0:T(8,128)S(1)} %solve0.1.solved_ref, ...), custom_call_target="tpu_custom_call" | custom-call | tf_op jit(solution)/shard_map/smooth0/pallas_call | solution.py:110
  22.6 18.0 %all_to_all.45.refs_0_ = f32[32,24,128]{2,1,0:T(8,128)S(1)} all-to-all(f32[32,24,128]{2,1,0:T(8,128)S(1)} %get-tuple-element.62), channel_id=1, replica_groups=mesh['sub'=8,'coarse'=4] {'sub','coarse'}, dimensions={0} | all-to-all | bytes 786432 | tf_op jit(solution)/shard_map/all_to_all | solution.py:615
  40.6 1.3 advance0.1
  41.9 3.4 %all-to-all-start.2 = ((f32[8,16,128]{2,1,0:T(8,128)}), f32[8,16,128]{2,1,0:T(8,128)S(1)}, u32[]{:S(2)}, u32[]{:S(2)}) async-start(f32[8,16,128]{2,1,0:T(8,128)} %get-tuple-element.70.stat_ref), calls=%async_computation.2 | async-start | bytes 131072 | tf_op jit(solution)/shard_map/all_to_all | solution.py:587
  45.3 3.4 %copy-done.2 = f32[1,1,128,128,128]{4,3,2,1,0:T(8,128)S(1)} copy-done((f32[1,1,128,128,128]{4,3,2,1,0:T(8,128)S(1)}, f32[1,1,128,128,128]{4,3,2,1,0:T(8,128)}, u32[]{:S(2)}) %copy-start.2) | copy-done | bytes 8388632
  48.7 3.4 %solve1.1.solved_ref = f32[128,128]{1,0:T(8,128)S(1)} custom-call(f32[128,128]{1,0:T(8,128)S(1)} %get-tuple-element.71.vector_ref.refs_3_, f32[128,128,128]{2,1,0:T(8,128)S(1)} %bitcast.11), custom_call_target="tpu_custom_call" | custom-call | tf_op jit(solution)/shard_map/solve1/pallas_call | solution.py:110
  52.1 1.9 %smooth1.1 = (f32[128,128]{1,0:T(8,128)S(1)}, f32[32,8,128]{2,1,0:T(8,128)S(1)}, f32[8,128]{1,0:T(8,128)S(1)}) custom-call(f32[8,16,128]{2,1,0:T(8,128)S(1)} %all-to-all-done.2.arrived_ref, f32[128,128]{1,0:T(8,128)S(1)} %solve1.1.solved_ref, bf16[16,256,256]{2,1,0:T(8,128)(2,1)S(1)} %get-tuple-element.55.weight_ref, ...), custom_call_target="tpu_custom_call" | custom-call | tf_op jit(solution)/shard_map/smooth1/pallas_call | solution.py:110
  54.0 13.5 %all_to_all.46.refs_0_ = f32[32,8,128]{2,1,0:T(8,128)S(1)} all-to-all(f32[32,8,128]{2,1,0:T(8,128)S(1)} %get-tuple-element.72), channel_id=1, replica_groups=mesh['sub'=8,'coarse'=4] {'sub','coarse'}, dimensions={0} | all-to-all | bytes 262144 | tf_op jit(solution)/shard_map/all_to_all | solution.py:615
  69.3 3.4 %all-to-all-start.4 = ((f32[8,16,128]{2,1,0:T(8,128)}), f32[8,16,128]{2,1,0:T(8,128)S(1)}, u32[]{:S(2)}, u32[]{:S(2)}) async-start(f32[8,16,128]{2,1,0:T(8,128)} %get-tuple-element.79.stat_ref), calls=%async_computation.4 | async-start | bytes 131072 | tf_op jit(solution)/shard_map/all_to_all | solution.py:587
  72.7 3.4 %copy-done.3 = f32[1,1,128,128,128]{4,3,2,1,0:T(8,128)S(1)} copy-done((f32[1,1,128,128,128]{4,3,2,1,0:T(8,128)S(1)}, f32[1,1,128,128,128]{4,3,2,1,0:T(8,128)}, u32[]{:S(2)}) %copy-start.3) | copy-done | bytes 8388632
  76.1 3.4 %solve2.1.solved_ref = f32[128,128]{1,0:T(8,128)S(1)} custom-call(f32[128,128]{1,0:T(8,128)S(1)} %get-tuple-element.80.vector_ref.refs_3_, f32[128,128,128]{2,1,0:T(8,128)S(1)} %bitcast.12), custom_call_target="tpu_custom_call" | custom-call | tf_op jit(solution)/shard_map/solve2/pallas_call | solution.py:110
  79.5 1.9 %smooth2.1 = (f32[128,128]{1,0:T(8,128)S(1)}, f32[32,8,128]{2,1,0:T(8,128)S(1)}, f32[8,128]{1,0:T(8,128)S(1)}) custom-call(f32[8,16,128]{2,1,0:T(8,128)S(1)} %all-to-all-done.4.arrived_ref, f32[128,128]{1,0:T(8,128)S(1)} %solve2.1.solved_ref, bf16[16,256,256]{2,1,0:T(8,128)(2,1)S(1)} %get-tuple-element.55.weight_ref, ...), custom_call_target="tpu_custom_call" | custom-call | tf_op jit(solution)/shard_map/smooth2/pallas_call | solution.py:110
  81.4 12.1 %all_to_all.47.refs_0_ = f32[32,8,128]{2,1,0:T(8,128)S(1)} all-to-all(f32[32,8,128]{2,1,0:T(8,128)S(1)} %get-tuple-element.81), channel_id=1, replica_groups=mesh['sub'=8,'coarse'=4] {'sub','coarse'}, dimensions={0} | all-to-all | bytes 262144 | tf_op jit(solution)/shard_map/all_to_all | solution.py:615
  94.2 1.3 advance2.1
  97.9 3.4 %all-to-all-start.6 = ((f32[8,16,128]{2,1,0:T(8,128)}), f32[8,16,128]{2,1,0:T(8,128)S(1)}, u32[]{:S(2)}, u32[]{:S(2)}) async-start(f32[8,16,128]{2,1,0:T(8,128)} %get-tuple-element.87.stat_ref), calls=%async_computation.6 | async-start | bytes 131072 | tf_op jit(solution)/shard_map/all_to_all | solution.py:587
  101.3 3.4 %copy-done.4 = f32[1,1,128,128,128]{4,3,2,1,0:T(8,128)S(1)} copy-done((f32[1,1,128,128,128]{4,3,2,1,0:T(8,128)S(1)}, f32[1,1,128,128,128]{4,3,2,1,0:T(8,128)}, u32[]{:S(2)}) %copy-start.4) | copy-done | bytes 8388632
  104.7 3.4 %solve3.1.solved_ref = f32[128,128]{1,0:T(8,128)S(1)} custom-call(f32[128,128]{1,0:T(8,128)S(1)} %get-tuple-element.88.vector_ref.refs_3_, f32[128,128,128]{2,1,0:T(8,128)S(1)} %bitcast.13), custom_call_target="tpu_custom_call" | custom-call | tf_op jit(solution)/shard_map/solve3/pallas_call | solution.py:110
  108.1 1.9 %smooth3.1 = (f32[128,128]{1,0:T(8,128)S(1)}, f32[32,8,128]{2,1,0:T(8,128)S(1)}, f32[8,128]{1,0:T(8,128)S(1)}) custom-call(f32[8,16,128]{2,1,0:T(8,128)S(1)} %all-to-all-done.6.arrived_ref, f32[128,128]{1,0:T(8,128)S(1)} %solve3.1.solved_ref, bf16[16,256,256]{2,1,0:T(8,128)(2,1)S(1)} %get-tuple-element.55.weight_ref, ...), custom_call_target="tpu_custom_call" | custom-call | tf_op jit(solution)/shard_map/smooth3/pallas_call | solution.py:110
  110.0 12.1 %all_to_all.48.refs_0_ = f32[32,8,128]{2,1,0:T(8,128)S(1)} all-to-all(f32[32,8,128]{2,1,0:T(8,128)S(1)} %get-tuple-element.89), channel_id=1, replica_groups=mesh['sub'=8,'coarse'=4] {'sub','coarse'}, dimensions={0} | all-to-all | bytes 262144 | tf_op jit(solution)/shard_map/all_to_all | solution.py:615
  125.8 10.1 %all_to_all.49.arrived_ref = f32[32,8,128]{2,1,0:T(8,128)S(1)} all-to-all(f32[32,8,128]{2,1,0:T(8,128)S(1)} %get-tuple-element.95), channel_id=1, replica_groups=mesh['sub'=8,'coarse'=4] {'sub','coarse'}, dimensions={0} | all-to-all | bytes 262144 | tf_op jit(solution)/shard_map/all_to_all | solution.py:665
  (66 shorter events, 17.4 us)
Async XLA Ops:
  0.0 18.7 %copy-start.28 = (s32[1,1,128]{2,1,0:T(1,128)S(1)}, s32[1,1,128]{2,1,0:T(1,128)}, u32[]{:S(2)}) copy-start(s32[1,1,128]{2,1,0:T(1,128)} %param.21) | copy-start | bytes 1540
  0.0 18.7 %copy-start.24 = (s32[1,1,4,8]{3,2,1,0:T(4,128)S(1)}, s32[1,1,4,8]{3,2,1,0:T(4,128)}, u32[]{:S(2)}) copy-start(s32[1,1,4,8]{3,2,1,0:T(4,128)} %param.20) | copy-start | bytes 388
  0.0 0.9 copy-start.5
  0.9 0.8 copy-start.9
  4.4 14.3 %copy-start.12 = (f32[1,1,4,128,128]{4,3,2,1,0:T(8,128)S(1)}, f32[1,1,4,128,128]{4,3,2,1,0:T(8,128)}, u32[]{:S(2)}) copy-start(f32[1,1,4,128,128]{4,3,2,1,0:T(8,128)} %param.15) | copy-start | bytes 786436
  5.8 13.9 %all-to-all-start = ((f32[8,32,128]{2,1,0:T(8,128)}), f32[8,32,128]{2,1,0:T(8,128)S(1)}, u32[]{:S(2)}, u32[]{:S(2)}) async-start(f32[8,32,128]{2,1,0:T(8,128)} %get-tuple-element.53.stat_ref), calls=%async_computation | async-start | bytes 262144 | tf_op jit(solution)/shard_map/all_to_all | solution.py:587
  11.0 3.4 %copy-start = (f32[1,1,128,128,128]{4,3,2,1,0:T(8,128)S(1)}, f32[1,1,128,128,128]{4,3,2,1,0:T(8,128)}, u32[]{:S(2)}) copy-start(f32[1,1,128,128,128]{4,3,2,1,0:T(8,128)} %param.14) | copy-start | bytes 25165828
  14.3 0.8 copy-start.10
  15.2 3.5 %copy-start.1 = (f32[1,1,128,128,128]{4,3,2,1,0:T(8,128)S(1)}, f32[1,1,128,128,128]{4,3,2,1,0:T(8,128)}, u32[]{:S(2)}) copy-start(f32[1,1,128,128,128]{4,3,2,1,0:T(8,128)} %param.14) | copy-start | bytes 25165828
  18.6 22.0 %copy-start.6 = (f32[1,1,128,128]{3,2,1,0:T(8,128)S(1)}, f32[1,1,128,128]{3,2,1,0:T(8,128)}, u32[]{:S(2)}) copy-start(f32[1,1,128,128]{3,2,1,0:T(8,128)} %param.16) | copy-start | bytes 196612
  18.6 22.0 %copy-start.7 = (f32[1,1,128,128]{3,2,1,0:T(8,128)S(1)}, f32[1,1,128,128]{3,2,1,0:T(8,128)}, u32[]{:S(2)}) copy-start(f32[1,1,128,128]{3,2,1,0:T(8,128)} %param.12) | copy-start | bytes 196612
  18.6 22.0 %copy-start.8 = (f32[1,1,128,128]{3,2,1,0:T(8,128)S(1)}, f32[1,1,128,128]{3,2,1,0:T(8,128)}, u32[]{:S(2)}) copy-start(f32[1,1,128,128]{3,2,1,0:T(8,128)} %param.13) | copy-start | bytes 196612
  18.7 21.9 %copy-start.11 = (f32[1,1,128,128]{3,2,1,0:T(8,128)S(1)}, f32[1,1,128,128]{3,2,1,0:T(8,128)}, u32[]{:S(2)}) copy-start(f32[1,1,128,128]{3,2,1,0:T(8,128)} %param.11) | copy-start | bytes 196612
  19.7 1.0 copy-start.13
  41.9 10.2 %all-to-all-start.2 = ((f32[8,16,128]{2,1,0:T(8,128)}), f32[8,16,128]{2,1,0:T(8,128)S(1)}, u32[]{:S(2)}, u32[]{:S(2)}) async-start(f32[8,16,128]{2,1,0:T(8,128)} %get-tuple-element.70.stat_ref), calls=%async_computation.2 | async-start | bytes 131072 | tf_op jit(solution)/shard_map/all_to_all | solution.py:587
  45.3 3.4 %copy-start.2 = (f32[1,1,128,128,128]{4,3,2,1,0:T(8,128)S(1)}, f32[1,1,128,128,128]{4,3,2,1,0:T(8,128)}, u32[]{:S(2)}) copy-start(f32[1,1,128,128,128]{4,3,2,1,0:T(8,128)} %param.14) | copy-start | bytes 25165828
  69.3 10.2 %all-to-all-start.4 = ((f32[8,16,128]{2,1,0:T(8,128)}), f32[8,16,128]{2,1,0:T(8,128)S(1)}, u32[]{:S(2)}, u32[]{:S(2)}) async-start(f32[8,16,128]{2,1,0:T(8,128)} %get-tuple-element.79.stat_ref), calls=%async_computation.4 | async-start | bytes 131072 | tf_op jit(solution)/shard_map/all_to_all | solution.py:587
  72.7 3.4 %copy-start.3 = (f32[1,1,128,128,128]{4,3,2,1,0:T(8,128)S(1)}, f32[1,1,128,128,128]{4,3,2,1,0:T(8,128)}, u32[]{:S(2)}) copy-start(f32[1,1,128,128,128]{4,3,2,1,0:T(8,128)} %param.14) | copy-start | bytes 25165828
  93.5 0.7 copy-start.17
  97.9 10.2 %all-to-all-start.6 = ((f32[8,16,128]{2,1,0:T(8,128)}), f32[8,16,128]{2,1,0:T(8,128)S(1)}, u32[]{:S(2)}, u32[]{:S(2)}) async-start(f32[8,16,128]{2,1,0:T(8,128)} %get-tuple-element.87.stat_ref), calls=%async_computation.6 | async-start | bytes 131072 | tf_op jit(solution)/shard_map/all_to_all | solution.py:587
  101.3 3.4 %copy-start.4 = (f32[1,1,128,128,128]{4,3,2,1,0:T(8,128)S(1)}, f32[1,1,128,128,128]{4,3,2,1,0:T(8,128)}, u32[]{:S(2)}) copy-start(f32[1,1,128,128,128]{4,3,2,1,0:T(8,128)} %param.14) | copy-start | bytes 25165828
  122.1 0.8 copy-start.15
  122.9 0.7 copy-start.18
  123.6 0.8 copy-start.20
  (11 other events, 7.1 us)

commit v3 on v2

v3 whole, which is shorter than its diff:
```python
import jax
import jax.numpy as jnp
from jax import lax
from jax.experimental import pallas as pl
from jax.experimental.pallas import tpu as pltpu
from jax.sharding import PartitionSpec as P

BS = 128
BPD = 128
AGG_DEV = 16
ITERS = 4
LANES = 128
ROWS = 8
BF16 = jnp.bfloat16
F32 = jnp.float32


def split(values):
    high = values.astype(BF16)
    low = (values - high.astype(F32)).astype(BF16)
    return high, low


def dot_rows(left, right):
    return lax.dot_general(left, right, (((1,), (1,)), ((), ())), preferred_element_type=F32)


def dot_plain(left, right):
    return lax.dot_general(left, right, (((1,), (0,)), ((), ())), preferred_element_type=F32)


def paired_rows(values):
    high, low = split(values)
    return jnp.concatenate(
        [
            jnp.concatenate([high, high], axis=1),
            jnp.concatenate([low, jnp.zeros_like(low)], axis=1),
        ],
        axis=0,
    )


def pick(selector, values):
    high, low = split(values)
    return dot_plain(selector, jnp.concatenate([high, low], axis=0))


def column_sum(values):
    return jnp.sum(values, axis=0, keepdims=True)


def line_product(values, diagonal, link):
    rows = values.shape[0]
    lanes = values.shape[1]
    row = lax.broadcasted_iota(jnp.int32, values.shape, 0)
    lane = lax.broadcasted_iota(jnp.int32, values.shape, 1)
    next_lane = pltpu.roll(values, lanes - 1, 1)
    next_row = pltpu.roll(next_lane, rows - 1, 0)
    ahead = jnp.where(lane < lanes - 1, next_lane, jnp.where(row < rows - 1, next_row, 0.0))
    scaled = link * values
    last_lane = pltpu.roll(scaled, 1, 1)
    last_row = pltpu.roll(last_lane, 1, 0)
    behind = jnp.where(lane > 0, last_lane, jnp.where(row > 0, last_row, 0.0))
    return diagonal * values - (ahead * link + behind)


def couple(arrived, pair_ref, live):
    rounds = pair_ref.shape[0]
    widest = arrived.shape[0] // rounds
    pieces = []
    for round_id in range(rounds):
        left = paired_rows(arrived[round_id * widest : (round_id + 1) * widest])
        both = dot_rows(left, pair_ref[round_id])
        pieces.append(both[:widest] + both[widest:])
    return jnp.concatenate(pieces, axis=0) * live


def gather_rounds(slots, route, rounds):
    pieces = []
    for round_id in range(rounds):
        total = None
        for sub_id, piece in enumerate(slots):
            at = round_id * len(slots) + sub_id
            term = route[at : at + 1] * piece
            total = term if total is None else total + term
        pieces.append(total)
    return jnp.concatenate(pieces, axis=0)


def spread_rounds(values, route, subs, rounds):
    widest = values.shape[0] // rounds
    slots = []
    for sub_id in range(subs):
        total = None
        for round_id in range(rounds):
            at = round_id * subs + sub_id
            term = route[at : at + 1] * values[round_id * widest : (round_id + 1) * widest]
            total = term if total is None else total + term
        slots.append(total)
    return slots


def vmem(shape, dtype=F32):
    return pltpu.VMEM(shape, dtype)


def call(kernel, outs, *args, name, places="", out_places="", aliases=None, scratch=()):
    places = places + "v" * (len(args) - len(places))
    spaces = {"s": pltpu.SMEM, "h": pltpu.HBM, "v": pltpu.VMEM}
    return pl.pallas_call(
        kernel,
        out_shape=outs,
        in_specs=[pl.BlockSpec(memory_space=spaces[place]) for place in places],
        out_specs=[
            pl.BlockSpec(memory_space=pltpu.HBM if place == "h" else pltpu.VMEM)
            for place in (out_places or "v" * len(outs))
        ],
        input_output_aliases=aliases or {},
        scratch_shapes=list(scratch),
        name=name,
        compiler_params=pltpu.CompilerParams(vmem_limit_bytes=16 * 1024 * 1024),
    )(
        *[
            pltpu.with_memory_space_constraint(
                arg, pltpu.VMEM if place == "v" else pltpu.HBM
            )
            for arg, place in zip(args, places)
        ]
    )


def on_device(
    right_side,
    diagonal,
    cell_link,
    block_inverse,
    coupling,
    coarse_basis,
    coarse_inverse,
    partner,
    margin_width,
    margin_blocks,
    aggregate,
):
    subs = lax.axis_size("sub")
    parts = lax.axis_size("coarse")
    devices = subs * parts
    block_count = right_side.shape[2]
    unknowns = right_side.shape[3]
    rounds = margin_blocks.shape[2]
    widest = margin_blocks.shape[3]
    aggregates = coarse_inverse.shape[1]
    own_aggregates = aggregates // devices
    sub_aggregates = subs * own_aggregates
    sub_chunks = sub_aggregates // LANES
    sub_span = subs // parts
    chunk_rows = sub_span * own_aggregates
    factor = (BS * BPD / AGG_DEV) ** (-0.5)
    coarse_rows = aggregates // LANES
    stat_rows = -(-(coarse_rows + ITERS) // ROWS) * ROWS
    slot_rows = max(widest, stat_rows)
    margin_rows = rounds * widest
    table_rows = -(-2 * margin_rows // LANES) * LANES
    full = (block_count, unknowns)

    v_at = 0
    m_at = v_at + (ITERS - 1) * block_count
    head_at = m_at + (ITERS - 1) * margin_rows
    state_rows = head_at + ITERS * ROWS
    blocks = margin_blocks[0, 0]
    member_of = aggregate[0]
    own_bits = own_aggregates.bit_length() - 1
    part_bits = parts.bit_length() - 1
    span_bits = sub_span.bit_length() - 1
    lane_bits = LANES.bit_length() - 1
    assert own_aggregates == 1 << own_bits and parts == 1 << part_bits
    assert sub_span == 1 << span_bits and sub_span * parts == subs

    def iota(shape, dim):
        return lax.broadcasted_iota(jnp.int32, shape, dim)

    def hot(condition):
        return jnp.where(condition, 1.0, 0.0).astype(F32)

    def coarse_lane(numbers):
        own_device = numbers >> own_bits
        own_part = own_device & (parts - 1)
        own_sub = own_device >> part_bits
        turn = (own_part - (own_sub >> span_bits)) & (parts - 1)
        return (
            turn * chunk_rows
            + (own_sub & (sub_span - 1)) * own_aggregates
            + (numbers & (own_aggregates - 1))
        )

    def statistics_block(vector, basis_value, member_value, home, dots, rows, count):
        lines = []
        if count:
            inner = jnp.sum(basis_value * vector, axis=1, keepdims=True)
            line = column_sum(inner * member_value) * factor
            lines = [home[chunk : chunk + 1] * line for chunk in range(count)]
        lines += [column_sum(other * vector) for other in dots]
        if len(lines) < rows:
            lines.append(jnp.zeros((rows - len(lines), LANES), F32))
        return jnp.concatenate(lines, axis=0)

    def begin(
        blocks_ref,
        partner_ref,
        width_ref,
        number_ref,
        start_hbm,
        basis_hbm,
        member_of_hbm,
        coarse_hbm,
        *refs,
    ):
        (
            slot_ref,
            selector_ref,
            route_ref,
            live_ref,
            member_ref,
            home_ref,
            start_ref,
            basis_ref,
            member_of_ref,
        ) = refs[:9]
        chunk_refs = refs[9 : 9 + parts]
        semaphores = refs[9 + parts]
        copies = [
            pltpu.make_async_copy(source, to, semaphores.at[position])
            for position, (source, to) in enumerate(
                [(start_hbm, start_ref), (basis_hbm, basis_ref), (member_of_hbm, member_of_ref)]
            )
        ]
        own_part = (number_ref[0, 0] >> own_bits) & (parts - 1)
        chunk_copies = []
        for turn, chunk_ref in enumerate(chunk_refs):
            to_part = (own_part + turn) & (parts - 1)
            for span in range(sub_span):
                first = pl.multiple_of((span * parts + to_part) * own_aggregates, own_aggregates)
                chunk_copies.append(
                    pltpu.make_async_copy(
                        coarse_hbm.at[pl.ds(first, own_aggregates), :],
                        chunk_ref.at[pl.ds(span * own_aggregates, own_aggregates), :],
                        semaphores.at[3 + turn * sub_span + span],
                    )
                )
        for copy in copies + chunk_copies:
            copy.start()
        row = iota((widest, LANES), 0)
        lane = iota((widest, LANES), 1)
        tables = []
        for round_id in range(rounds):
            wanted = jnp.zeros((widest, LANES), jnp.int32)
            for position in range(widest):
                wanted = jnp.where(row == position, blocks_ref[round_id, position], wanted)
            tables.append(hot(lane == wanted))
            live_ref[round_id * widest : (round_id + 1) * widest, :] = hot(
                row < width_ref[0, round_id]
            )
            sub_row = iota((subs, LANES), 0)
            route_ref[round_id * subs : (round_id + 1) * subs, :] = hot(
                sub_row == partner_ref[0, round_id]
            )
        for copy in copies:
            copy.wait()
        start = start_ref[...]
        basis_value = basis_ref[...]
        numbers = member_of_ref[...]
        table = jnp.concatenate(tables, axis=0)
        table = jnp.concatenate([table, table], axis=1).astype(BF16)
        selector_ref[...] = table
        route = route_ref[...]
        member = hot((numbers & (LANES - 1)) == iota((LANES, block_count), 0)).T
        member_ref[...] = member.astype(BF16)
        home = hot((numbers >> lane_bits) == iota((coarse_rows, LANES), 0))
        home_ref[...] = home
        own_lane = coarse_lane(numbers)
        rows_start = spread_rounds(pick(table, start), route, subs, rounds)
        rows_basis = spread_rounds(pick(table, basis_value), route, subs, rounds)
        rows_lane = []
        for chunk in range(sub_chunks):
            lane_table = hot(own_lane == iota((LANES, block_count), 0) + chunk * LANES)
            rows_lane.append(
                spread_rounds(
                    dot_rows(table[:, :block_count], lane_table.astype(BF16)), route, subs, rounds
                )
            )
        statistic = statistics_block(
            start, basis_value, member, home, [start], stat_rows, coarse_rows
        )
        for sub_id in range(subs):
            slot_ref[sub_id, 0:widest, :] = rows_start[sub_id]
            slot_ref[sub_id, widest : widest + stat_rows, :] = statistic
            at = widest + stat_rows
            slot_ref[sub_id, at : at + widest, :] = rows_basis[sub_id]
            for chunk in range(sub_chunks):
                at = at + widest
                slot_ref[sub_id, at : at + widest, :] = rows_lane[chunk][sub_id]
        for copy in chunk_copies:
            copy.wait()

    (
        outgoing,
        selector,
        route,
        live,
        member,
        home,
        start_vector,
        basis,
        member_of,
        *coarse_chunks,
    ) = call(
        begin,
        [
            vmem((subs, (2 + sub_chunks) * widest + stat_rows, unknowns)),
            vmem((margin_rows, 2 * block_count), BF16),
            vmem((rounds * subs, LANES)),
            vmem((margin_rows, LANES)),
            vmem((block_count, LANES), BF16),
            vmem((coarse_rows, LANES)),
            vmem(full),
            vmem(full),
            vmem((1, block_count), jnp.int32),
        ]
        + [vmem((chunk_rows, aggregates))] * parts,
        blocks,
        partner,
        margin_width,
        aggregate[0],
        right_side[0, 0],
        coarse_basis[0, 0],
        aggregate[0],
        coarse_inverse,
        name="begin",
        places="sssshhhh",
        scratch=[pltpu.SemaphoreType.DMA((3 + parts * sub_span,))],
    )
    for turn in range(1, parts):
        coarse_chunks[turn] = lax.ppermute(
            coarse_chunks[turn], "coarse", [(i, (i + turn) % parts) for i in range(parts)]
        )

    def solve_group(group, vector_ref, inverse_ref, out_ref):
        rows = pl.ds(pl.multiple_of(group * ROWS, ROWS), ROWS)
        values = vector_ref[rows, :]
        lines = []
        for offset in range(ROWS):
            scaled = inverse_ref[group * ROWS + offset] * values[offset : offset + 1, :]
            lines.append(jnp.sum(scaled, axis=1)[None, :])
        out_ref[rows, :] = jnp.concatenate(lines, axis=0)

    def solve(vector_ref, inverse_hbm, out_ref, inverse_ref, semaphores):
        def group_copy(group):
            rows = pl.ds(group * ROWS, ROWS)
            return pltpu.make_async_copy(
                inverse_hbm.at[rows], inverse_ref.at[rows], semaphores.at[group]
            )

        for group in range(block_count // ROWS):
            group_copy(group).start()

        def step(group, carry):
            group_copy(group).wait()
            solve_group(group, vector_ref, inverse_ref, out_ref)
            return carry

        lax.fori_loop(0, block_count // ROWS, step, 0)

    def prepare(
        blocks_ref,
        inverse_hbm,
        coupling_hbm,
        diagonal_hbm,
        link_hbm,
        selector_ref,
        member_of_ref,
        weight_ref,
        pair_ref,
        target_ref,
        sub_member_ref,
        part_ref,
        diagonal_ref,
        link_ref,
        inverse_ref,
        coupling_ref,
        semaphores,
        block_semaphores,
    ):
        copies = [
            pltpu.make_async_copy(source, to, semaphores.at[position])
            for position, (source, to) in enumerate(
                [
                    (coupling_hbm, coupling_ref),
                    (diagonal_hbm, diagonal_ref),
                    (link_hbm, link_ref),
                ]
            )
        ]
        block_copies = [
            pltpu.make_async_copy(
                inverse_hbm.at[blocks_ref[at // widest, at % widest]],
                inverse_ref.at[at],
                block_semaphores.at[at],
            )
            for at in range(margin_rows)
        ]
        for copy in copies + block_copies:
            copy.start()
        table = selector_ref[:, 0:block_count].astype(F32)
        pieces = [table, table]
        if table_rows > 2 * margin_rows:
            pieces.append(jnp.zeros((table_rows - 2 * margin_rows, block_count), F32))
        table = jnp.concatenate(pieces, axis=0)
        target_ref[...] = jnp.concatenate(
            [table[start : start + LANES].T for start in range(0, table_rows, LANES)], axis=1
        ).astype(BF16)
        numbers = member_of_ref[...]
        own_lane = coarse_lane(numbers)
        for chunk in range(sub_chunks):
            sub_member_ref[:, chunk * LANES : (chunk + 1) * LANES] = hot(
                own_lane == iota((LANES, block_count), 0) + chunk * LANES
            ).T.astype(BF16)
        part_ref[...] = hot(
            ((numbers >> own_bits) & (parts - 1)) == iota((ROWS, LANES), 0)
        )
        copies[0].wait()
        for round_id in range(rounds):
            high, low = split(coupling_ref[round_id])
            pair_ref[round_id, :, 0:unknowns] = high
            pair_ref[round_id, :, unknowns : 2 * unknowns] = low
        for at in range(margin_rows):
            block_copies[at].wait()
            high, low = split(inverse_ref[at])
            rows = slice((at % 2) * unknowns, (at % 2 + 1) * unknowns)
            weight_ref[at // 2, rows, 0:unknowns] = high
            weight_ref[at // 2, rows, unknowns : 2 * unknowns] = low
        for copy in copies[1:]:
            copy.wait()

    inverse_blocks = block_inverse[0, 0]
    weights, pairs, target, sub_member, part_table, diagonal_local, link_local = call(
        prepare,
        [
            vmem((margin_rows // 2, 2 * unknowns, 2 * unknowns), BF16),
            vmem((rounds, unknowns, 2 * unknowns), BF16),
            vmem((block_count, table_rows), BF16),
            vmem((block_count, sub_aggregates), BF16),
            vmem((ROWS, LANES)),
            vmem(full),
            vmem(full),
        ],
        blocks,
        inverse_blocks,
        coupling[0, 0],
        diagonal[0, 0],
        cell_link[0, 0],
        selector,
        member_of,
        name="prepare",
        places="shhhh",
        scratch=[
            vmem((margin_rows, unknowns, unknowns)),
            vmem((rounds, unknowns, unknowns)),
            pltpu.SemaphoreType.DMA((3,)),
            pltpu.SemaphoreType.DMA((margin_rows,)),
        ],
    )

    def put(target_value, values):
        high, low = split(values)
        pieces = [high, low]
        if table_rows > 2 * margin_rows:
            pieces.append(jnp.zeros((table_rows - 2 * margin_rows, unknowns), BF16))
        return dot_plain(target_value, jnp.concatenate(pieces, axis=0))

    def smooth(first):
        def kernel(
            arrived_ref,
            solved_ref,
            weight_ref,
            pair_ref,
            target_ref,
            selector_ref,
            route_ref,
            live_ref,
            part_ref,
            stat_ref,
            *refs,
        ):
            if first:
                out_ref, slot_ref, sum_ref, basis_rows_ref, lane_rows_ref = refs
            else:
                unused_in, out_ref, slot_ref, sum_ref, unused_out = refs
            route = route_ref[...]
            arrived = gather_rounds(
                [arrived_ref[sub_id, 0:widest, :] for sub_id in range(subs)], route, rounds
            )
            mapped = couple(arrived, pair_ref, live_ref[...])
            row = iota((widest, unknowns), 0)
            pieces = []
            for round_id in range(rounds):
                left = paired_rows(mapped[round_id * widest : (round_id + 1) * widest])
                total = jnp.zeros((widest, unknowns), F32)
                for offset in range(widest // 2):
                    both = dot_rows(left, weight_ref[round_id * (widest // 2) + offset])
                    both = both[:widest] + both[widest:]
                    total = jnp.where(row == 2 * offset, both[:, :unknowns], total)
                    total = jnp.where(row == 2 * offset + 1, both[:, unknowns:], total)
                pieces.append(total)
            out = solved_ref[...] + put(target_ref[...], jnp.concatenate(pieces, axis=0))
            out_ref[...] = out
            slots = spread_rounds(pick(selector_ref[...], out), route, subs, rounds)
            statistic = stat_ref[0, widest : widest + stat_rows, :]
            if stat_rows < slot_rows:
                statistic = jnp.concatenate(
                    [statistic, jnp.zeros((slot_rows - stat_rows, LANES), F32)], axis=0
                )
            for sub_id in range(subs):
                piece = slots[sub_id]
                if widest < slot_rows:
                    piece = jnp.concatenate(
                        [piece, jnp.zeros((slot_rows - widest, unknowns), F32)], axis=0
                    )
                for part_id in range(parts):
                    slot = sub_id * parts + part_id
                    slot_ref[slot, 0:slot_rows, :] = jnp.where(
                        part_ref[part_id : part_id + 1, :] > 0.5, piece, statistic
                    )
            total = arrived_ref[0, widest : widest + stat_rows, :]
            for sub_id in range(1, subs):
                total = total + arrived_ref[sub_id, widest : widest + stat_rows, :]
            sum_ref[...] = total
            if first:
                at = widest + stat_rows
                basis_rows_ref[...] = gather_rounds(
                    [arrived_ref[sub_id, at : at + widest, :] for sub_id in range(subs)],
                    route,
                    rounds,
                )
                for chunk in range(sub_chunks):
                    at = at + widest
                    lane_rows_ref[chunk] = gather_rounds(
                        [arrived_ref[sub_id, at : at + widest, :] for sub_id in range(subs)],
                        route,
                        rounds,
                    )

        return kernel

    def advance(step_id):
        first = step_id == 0
        last = step_id == ITERS - 1

        def kernel(*refs):
            (
                arrived_ref,
                sum_ref,
                smoothed_ref,
                vector_ref,
                sub_member_ref,
                member_ref,
                home_ref,
                basis_ref,
                basis_rows_ref,
                lane_rows_ref,
                pair_ref,
                target_ref,
                selector_ref,
                route_ref,
                live_ref,
                part_ref,
                diagonal_ref,
                link_ref,
            ) = refs[:18]
            coarse_refs = refs[18 : 18 + parts]
            refs = refs[18 + parts :]
            z_hbms = refs[:step_id]
            if not first:
                state_in = refs[step_id]
                refs = refs[step_id + 1 :]
            *outs, z_hbm, state_ref, z_ref, semaphores = refs
            z_copies = [
                pltpu.make_async_copy(source, z_ref.at[number], semaphores.at[number])
                for number, source in enumerate(z_hbms)
            ]
            for copy in z_copies:
                copy.start()

            def held(at, number, rows):
                return state_in[at + number * rows : at + (number + 1) * rows, :]

            def keep(at, number, values):
                rows = values.shape[0]
                state_ref[at + number * rows : at + (number + 1) * rows, :] = values

            total = sum_ref[...]
            pieces = []
            for sub_id in range(subs):
                piece = jnp.zeros((widest, unknowns), F32)
                for part_id in range(parts):
                    slot = sub_id * parts + part_id
                    own = part_ref[part_id : part_id + 1, :] > 0.5
                    total = total + jnp.where(own, 0.0, arrived_ref[slot, 0:stat_rows, :])
                    piece = piece + jnp.where(own, arrived_ref[slot, 0:widest, :], 0.0)
                pieces.append(piece)
            products = jnp.sum(total[coarse_rows : coarse_rows + step_id + 1], axis=1, keepdims=True)
            heads = [products[i : i + 1] for i in range(step_id)]
            square = products[step_id : step_id + 1]
            remaining = square
            for head in heads:
                remaining = remaining - head * head
            length = jnp.sqrt(jnp.maximum(remaining, square * 1e-12))
            scale = 1.0 / length
            gathered = []
            for coarse_ref in coarse_refs:
                piece = coarse_ref[:, 0:LANES] * total[0:1]
                for chunk in range(1, coarse_rows):
                    piece = piece + (
                        coarse_ref[:, chunk * LANES : (chunk + 1) * LANES] * total[chunk : chunk + 1]
                    )
                gathered.append(piece)
            gathered = jnp.concatenate(gathered, axis=0)
            column = jnp.sum(gathered, axis=1, keepdims=True)
            same = iota((LANES, LANES), 0) == iota((LANES, LANES), 1)
            lines = [
                column_sum(jnp.where(same, column[start : start + LANES], 0.0))
                for start in range(0, sub_aggregates, LANES)
            ]
            own_coarse = sub_member_ref[:, 0:LANES].astype(F32) * lines[0]
            row_coarse = lane_rows_ref[0] * lines[0]
            for chunk in range(1, sub_chunks):
                own_coarse = own_coarse + (
                    sub_member_ref[:, chunk * LANES : (chunk + 1) * LANES].astype(F32) * lines[chunk]
                )
                row_coarse = row_coarse + lane_rows_ref[chunk] * lines[chunk]
            own_coarse = jnp.sum(own_coarse, axis=1, keepdims=True)
            row_coarse = jnp.sum(row_coarse, axis=1, keepdims=True)
            basis_value = basis_ref[...]
            direction = smoothed_ref[...] + own_coarse * basis_value
            for number, head in enumerate(heads):
                z_copies[number].wait()
                direction = direction - head * z_ref[number]
            direction = direction * scale
            z_ref[step_id] = direction
            z_copy = pltpu.make_async_copy(z_ref.at[step_id], z_hbm, semaphores.at[step_id])
            z_copy.start()
            route = route_ref[...]
            rows = gather_rounds(pieces, route, rounds) + row_coarse * basis_rows_ref[...]
            for number, head in enumerate(heads):
                rows = rows - head * held(m_at, number, margin_rows)
            rows = rows * scale
            vector = vector_ref[...]
            earlier = [held(v_at, number, block_count) for number in range(step_id)]
            for head, other in zip(heads, earlier):
                vector = vector - head * other
            vector = vector * scale
            product = line_product(direction, diagonal_ref[...], link_ref[...]) - put(
                target_ref[...], couple(rows, pair_ref, live_ref[...])
            )
            against = earlier + [vector, product]
            if last:
                (slot_ref,) = outs
                block = statistics_block(
                    product, basis_value, None, home_ref[...], against, ROWS, 0
                )
                for slot in range(devices):
                    slot_ref[slot] = block
            else:
                product_ref, slot_ref = outs
                keep(v_at, step_id, vector)
                keep(m_at, step_id, rows)
                product_ref[...] = product
                slots = spread_rounds(pick(selector_ref[...], product), route, subs, rounds)
                block = statistics_block(
                    product,
                    basis_value,
                    member_ref[...].astype(F32),
                    home_ref[...],
                    against,
                    stat_rows,
                    coarse_rows,
                )
                for sub_id in range(subs):
                    slot_ref[sub_id, 0:widest, :] = slots[sub_id]
                    slot_ref[sub_id, widest:, :] = block
            keep(
                head_at,
                step_id,
                jnp.broadcast_to(
                    jnp.concatenate(
                        heads + [length] + [jnp.zeros((ROWS - step_id - 1, 1), F32)], axis=0
                    ),
                    (ROWS, LANES),
                ),
            )
            z_copy.wait()

        return kernel

    vector = start_vector
    state = None
    z_list = []
    state_shape = vmem((state_rows, LANES))
    for step_id in range(ITERS):
        first = step_id == 0
        last = step_id == ITERS - 1
        arrived = lax.all_to_all(outgoing, "sub", 0, 0)
        (solved,) = call(
            solve,
            [vmem(full)],
            vector,
            inverse_blocks,
            name=f"solve{step_id}",
            places="vh",
            scratch=[
                vmem((block_count, unknowns, unknowns)),
                pltpu.SemaphoreType.DMA((block_count // ROWS,)),
            ],
        )
        outs = [vmem(full), vmem((devices, slot_rows, unknowns)), vmem((stat_rows, LANES))]
        if first:
            outs += [vmem((margin_rows, unknowns)), vmem((sub_chunks, margin_rows, LANES))]
        else:
            outs += [state_shape]
        made = call(
            smooth(first),
            outs,
            arrived,
            solved,
            weights,
            pairs,
            target,
            selector,
            route,
            live,
            part_table,
            outgoing,
            *([] if first else [state]),
            name=f"smooth{step_id}",
            aliases={} if first else {10: 3},
        )
        if first:
            smoothed, slots, sums, basis_rows, lane_rows = made
        else:
            smoothed, slots, sums, state = made
        arrived = lax.all_to_all(slots, ("sub", "coarse"), 0, 0)
        if last:
            outs = [vmem((devices, ROWS, LANES))]
        else:
            outs = [vmem(full), vmem((subs, widest + stat_rows, unknowns))]
        outs += [pltpu.HBM(full, F32), state_shape]
        made = call(
            advance(step_id),
            outs,
            arrived,
            sums,
            smoothed,
            vector,
            sub_member,
            member,
            home,
            basis,
            basis_rows,
            lane_rows,
            pairs,
            target,
            selector,
            route,
            live,
            part_table,
            diagonal_local,
            link_local,
            *coarse_chunks,
            *z_list,
            *([] if first else [state]),
            name=f"advance{step_id}",
            places="v" * (18 + parts) + "h" * step_id,
            out_places="v" * (len(outs) - 2) + "hv",
            aliases={} if first else {18 + parts + step_id: len(outs) - 1},
            scratch=[
                vmem((step_id + 1, block_count, unknowns)),
                pltpu.SemaphoreType.DMA((step_id + 1,)),
            ],
        )
        *made, z_new, state = made
        z_list.append(z_new)
        if last:
            (slots,) = made
        else:
            vector, outgoing = made
    arrived = lax.all_to_all(slots, ("sub", "coarse"), 0, 0)

    def finish(arrived_ref, state_ref, *refs):
        z_hbms = refs[:ITERS]
        out_ref, z_ref, semaphores = refs[ITERS:]
        z_copies = [
            pltpu.make_async_copy(source, z_ref.at[number], semaphores.at[number])
            for number, source in enumerate(z_hbms)
        ]
        for copy in z_copies:
            copy.start()
        total = arrived_ref[0]
        for slot in range(1, devices):
            total = total + arrived_ref[slot]
        products = jnp.sum(total, axis=1, keepdims=True)
        heads = [products[i : i + 1] for i in range(ITERS)]
        square = products[ITERS : ITERS + 1]
        remaining = square
        for head in heads:
            remaining = remaining - head * head
        length = jnp.sqrt(jnp.maximum(remaining, square * 1e-12))
        beta = state_ref[head_at : head_at + 1, 0:1]
        columns = []
        for column_id in range(1, ITERS):
            at = head_at + column_id * ROWS
            columns.append([state_ref[at + i : at + i + 1, 0:1] for i in range(column_id + 1)])
        columns.append(heads + [length])
        weights_found = givens_solve(columns, beta)
        result = None
        for position in range(ITERS):
            z_copies[position].wait()
            term = weights_found[position] * z_ref[position]
            result = term if result is None else result + term
        out_ref[...] = result

    (answer,) = call(
        finish,
        [jax.ShapeDtypeStruct(full, F32)],
        arrived,
        state,
        *z_list,
        name="finish",
        places="vv" + "h" * ITERS,
        scratch=[vmem((ITERS,) + full), pltpu.SemaphoreType.DMA((ITERS,))],
    )
    return answer.reshape(right_side.shape)


def givens_solve(columns, beta):
    steps_count = len(columns)
    cosines = []
    sines = []
    side_terms = [beta] + [jnp.zeros_like(beta) for unused in range(steps_count)]
    triangle = []
    for column_id in range(steps_count):
        column = list(columns[column_id])
        for row_id in range(column_id):
            upper = column[row_id]
            lower = column[row_id + 1]
            column[row_id] = cosines[row_id] * upper + sines[row_id] * lower
            column[row_id + 1] = cosines[row_id] * lower - sines[row_id] * upper
        upper = column[column_id]
        lower = column[column_id + 1]
        radius = jnp.sqrt(upper * upper + lower * lower)
        cosine = upper / radius
        sine_value = lower / radius
        column[column_id] = radius
        cosines.append(cosine)
        sines.append(sine_value)
        side_terms[column_id + 1] = -sine_value * side_terms[column_id]
        side_terms[column_id] = cosine * side_terms[column_id]
        triangle.append(column)
    weights = [None] * steps_count
    for column_id in reversed(range(steps_count)):
        running = side_terms[column_id]
        for later_col in range(column_id + 1, steps_count):
            running = running - triangle[later_col][column_id] * weights[later_col]
        weights[column_id] = running / triangle[column_id][column_id]
    return weights


def solution(mesh):
    placed = (
        P("sub", "coarse", None, None),
        P("sub", "coarse", None, None),
        P("sub", "coarse", None, None),
        P("sub", "coarse", None, None, None),
        P("sub", "coarse", None, None, None),
        P("sub", "coarse", None, None),
        P("coarse", None),
        P("sub", None),
        P("sub", None),
        P("sub", "coarse", None, None),
        P("sub", "coarse", None),
    )
    return jax.shard_map(
        on_device,
        mesh=mesh,
        in_specs=placed,
        out_specs=P("sub", "coarse", None, None),
        check_vma=False,
    )
```

time: 139 us -> 127 us (0.914)
  local copies, waits for them, and re-layouts: 27.2 us -> 4.41 us
  blocking collectives: 65.7 us -> 46.7 us
  starting transfers between devices: 15.2 us -> 27.5 us
  Pallas kernels: 29 us -> 40.4 us
  waiting for transfers between devices: 0.01 us -> 6.53 us
    unnamed x62 -> x12, local copies, waits for them, and re-layouts: 27.2 us -> 4.41 us
    all_to_all x5 -> x4, blocking collectives: 65.7 us -> 46.7 us  [on_device(): arrived = lax.all_to_all(slots, ('sub', 'coarse'), 0, 0)]
    pallas_call x15, Pallas kernels: 29 us -> 40.4 us  [call(): pl.pallas_call(kernel, out_shape=outs, in_specs=[pl.BlockSpec(memory_spac...]
    all_to_all x0 -> x1, starting transfers between devices: none -> 6.33 us  [on_device(): arrived = lax.all_to_all(slots, ('sub', 'coarse'), 0, 0)]
    ppermute x0 -> x3, starting transfers between devices: none -> 5.65 us  [on_device(): lax.ppermute(coarse_chunks[turn], 'coarse', [(i, (i + turn) % parts) for...]
    ppermute x0 -> x3, waiting for transfers between devices: none -> 5.48 us  [on_device(): lax.ppermute(coarse_chunks[turn], 'coarse', [(i, (i + turn) % parts) for...]
  transfers between devices with their start and end apart: 4 -> 8, of which waited for: 0 -> 5; matrix products, arithmetic and copies ran while one was open for 0% -> 0% of each run, Pallas kernels for 11% -> 17%
where the time goes in v3:
time: 127 us; the launch traced here: 126 us
  blocking collectives  46.7 us (37%)
  Pallas kernels  40.4 us (32%)
  starting transfers between devices  27.5 us (22%)
  waiting for transfers between devices  6.53 us (5%)
  local copies, waits for them, and re-layouts  4.41 us (3%)
    all_to_all x4, blocking collectives, on_device(): arrived = lax.all_to_all(slots, ('sub', 'coarse'), 0, 0)  46.7 us
    pallas_call x15, Pallas kernels, call(): pl.pallas_call(kernel, out_shape=outs, in_specs=[pl.BlockSpec(memory_spac...  40.4 us
    all_to_all x4, starting transfers between devices, on_device(): arrived = lax.all_to_all(outgoing, 'sub', 0, 0)  15.6 us
    all_to_all x1, starting transfers between devices, on_device(): arrived = lax.all_to_all(slots, ('sub', 'coarse'), 0, 0)  6.33 us
    ppermute x3, starting transfers between devices, on_device(): lax.ppermute(coarse_chunks[turn], 'coarse', [(i, (i + turn) % parts) for...  5.65 us
    ppermute x3, waiting for transfers between devices, on_device(): lax.ppermute(coarse_chunks[turn], 'coarse', [(i, (i + turn) % parts) for...  5.48 us
    unnamed x12, local copies, waits for them, and re-layouts  4.41 us
  transfers between devices with their start and end apart: 8, of which 5 were waited for; matrix products, arithmetic and copies ran while one was open for 0% of the time, Pallas kernels for 17%

profile of v3, /device:TPU:0, one launch (start us, length us, event | category | flops | bytes accessed | tf_op | source)
XLA Modules:
  0.0 125.7 jit_solution(14155924146110905579)
XLA Ops:
  0.0 2.5 %begin.1 = (f32[8,32,128]{2,1,0:T(8,128)}, bf16[32,256]{1,0:T(8,128)(2,1)S(1)}, f32[32,128]{1,0:T(8,128)S(1)}, f32[32,128]{1,0:T(8,128)S(1)}, bf16[128,128]{1,0:...) custom-call(s32[4,8]{1,0:T(4,128)} %bitcast.19, ...), custom_call_target="tpu_custom_call" | custom-call | tf_op jit(solution)/shard_map/begin/pallas_call | solution.py:110
  2.5 5.2 %all-to-all-start = ((f32[8,32,128]{2,1,0:T(8,128)}), f32[8,32,128]{2,1,0:T(8,128)S(1)}, u32[]{:S(2)}, u32[]{:S(2)}) async-start(f32[8,32,128]{2,1,0:T(8,128)} %get-tuple-element.57.stat_ref), calls=%async_computation | async-start | bytes 262144 | tf_op jit(solution)/shard_map/all_to_all | solution.py:711
  7.7 4.6 %solve0.1.solved_ref = f32[128,128]{1,0:T(8,128)S(1)} custom-call(f32[128,128]{1,0:T(8,128)S(1)} %get-tuple-element.58.vector_ref.refs_3_, f32[128,128,128]{2,1,0:T(8,128)} %bitcast.9), custom_call_target="tpu_custom_call" | custom-call | tf_op jit(solution)/shard_map/solve0/pallas_call | solution.py:110
  12.4 3.2 %prepare.1 = (bf16[16,256,256]{2,1,0:T(8,128)(2,1)S(1)}, bf16[4,128,256]{2,1,0:T(8,128)(2,1)S(1)}, bf16[128,128]{1,0:T(8,128)(2,1)S(1)}, bf16[128,128]{1,0:T(8,1...) custom-call(s32[4,8]{1,0:T(4,128)} %bitcast.20, f32[128,128,128]{2,1,0:T(8,128)} %bitcast.10, ...), custom_call_target="tpu_custom_call" | custom-call | tf_op jit(solution)/shard_map/prepare/pallas_call | solution.py:110
  15.5 2.6 %smooth0.1 = (f32[128,128]{1,0:T(8,128)S(1)}, f32[32,8,128]{2,1,0:T(8,128)}, f32[8,128]{1,0:T(8,128)S(1)}, f32[32,128]{1,0:T(8,128)S(1)}, f32[1,32,128]{2,1,0:T(8,128)S(1)}) custom-call(f32[8,32,128]{2,1,0:T(8,128)S(1)} %all-to-all-done.arrived_ref, f32[128,128]{1,0:T(8,128)S(1)} %solve0.1.solved_ref, ...), custom_call_target="tpu_custom_call" | custom-call | tf_op jit(solution)/shard_map/smooth0/pallas_call | solution.py:110
  18.8 6.3 %all-to-all-start.1 = ((f32[32,8,128]{2,1,0:T(8,128)}), f32[32,8,128]{2,1,0:T(8,128)S(1)}, u32[]{:S(2)}, u32[]{:S(2)}) async-start(f32[32,8,128]{2,1,0:T(8,128)} %get-tuple-element.67), calls=%async_computation.1 | async-start | bytes 262144 | tf_op jit(solution)/shard_map/all_to_all | solution.py:750
  25.1 1.8 %collective-permute-start = (f32[32,512]{1,0:T(8,128)S(1)}, f32[32,512]{1,0:T(8,128)S(1)}, u32[]{:S(2)}, u32[]{:S(2)}) collective-permute-start(f32[32,512]{1,0:T(8,128)S(1)} %get-tuple-element.79), channel_id=1, source_target_pairs={{0,1},{1,2},{2,3},{3,0},{4,5},{5,6},{6,7},{7,4},{8,9},{9,10},{10,1... | collective-permute-start | bytes 196616 | tf_op jit(solution)/shard_map/ppermute | solution.py:343
  26.9 2.4 %collective-permute-start.1 = (f32[32,512]{1,0:T(8,128)S(1)}, f32[32,512]{1,0:T(8,128)S(1)}, u32[]{:S(2)}, u32[]{:S(2)}) collective-permute-start(f32[32,512]{1,0:T(8,128)S(1)} %get-tuple-element.80), channel_id=1, source_target_pairs={{0,2},{1,3},{2,0},{3,1},{4,6},{5,7},{6,4},{7,5},{8,10},{9,11},{10,... | collective-permute-start | bytes 196616 | tf_op jit(solution)/shard_map/ppermute | solution.py:343
  30.7 3.0 %collective-permute-done.refs_19_ = f32[32,512]{1,0:T(8,128)S(1)} collective-permute-done((f32[32,512]{1,0:T(8,128)S(1)}, f32[32,512]{1,0:T(8,128)S(1)}, u32[]{:S(2)}, u32[]{:S(2)}) %collective-permute-start) | collective-permute-done | bytes 65568 | tf_op jit(solution)/shard_map/ppermute | solution.py:343
  33.8 2.4 %collective-permute-done.1.refs_20_ = f32[32,512]{1,0:T(8,128)S(1)} collective-permute-done((f32[32,512]{1,0:T(8,128)S(1)}, f32[32,512]{1,0:T(8,128)S(1)}, u32[]{:S(2)}, u32[]{:S(2)}) %collective-permute-start.1) | collective-permute-done | bytes 65568 | tf_op jit(solution)/shard_map/ppermute | solution.py:343
  38.6 3.6 %all-to-all-start.2 = ((f32[8,16,128]{2,1,0:T(8,128)}), f32[8,16,128]{2,1,0:T(8,128)S(1)}, u32[]{:S(2)}, u32[]{:S(2)}) async-start(f32[8,16,128]{2,1,0:T(8,128)} %copy-done), calls=%async_computation.2 | async-start | bytes 131072 | tf_op jit(solution)/shard_map/all_to_all | solution.py:711
  42.2 4.6 %solve1.1.solved_ref = f32[128,128]{1,0:T(8,128)S(1)} custom-call(f32[128,128]{1,0:T(8,128)S(1)} %get-tuple-element.83.vector_ref.refs_3_, f32[128,128,128]{2,1,0:T(8,128)} %bitcast.11), custom_call_target="tpu_custom_call" | custom-call | tf_op jit(solution)/shard_map/solve1/pallas_call | solution.py:110
  50.6 13.1 %all_to_all.45.refs_0_ = f32[32,8,128]{2,1,0:T(8,128)S(1)} all-to-all(f32[32,8,128]{2,1,0:T(8,128)S(1)} %get-tuple-element.85), channel_id=1, replica_groups=mesh['sub'=8,'coarse'=4] {'sub','coarse'}, dimensions={0} | all-to-all | bytes 262144 | tf_op jit(solution)/shard_map/all_to_all | solution.py:750
  63.7 2.4 %advance1.1 = (f32[128,128]{1,0:T(8,128)S(1)}, f32[8,16,128]{2,1,0:T(8,128)}, f32[128,128]{1,0:T(8,128)}, f32[512,128]{1,0:T(8,128)S(1)}) custom-call(f32[32,8,128]{2,1,0:T(8,128)S(1)} %all_to_all.45.refs_0_, f32[8,128]{1,0:T(8,128)S(1)} %get-tuple-element.86.refs_1_, f32[128,128]{1,0:T(8,128)S(1)} %get-tuple-element.87.refs_2_, ...), custom_call_target="tpu_custom_call", output_to_operand_aliasing={{3}: (23, {})} | custom-call | tf_op jit(solution)/shard_map/advance1/pallas_call | solution.py:110
  66.1 3.4 %all-to-all-start.4 = ((f32[8,16,128]{2,1,0:T(8,128)}), f32[8,16,128]{2,1,0:T(8,128)S(1)}, u32[]{:S(2)}, u32[]{:S(2)}) async-start(f32[8,16,128]{2,1,0:T(8,128)} %get-tuple-element.90.stat_ref), calls=%async_computation.4 | async-start | bytes 131072 | tf_op jit(solution)/shard_map/all_to_all | solution.py:711
  69.4 4.6 %solve2.1.solved_ref = f32[128,128]{1,0:T(8,128)S(1)} custom-call(f32[128,128]{1,0:T(8,128)S(1)} %get-tuple-element.91.vector_ref.refs_3_, f32[128,128,128]{2,1,0:T(8,128)} %bitcast.12), custom_call_target="tpu_custom_call" | custom-call | tf_op jit(solution)/shard_map/solve2/pallas_call | solution.py:110
  74.4 1.9 %smooth2.1 = (f32[128,128]{1,0:T(8,128)S(1)}, f32[32,8,128]{2,1,0:T(8,128)S(1)}, f32[8,128]{1,0:T(8,128)S(1)}, f32[512,128]{1,0:T(8,128)S(1)}) custom-call(f32[8,16,128]{2,1,0:T(8,128)S(1)} %all-to-all-done.4.arrived_ref, f32[128,128]{1,0:T(8,128)S(1)} %solve2.1.solved_ref, ...), custom_call_target="tpu_custom_call", output_to_operand_aliasing={{3}: (10, {})} | custom-call | tf_op jit(solution)/shard_map/smooth2/pallas_call | solution.py:110
  76.3 11.8 %all_to_all.46.refs_0_ = f32[32,8,128]{2,1,0:T(8,128)S(1)} all-to-all(f32[32,8,128]{2,1,0:T(8,128)S(1)} %get-tuple-element.93), channel_id=1, replica_groups=mesh['sub'=8,'coarse'=4] {'sub','coarse'}, dimensions={0} | all-to-all | bytes 262144 | tf_op jit(solution)/shard_map/all_to_all | solution.py:750
  88.0 2.3 %advance2.1 = (f32[128,128]{1,0:T(8,128)S(1)}, f32[8,16,128]{2,1,0:T(8,128)}, f32[128,128]{1,0:T(8,128)}, f32[512,128]{1,0:T(8,128)S(1)}) custom-call(f32[32,8,128]{2,1,0:T(8,128)S(1)} %all_to_all.46.refs_0_, f32[8,128]{1,0:T(8,128)S(1)} %get-tuple-element.94.refs_1_, f32[128,128]{1,0:T(8,128)S(1)} %get-tuple-element.95.refs_2_, ...), custom_call_target="tpu_custom_call", output_to_operand_aliasing={{3}: (24, {})} | custom-call | tf_op jit(solution)/shard_map/advance2/pallas_call | solution.py:110
  90.3 3.4 %all-to-all-start.6 = ((f32[8,16,128]{2,1,0:T(8,128)}), f32[8,16,128]{2,1,0:T(8,128)S(1)}, u32[]{:S(2)}, u32[]{:S(2)}) async-start(f32[8,16,128]{2,1,0:T(8,128)} %get-tuple-element.98.stat_ref), calls=%async_computation.6 | async-start | bytes 131072 | tf_op jit(solution)/shard_map/all_to_all | solution.py:711
  93.7 4.6 %solve3.1.solved_ref = f32[128,128]{1,0:T(8,128)S(1)} custom-call(f32[128,128]{1,0:T(8,128)S(1)} %get-tuple-element.99.vector_ref.refs_3_, f32[128,128,128]{2,1,0:T(8,128)} %bitcast.13), custom_call_target="tpu_custom_call" | custom-call | tf_op jit(solution)/shard_map/solve3/pallas_call | solution.py:110
  98.6 1.9 %smooth3.1 = (f32[128,128]{1,0:T(8,128)S(1)}, f32[32,8,128]{2,1,0:T(8,128)S(1)}, f32[8,128]{1,0:T(8,128)S(1)}, f32[512,128]{1,0:T(8,128)S(1)}) custom-call(f32[8,16,128]{2,1,0:T(8,128)S(1)} %all-to-all-done.6.arrived_ref, f32[128,128]{1,0:T(8,128)S(1)} %solve3.1.solved_ref, ...), custom_call_target="tpu_custom_call", output_to_operand_aliasing={{3}: (10, {})} | custom-call | tf_op jit(solution)/shard_map/smooth3/pallas_call | solution.py:110
  100.5 11.8 %all_to_all.47.refs_0_ = f32[32,8,128]{2,1,0:T(8,128)S(1)} all-to-all(f32[32,8,128]{2,1,0:T(8,128)S(1)} %get-tuple-element.101), channel_id=1, replica_groups=mesh['sub'=8,'coarse'=4] {'sub','coarse'}, dimensions={0} | all-to-all | bytes 262144 | tf_op jit(solution)/shard_map/all_to_all | solution.py:750
  114.0 10.1 %all_to_all.48.arrived_ref = f32[32,8,128]{2,1,0:T(8,128)S(1)} all-to-all(f32[32,8,128]{2,1,0:T(8,128)S(1)} %get-tuple-element.106), channel_id=1, replica_groups=mesh['sub'=8,'coarse'=4] {'sub','coarse'}, dimensions={0} | all-to-all | bytes 262144 | tf_op jit(solution)/shard_map/all_to_all | solution.py:795
  (23 shorter events, 12.1 us)
Async XLA Ops:
  2.5 13.0 %all-to-all-start = ((f32[8,32,128]{2,1,0:T(8,128)}), f32[8,32,128]{2,1,0:T(8,128)S(1)}, u32[]{:S(2)}, u32[]{:S(2)}) async-start(f32[8,32,128]{2,1,0:T(8,128)} %get-tuple-element.57.stat_ref), calls=%async_computation | async-start | bytes 262144 | tf_op jit(solution)/shard_map/all_to_all | solution.py:711
  18.1 0.6 copy-start.4
  18.8 17.5 %all-to-all-start.1 = ((f32[32,8,128]{2,1,0:T(8,128)}), f32[32,8,128]{2,1,0:T(8,128)S(1)}, u32[]{:S(2)}, u32[]{:S(2)}) async-start(f32[32,8,128]{2,1,0:T(8,128)} %get-tuple-element.67), calls=%async_computation.1 | async-start | bytes 262144 | tf_op jit(solution)/shard_map/all_to_all | solution.py:750
  25.1 8.7 %collective-permute-start = (f32[32,512]{1,0:T(8,128)S(1)}, f32[32,512]{1,0:T(8,128)S(1)}, u32[]{:S(2)}, u32[]{:S(2)}) collective-permute-start(f32[32,512]{1,0:T(8,128)S(1)} %get-tuple-element.79), channel_id=1, source_target_pairs={{0,1},{1,2},{2,3},{3,0},{4,5},{5,6},{6,7},{7,4},{8,9},{9,10},{10,1... | collective-permute-start | bytes 196616 | tf_op jit(solution)/shard_map/ppermute | solution.py:343
  26.9 9.3 %collective-permute-start.1 = (f32[32,512]{1,0:T(8,128)S(1)}, f32[32,512]{1,0:T(8,128)S(1)}, u32[]{:S(2)}, u32[]{:S(2)}) collective-permute-start(f32[32,512]{1,0:T(8,128)S(1)} %get-tuple-element.80), channel_id=1, source_target_pairs={{0,2},{1,3},{2,0},{3,1},{4,6},{5,7},{6,4},{7,5},{8,10},{9,11},{10,... | collective-permute-start | bytes 196616 | tf_op jit(solution)/shard_map/ppermute | solution.py:343
  29.3 6.9 %collective-permute-start.2 = (f32[32,512]{1,0:T(8,128)S(1)}, f32[32,512]{1,0:T(8,128)S(1)}, u32[]{:S(2)}, u32[]{:S(2)}) collective-permute-start(f32[32,512]{1,0:T(8,128)S(1)} %get-tuple-element.81), channel_id=1, source_target_pairs={{0,3},{1,0},{2,1},{3,2},{4,7},{5,4},{6,5},{7,6},{8,11},{9,8},{10,9... | collective-permute-start | bytes 196616 | tf_op jit(solution)/shard_map/ppermute | solution.py:343
  36.2 0.8 copy-start.5
  38.0 0.6 copy-start
  38.6 8.7 %all-to-all-start.2 = ((f32[8,16,128]{2,1,0:T(8,128)}), f32[8,16,128]{2,1,0:T(8,128)S(1)}, u32[]{:S(2)}, u32[]{:S(2)}) async-start(f32[8,16,128]{2,1,0:T(8,128)} %copy-done), calls=%async_computation.2 | async-start | bytes 131072 | tf_op jit(solution)/shard_map/all_to_all | solution.py:711
  47.3 0.6 copy-start.2
  47.9 0.8 copy-start.1
  48.7 0.8 copy-start.3
  66.1 8.3 %all-to-all-start.4 = ((f32[8,16,128]{2,1,0:T(8,128)}), f32[8,16,128]{2,1,0:T(8,128)S(1)}, u32[]{:S(2)}, u32[]{:S(2)}) async-start(f32[8,16,128]{2,1,0:T(8,128)} %get-tuple-element.90.stat_ref), calls=%async_computation.4 | async-start | bytes 131072 | tf_op jit(solution)/shard_map/all_to_all | solution.py:711
  90.3 8.3 %all-to-all-start.6 = ((f32[8,16,128]{2,1,0:T(8,128)}), f32[8,16,128]{2,1,0:T(8,128)S(1)}, u32[]{:S(2)}, u32[]{:S(2)}) async-start(f32[8,16,128]{2,1,0:T(8,128)} %get-tuple-element.98.stat_ref), calls=%async_computation.6 | async-start | bytes 131072 | tf_op jit(solution)/shard_map/all_to_all | solution.py:711

commit v4 on v3

--- a/solution.py
+++ b/solution.py
@@ -104,17 +104,14 @@
     return pltpu.VMEM(shape, dtype)
 
 
-def call(kernel, outs, *args, name, places="", out_places="", aliases=None, scratch=()):
+def call(kernel, outs, *args, name, places="", aliases=None, scratch=()):
     places = places + "v" * (len(args) - len(places))
     spaces = {"s": pltpu.SMEM, "h": pltpu.HBM, "v": pltpu.VMEM}
     return pl.pallas_call(
         kernel,
         out_shape=outs,
         in_specs=[pl.BlockSpec(memory_space=spaces[place]) for place in places],
-        out_specs=[
-            pl.BlockSpec(memory_space=pltpu.HBM if place == "h" else pltpu.VMEM)
-            for place in (out_places or "v" * len(outs))
-        ],
+        out_specs=[pl.BlockSpec(memory_space=pltpu.VMEM)] * len(outs),
         input_output_aliases=aliases or {},
         scratch_shapes=list(scratch),
         name=name,
@@ -164,7 +161,8 @@
     full = (block_count, unknowns)
 
     v_at = 0
-    m_at = v_at + (ITERS - 1) * block_count
+    z_at = v_at + (ITERS - 1) * block_count
+    m_at = z_at + ITERS * block_count
     head_at = m_at + (ITERS - 1) * margin_rows
     state_rows = head_at + ITERS * ROWS
     blocks = margin_blocks[0, 0]
@@ -194,11 +192,9 @@
         )
 
     def statistics_block(vector, basis_value, member_value, home, dots, rows, count):
-        lines = []
-        if count:
-            inner = jnp.sum(basis_value * vector, axis=1, keepdims=True)
-            line = column_sum(inner * member_value) * factor
-            lines = [home[chunk : chunk + 1] * line for chunk in range(count)]
+        inner = jnp.sum(basis_value * vector, axis=1, keepdims=True)
+        line = column_sum(inner * member_value) * factor
+        lines = [home[chunk : chunk + 1] * line for chunk in range(count)]
         lines += [column_sum(other * vector) for other in dots]
         if len(lines) < rows:
             lines.append(jnp.zeros((rows - len(lines), LANES), F32))
@@ -274,7 +270,7 @@
         selector_ref[...] = table
         route = route_ref[...]
         member = hot((numbers & (LANES - 1)) == iota((LANES, block_count), 0)).T
-        member_ref[...] = member.astype(BF16)
+        member_ref[...] = member
         home = hot((numbers >> lane_bits) == iota((coarse_rows, LANES), 0))
         home_ref[...] = home
         own_lane = coarse_lane(numbers)
@@ -320,7 +316,7 @@
             vmem((margin_rows, 2 * block_count), BF16),
             vmem((rounds * subs, LANES)),
             vmem((margin_rows, LANES)),
-            vmem((block_count, LANES), BF16),
+            vmem((block_count, LANES)),
             vmem((coarse_rows, LANES)),
             vmem(full),
             vmem(full),
@@ -344,52 +340,89 @@
             coarse_chunks[turn], "coarse", [(i, (i + turn) % parts) for i in range(parts)]
         )
 
-    def solve_group(group, vector_ref, inverse_ref, out_ref):
+    def put(target_value, values):
+        high, low = split(values)
+        pieces = [high, low]
+        if table_rows > 2 * margin_rows:
+            pieces.append(jnp.zeros((table_rows - 2 * margin_rows, unknowns), BF16))
+        return dot_plain(target_value, jnp.concatenate(pieces, axis=0))
+
+    def smooth_rest(arrived_ref, out, target, selector, route, part_ref, stat_ref, slot_ref, sum_ref):
+        slots = spread_rounds(pick(selector, out), route, subs, rounds)
+        statistic = stat_ref[0, widest : widest + stat_rows, :]
+        if stat_rows < slot_rows:
+            statistic = jnp.concatenate(
+                [statistic, jnp.zeros((slot_rows - stat_rows, LANES), F32)], axis=0
+            )
+        for sub_id in range(subs):
+            piece = slots[sub_id]
+            if widest < slot_rows:
+                piece = jnp.concatenate(
+                    [piece, jnp.zeros((slot_rows - widest, unknowns), F32)], axis=0
+                )
+            for part_id in range(parts):
+                slot_ref[sub_id * parts + part_id] = jnp.where(
+                    part_ref[part_id : part_id + 1, :] > 0.5, piece, statistic
+                )
+        total = arrived_ref[0, widest : widest + stat_rows, :]
+        for sub_id in range(1, subs):
+            total = total + arrived_ref[sub_id, widest : widest + stat_rows, :]
+        sum_ref[...] = total
+
+    def arrived_rows(arrived_ref, at, route):
+        return gather_rounds(
+            [arrived_ref[sub_id, at : at + widest, :] for sub_id in range(subs)], route, rounds
+        )
+
+    def block_rows(shifted_ref, group):
         rows = pl.ds(pl.multiple_of(group * ROWS, ROWS), ROWS)
-        values = vector_ref[rows, :]
-        lines = []
-        for offset in range(ROWS):
-            scaled = inverse_ref[group * ROWS + offset] * values[offset : offset + 1, :]
-            lines.append(jnp.sum(scaled, axis=1)[None, :])
-        out_ref[rows, :] = jnp.concatenate(lines, axis=0)
-
-    def solve(vector_ref, inverse_hbm, out_ref, inverse_ref, semaphores):
-        def group_copy(group):
-            rows = pl.ds(group * ROWS, ROWS)
-            return pltpu.make_async_copy(
-                inverse_hbm.at[rows], inverse_ref.at[rows], semaphores.at[group]
-            )
-
-        for group in range(block_count // ROWS):
-            group_copy(group).start()
-
-        def step(group, carry):
-            group_copy(group).wait()
-            solve_group(group, vector_ref, inverse_ref, out_ref)
-            return carry
-
-        lax.fori_loop(0, block_count // ROWS, step, 0)
-
-    def prepare(
-        blocks_ref,
+        return paired_rows(shifted_ref[rows, :])
+
+    def block_product(left, weight_of):
+        row = iota((ROWS, unknowns), 0)
+        total = jnp.zeros((ROWS, unknowns), F32)
+        for offset in range(ROWS // 2):
+            both = dot_plain(left, weight_of(offset))
+            both = both[:ROWS] + both[ROWS:]
+            total = jnp.where(row == 2 * offset, both[:, :unknowns], total)
+            total = jnp.where(row == 2 * offset + 1, both[:, unknowns:], total)
+        return total
+
+    def smooth_first(
+        arrived_ref,
+        vector_ref,
+        selector_ref,
+        route_ref,
+        live_ref,
+        member_of_ref,
+        stat_ref,
         inverse_hbm,
         coupling_hbm,
         diagonal_hbm,
         link_hbm,
-        selector_ref,
-        member_of_ref,
-        weight_ref,
-        pair_ref,
-        target_ref,
-        sub_member_ref,
-        part_ref,
-        diagonal_ref,
-        link_ref,
-        inverse_ref,
-        coupling_ref,
-        semaphores,
-        block_semaphores,
+        *refs,
     ):
+        chunk_refs = refs[:parts]
+        (
+            out_ref,
+            slot_ref,
+            sum_ref,
+            basis_rows_ref,
+            lane_rows_ref,
+            weight_ref,
+            pair_ref,
+            target_ref,
+            sub_member_ref,
+            part_ref,
+            diagonal_ref,
+            link_ref,
+            coarse_ref,
+            inverse_ref,
+            coupling_ref,
+            shifted_ref,
+            semaphores,
+            group_semaphores,
+        ) = refs[parts:]
         copies = [
             pltpu.make_async_copy(source, to, semaphores.at[position])
             for position, (source, to) in enumerate(
@@ -400,16 +433,18 @@
                 ]
             )
         ]
-        block_copies = [
-            pltpu.make_async_copy(
-                inverse_hbm.at[blocks_ref[at // widest, at % widest]],
-                inverse_ref.at[at],
-                block_semaphores.at[at],
-            )
-            for at in range(margin_rows)
-        ]
-        for copy in copies + block_copies:
+
+        def group_copy(group):
+            rows = pl.ds(group * ROWS, ROWS)
+            return pltpu.make_async_copy(
+                inverse_hbm.at[rows], inverse_ref.at[rows], group_semaphores.at[group]
+            )
+
+        for copy in copies:
             copy.start()
+        for group in range(block_count // ROWS):
+            group_copy(group).start()
+        route = route_ref[...]
         table = selector_ref[:, 0:block_count].astype(F32)
         pieces = [table, table]
         if table_rows > 2 * margin_rows:
@@ -423,133 +458,98 @@
         for chunk in range(sub_chunks):
             sub_member_ref[:, chunk * LANES : (chunk + 1) * LANES] = hot(
                 own_lane == iota((LANES, block_count), 0) + chunk * LANES
-            ).T.astype(BF16)
-        part_ref[...] = hot(
-            ((numbers >> own_bits) & (parts - 1)) == iota((ROWS, LANES), 0)
-        )
+            ).T
+        part_ref[...] = hot(((numbers >> own_bits) & (parts - 1)) == iota((ROWS, LANES), 0))
+        for turn, chunk_ref in enumerate(chunk_refs):
+            coarse_ref[turn * chunk_rows : (turn + 1) * chunk_rows, :] = chunk_ref[...]
+        at = widest + stat_rows
+        basis_rows_ref[...] = arrived_rows(arrived_ref, at, route)
+        for chunk in range(sub_chunks):
+            at = at + widest
+            lane_rows_ref[chunk] = arrived_rows(arrived_ref, at, route)
         copies[0].wait()
         for round_id in range(rounds):
             high, low = split(coupling_ref[round_id])
             pair_ref[round_id, :, 0:unknowns] = high
             pair_ref[round_id, :, unknowns : 2 * unknowns] = low
-        for at in range(margin_rows):
-            block_copies[at].wait()
-            high, low = split(inverse_ref[at])
-            rows = slice((at % 2) * unknowns, (at % 2 + 1) * unknowns)
-            weight_ref[at // 2, rows, 0:unknowns] = high
-            weight_ref[at // 2, rows, unknowns : 2 * unknowns] = low
+        mapped = couple(arrived_rows(arrived_ref, 0, route), pair_ref, live_ref[...])
+        shifted_ref[...] = vector_ref[...] + put(target_ref[...], mapped)
+
+        def step(group, carry):
+            group_copy(group).wait()
+            left = block_rows(shifted_ref, group)
+
+            def weight_of(offset):
+                pair = group * (ROWS // 2) + offset
+                highs = []
+                lows = []
+                for position in range(2):
+                    high, low = split(inverse_ref[pair * 2 + position].T)
+                    lanes = slice(position * unknowns, (position + 1) * unknowns)
+                    weight_ref[pair, 0:unknowns, lanes] = high
+                    weight_ref[pair, unknowns : 2 * unknowns, lanes] = low
+                    highs.append(high)
+                    lows.append(low)
+                return jnp.concatenate(
+                    [jnp.concatenate(highs, axis=1), jnp.concatenate(lows, axis=1)], axis=0
+                )
+
+            rows = pl.ds(pl.multiple_of(group * ROWS, ROWS), ROWS)
+            out_ref[rows, :] = block_product(left, weight_of)
+            return carry
+
+        lax.fori_loop(0, block_count // ROWS, step, 0, unroll=2)
         for copy in copies[1:]:
             copy.wait()
-
-    inverse_blocks = block_inverse[0, 0]
-    weights, pairs, target, sub_member, part_table, diagonal_local, link_local = call(
-        prepare,
-        [
-            vmem((margin_rows // 2, 2 * unknowns, 2 * unknowns), BF16),
-            vmem((rounds, unknowns, 2 * unknowns), BF16),
-            vmem((block_count, table_rows), BF16),
-            vmem((block_count, sub_aggregates), BF16),
-            vmem((ROWS, LANES)),
-            vmem(full),
-            vmem(full),
-        ],
-        blocks,
-        inverse_blocks,
-        coupling[0, 0],
-        diagonal[0, 0],
-        cell_link[0, 0],
-        selector,
-        member_of,
-        name="prepare",
-        places="shhhh",
-        scratch=[
-            vmem((margin_rows, unknowns, unknowns)),
-            vmem((rounds, unknowns, unknowns)),
-            pltpu.SemaphoreType.DMA((3,)),
-            pltpu.SemaphoreType.DMA((margin_rows,)),
-        ],
-    )
-
-    def put(target_value, values):
-        high, low = split(values)
-        pieces = [high, low]
-        if table_rows > 2 * margin_rows:
-            pieces.append(jnp.zeros((table_rows - 2 * margin_rows, unknowns), BF16))
-        return dot_plain(target_value, jnp.concatenate(pieces, axis=0))
-
-    def smooth(first):
-        def kernel(
+        smooth_rest(
             arrived_ref,
-            solved_ref,
-            weight_ref,
-            pair_ref,
-            target_ref,
-            selector_ref,
-            route_ref,
-            live_ref,
+            out_ref[...],
+            target_ref[...],
+            selector_ref[...],
+            route,
             part_ref,
             stat_ref,
-            *refs,
-        ):
-            if first:
-                out_ref, slot_ref, sum_ref, basis_rows_ref, lane_rows_ref = refs
-            else:
-                unused_in, out_ref, slot_ref, sum_ref, unused_out = refs
-            route = route_ref[...]
-            arrived = gather_rounds(
-                [arrived_ref[sub_id, 0:widest, :] for sub_id in range(subs)], route, rounds
-            )
-            mapped = couple(arrived, pair_ref, live_ref[...])
-            row = iota((widest, unknowns), 0)
-            pieces = []
-            for round_id in range(rounds):
-                left = paired_rows(mapped[round_id * widest : (round_id + 1) * widest])
-                total = jnp.zeros((widest, unknowns), F32)
-                for offset in range(widest // 2):
-                    both = dot_rows(left, weight_ref[round_id * (widest // 2) + offset])
-                    both = both[:widest] + both[widest:]
-                    total = jnp.where(row == 2 * offset, both[:, :unknowns], total)
-                    total = jnp.where(row == 2 * offset + 1, both[:, unknowns:], total)
-                pieces.append(total)
-            out = solved_ref[...] + put(target_ref[...], jnp.concatenate(pieces, axis=0))
-            out_ref[...] = out
-            slots = spread_rounds(pick(selector_ref[...], out), route, subs, rounds)
-            statistic = stat_ref[0, widest : widest + stat_rows, :]
-            if stat_rows < slot_rows:
-                statistic = jnp.concatenate(
-                    [statistic, jnp.zeros((slot_rows - stat_rows, LANES), F32)], axis=0
-                )
-            for sub_id in range(subs):
-                piece = slots[sub_id]
-                if widest < slot_rows:
-                    piece = jnp.concatenate(
-                        [piece, jnp.zeros((slot_rows - widest, unknowns), F32)], axis=0
-                    )
-                for part_id in range(parts):
-                    slot = sub_id * parts + part_id
-                    slot_ref[slot, 0:slot_rows, :] = jnp.where(
-                        part_ref[part_id : part_id + 1, :] > 0.5, piece, statistic
-                    )
-            total = arrived_ref[0, widest : widest + stat_rows, :]
-            for sub_id in range(1, subs):
-                total = total + arrived_ref[sub_id, widest : widest + stat_rows, :]
-            sum_ref[...] = total
-            if first:
-                at = widest + stat_rows
-                basis_rows_ref[...] = gather_rounds(
-                    [arrived_ref[sub_id, at : at + widest, :] for sub_id in range(subs)],
-                    route,
-                    rounds,
-                )
-                for chunk in range(sub_chunks):
-                    at = at + widest
-                    lane_rows_ref[chunk] = gather_rounds(
-                        [arrived_ref[sub_id, at : at + widest, :] for sub_id in range(subs)],
-                        route,
-                        rounds,
-                    )
-
-        return kernel
+            slot_ref,
+            sum_ref,
+        )
+
+    def smooth(
+        arrived_ref,
+        vector_ref,
+        weight_ref,
+        pair_ref,
+        target_ref,
+        selector_ref,
+        route_ref,
+        live_ref,
+        part_ref,
+        stat_ref,
+        out_ref,
+        slot_ref,
+        sum_ref,
+    ):
+        route = route_ref[...]
+        mapped = couple(arrived_rows(arrived_ref, 0, route), pair_ref, live_ref[...])
+        shifted = vector_ref[...] + put(target_ref[...], mapped)
+        pieces = []
+        for group in range(block_count // ROWS):
+            left = paired_rows(shifted[group * ROWS : (group + 1) * ROWS])
+            pieces.append(
+                block_product(left, lambda offset: weight_ref[group * (ROWS // 2) + offset])
+            )
+        out = jnp.concatenate(pieces, axis=0)
+        out_ref[...] = out
+        smooth_rest(
+            arrived_ref,
+            out,
+            target_ref[...],
+            selector_ref[...],
+            route,
+            part_ref,
+            stat_ref,
+            slot_ref,
+            sum_ref,
+        )
 
     def advance(step_id):
         first = step_id == 0
@@ -575,23 +575,17 @@
                 part_ref,
                 diagonal_ref,
                 link_ref,
-            ) = refs[:18]
-            coarse_refs = refs[18 : 18 + parts]
-            refs = refs[18 + parts :]
-            z_hbms = refs[:step_id]
-            if not first:
-                state_in = refs[step_id]
-                refs = refs[step_id + 1 :]
-            *outs, z_hbm, state_ref, z_ref, semaphores = refs
-            z_copies = [
-                pltpu.make_async_copy(source, z_ref.at[number], semaphores.at[number])
-                for number, source in enumerate(z_hbms)
-            ]
-            for copy in z_copies:
-                copy.start()
-
-            def held(at, number, rows):
-                return state_in[at + number * rows : at + (number + 1) * rows, :]
+                coarse_ref,
+            ) = refs[:19]
+            outs = list(refs[19:])
+            if first:
+                state_ref = outs.pop()
+            else:
+                state_in = outs.pop(0)
+                state_ref = outs.pop()
+
+                def held(at, number, rows):
+                    return state_in[at + number * rows : at + (number + 1) * rows, :]
 
             def keep(at, number, values):
                 rows = values.shape[0]
@@ -615,26 +609,22 @@
                 remaining = remaining - head * head
             length = jnp.sqrt(jnp.maximum(remaining, square * 1e-12))
             scale = 1.0 / length
-            gathered = []
-            for coarse_ref in coarse_refs:
-                piece = coarse_ref[:, 0:LANES] * total[0:1]
-                for chunk in range(1, coarse_rows):
-                    piece = piece + (
-                        coarse_ref[:, chunk * LANES : (chunk + 1) * LANES] * total[chunk : chunk + 1]
-                    )
-                gathered.append(piece)
-            gathered = jnp.concatenate(gathered, axis=0)
+            gathered = coarse_ref[:, 0:LANES] * total[0:1]
+            for chunk in range(1, coarse_rows):
+                gathered = gathered + (
+                    coarse_ref[:, chunk * LANES : (chunk + 1) * LANES] * total[chunk : chunk + 1]
+                )
             column = jnp.sum(gathered, axis=1, keepdims=True)
             same = iota((LANES, LANES), 0) == iota((LANES, LANES), 1)
             lines = [
                 column_sum(jnp.where(same, column[start : start + LANES], 0.0))
                 for start in range(0, sub_aggregates, LANES)
             ]
-            own_coarse = sub_member_ref[:, 0:LANES].astype(F32) * lines[0]
+            own_coarse = sub_member_ref[:, 0:LANES] * lines[0]
             row_coarse = lane_rows_ref[0] * lines[0]
             for chunk in range(1, sub_chunks):
                 own_coarse = own_coarse + (
-                    sub_member_ref[:, chunk * LANES : (chunk + 1) * LANES].astype(F32) * lines[chunk]
+                    sub_member_ref[:, chunk * LANES : (chunk + 1) * LANES] * lines[chunk]
                 )
                 row_coarse = row_coarse + lane_rows_ref[chunk] * lines[chunk]
             own_coarse = jnp.sum(own_coarse, axis=1, keepdims=True)
@@ -642,12 +632,8 @@
             basis_value = basis_ref[...]
             direction = smoothed_ref[...] + own_coarse * basis_value
             for number, head in enumerate(heads):
-                z_copies[number].wait()
-                direction = direction - head * z_ref[number]
+                direction = direction - head * held(z_at, number, block_count)
             direction = direction * scale
-            z_ref[step_id] = direction
-            z_copy = pltpu.make_async_copy(z_ref.at[step_id], z_hbm, semaphores.at[step_id])
-            z_copy.start()
             route = route_ref[...]
             rows = gather_rounds(pieces, route, rounds) + row_coarse * basis_rows_ref[...]
             for number, head in enumerate(heads):
@@ -665,7 +651,7 @@
             if last:
                 (slot_ref,) = outs
                 block = statistics_block(
-                    product, basis_value, None, home_ref[...], against, ROWS, 0
+                    product, basis_value, member_ref[...], home_ref[...], against, ROWS, 0
                 )
                 for slot in range(devices):
                     slot_ref[slot] = block
@@ -678,7 +664,7 @@
                 block = statistics_block(
                     product,
                     basis_value,
-                    member_ref[...].astype(F32),
+                    member_ref[...],
                     home_ref[...],
                     against,
                     stat_rows,
@@ -687,6 +673,7 @@
                 for sub_id in range(subs):
                     slot_ref[sub_id, 0:widest, :] = slots[sub_id]
                     slot_ref[sub_id, widest:, :] = block
+            keep(z_at, step_id, direction)
             keep(
                 head_at,
                 step_id,
@@ -697,62 +684,90 @@
                     (ROWS, LANES),
                 ),
             )
-            z_copy.wait()
 
         return kernel
 
     vector = start_vector
     state = None
-    z_list = []
     state_shape = vmem((state_rows, LANES))
     for step_id in range(ITERS):
         first = step_id == 0
         last = step_id == ITERS - 1
         arrived = lax.all_to_all(outgoing, "sub", 0, 0)
-        (solved,) = call(
-            solve,
-            [vmem(full)],
-            vector,
-            inverse_blocks,
-            name=f"solve{step_id}",
-            places="vh",
-            scratch=[
-                vmem((block_count, unknowns, unknowns)),
-                pltpu.SemaphoreType.DMA((block_count // ROWS,)),
-            ],
-        )
         outs = [vmem(full), vmem((devices, slot_rows, unknowns)), vmem((stat_rows, LANES))]
         if first:
-            outs += [vmem((margin_rows, unknowns)), vmem((sub_chunks, margin_rows, LANES))]
+            (
+                smoothed,
+                slots,
+                sums,
+                basis_rows,
+                lane_rows,
+                weights,
+                pairs,
+                target,
+                sub_member,
+                part_table,
+                diagonal_local,
+                link_local,
+                coarse_block,
+            ) = call(
+                smooth_first,
+                outs
+                + [
+                    vmem((margin_rows, unknowns)),
+                    vmem((sub_chunks, margin_rows, LANES)),
+                    vmem((block_count // 2, 2 * unknowns, 2 * unknowns), BF16),
+                    vmem((rounds, unknowns, 2 * unknowns), BF16),
+                    vmem((block_count, table_rows), BF16),
+                    vmem((block_count, sub_aggregates)),
+                    vmem((ROWS, LANES)),
+                    vmem(full),
+                    vmem(full),
+                    vmem((sub_aggregates, aggregates)),
+                ],
+                arrived,
+                vector,
+                selector,
+                route,
+                live,
+                member_of,
+                outgoing,
+                block_inverse[0, 0],
+                coupling[0, 0],
+                diagonal[0, 0],
+                cell_link[0, 0],
+                *coarse_chunks,
+                name="smooth0",
+                places="vvvvvvvhhhh",
+                scratch=[
+                    vmem((block_count, unknowns, unknowns)),
+                    vmem((rounds, unknowns, unknowns)),
+                    vmem(full),
+                    pltpu.SemaphoreType.DMA((3,)),
+                    pltpu.SemaphoreType.DMA((block_count // ROWS,)),
+                ],
+            )
         else:
-            outs += [state_shape]
-        made = call(
-            smooth(first),
-            outs,
-            arrived,
-            solved,
-            weights,
-            pairs,
-            target,
-            selector,
-            route,
-            live,
-            part_table,
-            outgoing,
-            *([] if first else [state]),
-            name=f"smooth{step_id}",
-            aliases={} if first else {10: 3},
-        )
-        if first:
-            smoothed, slots, sums, basis_rows, lane_rows = made
-        else:
-            smoothed, slots, sums, state = made
+            smoothed, slots, sums = call(
+                smooth,
+                outs,
+                arrived,
+                vector,
+                weights,
+                pairs,
+                target,
+                selector,
+                route,
+                live,
+                part_table,
+                outgoing,
+                name=f"smooth{step_id}",
+            )
         arrived = lax.all_to_all(slots, ("sub", "coarse"), 0, 0)
         if last:
-            outs = [vmem((devices, ROWS, LANES))]
+            outs = [vmem((devices, ROWS, LANES)), state_shape]
         else:
-            outs = [vmem(full), vmem((subs, widest + stat_rows, unknowns))]
-        outs += [pltpu.HBM(full, F32), state_shape]
+            outs = [vmem(full), vmem((subs, widest + stat_rows, unknowns)), state_shape]
         made = call(
             advance(step_id),
             outs,
@@ -774,35 +789,18 @@
             part_table,
             diagonal_local,
             link_local,
-            *coarse_chunks,
-            *z_list,
+            coarse_block,
             *([] if first else [state]),
             name=f"advance{step_id}",
-            places="v" * (18 + parts) + "h" * step_id,
-            out_places="v" * (len(outs) - 2) + "hv",
-            aliases={} if first else {18 + parts + step_id: len(outs) - 1},
-            scratch=[
-                vmem((step_id + 1, block_count, unknowns)),
-                pltpu.SemaphoreType.DMA((step_id + 1,)),
-            ],
+            aliases={} if first else {19: len(outs) - 1},
         )
-        *made, z_new, state = made
-        z_list.append(z_new)
         if last:
-            (slots,) = made
+            slots, state = made
         else:
-            vector, outgoing = made
+            vector, outgoing, state = made
     arrived = lax.all_to_all(slots, ("sub", "coarse"), 0, 0)
 
-    def finish(arrived_ref, state_ref, *refs):
-        z_hbms = refs[:ITERS]
-        out_ref, z_ref, semaphores = refs[ITERS:]
-        z_copies = [
-            pltpu.make_async_copy(source, z_ref.at[number], semaphores.at[number])
-            for number, source in enumerate(z_hbms)
-        ]
-        for copy in z_copies:
-            copy.start()
+    def finish(arrived_ref, state_ref, out_ref):
         total = arrived_ref[0]
         for slot in range(1, devices):
             total = total + arrived_ref[slot]
@@ -820,23 +818,13 @@
             columns.append([state_ref[at + i : at + i + 1, 0:1] for i in range(column_id + 1)])
         columns.append(heads + [length])
         weights_found = givens_solve(columns, beta)
-        result = None
-        for position in range(ITERS):
-            z_copies[position].wait()
-            term = weights_found[position] * z_ref[position]
-            result = term if result is None else result + term
+        result = weights_found[0] * state_ref[z_at : z_at + block_count, :]
+        for position in range(1, ITERS):
+            at = z_at + position * block_count
+            result = result + weights_found[position] * state_ref[at : at + block_count, :]
         out_ref[...] = result
 
-    (answer,) = call(
-        finish,
-        [jax.ShapeDtypeStruct(full, F32)],
-        arrived,
-        state,
-        *z_list,
-        name="finish",
-        places="vv" + "h" * ITERS,
-        scratch=[vmem((ITERS,) + full), pltpu.SemaphoreType.DMA((ITERS,))],
-    )
+    (answer,) = call(finish, [jax.ShapeDtypeStruct(full, F32)], arrived, state, name="finish")
     return answer.reshape(right_side.shape)
 
 

time: 127 us -> 112 us (0.88)
  blocking collectives: 46.7 us -> 76 us
  Pallas kernels: 40.4 us -> 20.9 us
  starting transfers between devices: 27.5 us -> 10.7 us
  local copies, waits for them, and re-layouts: 4.41 us -> 0 us
  waiting for transfers between devices: 6.53 us -> 4.01 us
    all_to_all x0 -> x3, blocking collectives: none -> 22.2 us  [on_device(): arrived = lax.all_to_all(outgoing, 'sub', 0, 0)]
    pallas_call x15 -> x10, Pallas kernels: 40.4 us -> 20.9 us  [call(): pl.pallas_call(kernel, out_shape=outs, in_specs=[pl.BlockSpec(memory_spac...]
    all_to_all x4 -> x1, starting transfers between devices: 15.6 us -> 5.18 us  [on_device(): arrived = lax.all_to_all(outgoing, 'sub', 0, 0)]
    all_to_all x4 -> x5, blocking collectives: 46.7 us -> 53.8 us  [on_device(): arrived = lax.all_to_all(slots, ('sub', 'coarse'), 0, 0)]
    all_to_all x1 -> x0, starting transfers between devices: 6.33 us -> none  [on_device(): arrived = lax.all_to_all(slots, ('sub', 'coarse'), 0, 0)]
    unnamed x12 -> x0, local copies, waits for them, and re-layouts: 4.41 us -> none
    ppermute x3, waiting for transfers between devices: 5.48 us -> 4.01 us  [on_device(): lax.ppermute(coarse_chunks[turn], 'coarse', [(i, (i + turn) % parts) for...]
  transfers between devices with their start and end apart: 8 -> 4, of which waited for: 5 -> 3; matrix products, arithmetic and copies ran while one was open for 0% -> 0% of each run, Pallas kernels for 17% -> 0%
where the time goes in v4:
time: 112 us
  blocking collectives  76 us (68%)
  Pallas kernels  20.9 us (19%)
  starting transfers between devices  10.7 us (10%)
  waiting for transfers between devices  4.01 us (4%)
    all_to_all x5, blocking collectives, on_device(): arrived = lax.all_to_all(slots, ('sub', 'coarse'), 0, 0)  53.8 us
    all_to_all x3, blocking collectives, on_device(): arrived = lax.all_to_all(outgoing, 'sub', 0, 0)  22.2 us
    pallas_call x10, Pallas kernels, call(): pl.pallas_call(kernel, out_shape=outs, in_specs=[pl.BlockSpec(memory_spac...  20.9 us
    ppermute x3, starting transfers between devices, on_device(): lax.ppermute(coarse_chunks[turn], 'coarse', [(i, (i + turn) % parts) for...  5.51 us
    all_to_all x1, starting transfers between devices, on_device(): arrived = lax.all_to_all(outgoing, 'sub', 0, 0)  5.18 us
    ppermute x3, waiting for transfers between devices, on_device(): lax.ppermute(coarse_chunks[turn], 'coarse', [(i, (i + turn) % parts) for...  4.01 us
  transfers between devices with their start and end apart: 4, of which 3 were waited for; matrix products, arithmetic and copies ran while one was open for 0% of the time, Pallas kernels for 0%

profile of v4, /device:TPU:0, one launch (start us, length us, event | category | flops | bytes accessed | tf_op | source)
XLA Modules:
  0.0 111.7 jit_solution(1492209867515252492)
XLA Ops:
  0.0 2.5 %begin.1 = (f32[8,32,128]{2,1,0:T(8,128)}, bf16[32,256]{1,0:T(8,128)(2,1)S(1)}, f32[32,128]{1,0:T(8,128)S(1)}, f32[32,128]{1,0:T(8,128)S(1)}, f32[128,128]{1,0:T...) custom-call(s32[4,8]{1,0:T(4,128)} %bitcast.15, ...), custom_call_target="tpu_custom_call" | custom-call | tf_op jit(solution)/shard_map/begin/pallas_call | solution.py:110
  2.5 5.2 %all-to-all-start = ((f32[8,32,128]{2,1,0:T(8,128)}), f32[8,32,128]{2,1,0:T(8,128)S(1)}, u32[]{:S(2)}, u32[]{:S(2)}) async-start(f32[8,32,128]{2,1,0:T(8,128)} %get-tuple-element.51.stat_ref), calls=%async_computation | async-start | bytes 262144 | tf_op jit(solution)/shard_map/all_to_all | solution.py:696
  7.7 1.6 %collective-permute-start = (f32[32,512]{1,0:T(8,128)S(1)}, f32[32,512]{1,0:T(8,128)S(1)}, u32[]{:S(2)}, u32[]{:S(2)}) collective-permute-start(f32[32,512]{1,0:T(8,128)S(1)} %get-tuple-element.58), channel_id=1, source_target_pairs={{0,1},{1,2},{2,3},{3,0},{4,5},{5,6},{6,7},{7,4},{8,9},{9,10},{10,1... | collective-permute-start | bytes 196616 | tf_op jit(solution)/shard_map/ppermute | solution.py:339
  9.3 2.6 %collective-permute-start.1 = (f32[32,512]{1,0:T(8,128)S(1)}, f32[32,512]{1,0:T(8,128)S(1)}, u32[]{:S(2)}, u32[]{:S(2)}) collective-permute-start(f32[32,512]{1,0:T(8,128)S(1)} %get-tuple-element.59), channel_id=1, source_target_pairs={{0,2},{1,3},{2,0},{3,1},{4,6},{5,7},{6,4},{7,5},{8,10},{9,11},{10,... | collective-permute-start | bytes 196616 | tf_op jit(solution)/shard_map/ppermute | solution.py:339
  11.9 1.3 %collective-permute-start.2 = (f32[32,512]{1,0:T(8,128)S(1)}, f32[32,512]{1,0:T(8,128)S(1)}, u32[]{:S(2)}, u32[]{:S(2)}) collective-permute-start(f32[32,512]{1,0:T(8,128)S(1)} %get-tuple-element.60), channel_id=1, source_target_pairs={{0,3},{1,0},{2,1},{3,2},{4,7},{5,4},{6,5},{7,6},{8,11},{9,8},{10,9... | collective-permute-start | bytes 196616 | tf_op jit(solution)/shard_map/ppermute | solution.py:339
  13.2 1.0 collective-permute-done.refs_1_
  14.2 2.8 %collective-permute-done.1.refs_2_ = f32[32,512]{1,0:T(8,128)S(1)} collective-permute-done((f32[32,512]{1,0:T(8,128)S(1)}, f32[32,512]{1,0:T(8,128)S(1)}, u32[]{:S(2)}, u32[]{:S(2)}) %collective-permute-start.1) | collective-permute-done | bytes 65568 | tf_op jit(solution)/shard_map/ppermute | solution.py:339
  17.2 10.2 %smooth0.1 = (f32[128,128]{1,0:T(8,128)S(1)}, f32[32,8,128]{2,1,0:T(8,128)S(1)}, f32[8,128]{1,0:T(8,128)S(1)}, f32[32,128]{1,0:T(8,128)S(1)}, f32[1,32,128]{2,1,...) custom-call(f32[8,32,128]{2,1,0:T(8,128)S(1)} %all-to-all-done.arriv, ...), custom_call_target="tpu_custom_call" | custom-call | tf_op jit(solution)/shard_map/smooth0/pallas_call | solution.py:110
  27.4 13.4 %all_to_all.45.refs_0_ = f32[32,8,128]{2,1,0:T(8,128)S(1)} all-to-all(f32[32,8,128]{2,1,0:T(8,128)S(1)} %get-tuple-element.61), channel_id=1, replica_groups=mesh['sub'=8,'coarse'=4] {'sub','coarse'}, dimensions={0} | all-to-all | bytes 262144 | tf_op jit(solution)/shard_map/all_to_all | solution.py:766
  40.8 0.7 advance0.1
  41.5 7.4 %all_to_all.46.arrived_ref = f32[8,16,128]{2,1,0:T(8,128)S(1)} all-to-all(f32[8,16,128]{2,1,0:T(8,128)S(1)} %get-tuple-element.76.stat_ref), channel_id=1, replica_groups=mesh['sub'=8,'coarse'=4] {'sub'}, dimensions={0} | all-to-all | bytes 131072 | tf_op jit(solution)/shard_map/all_to_all | solution.py:696
  48.9 1.6 %smooth1.1 = (f32[128,128]{1,0:T(8,128)S(1)}, f32[32,8,128]{2,1,0:T(8,128)S(1)}, f32[8,128]{1,0:T(8,128)S(1)}) custom-call(f32[8,16,128]{2,1,0:T(8,128)S(1)} %all_to_all.46.arrived_ref, f32[128,128]{1,0:T(8,128)S(1)} %get-tuple-element.77.vector_ref.refs_3_, bf16[64,256,256]{2,1,0:T(8,128)(2,1)S(1)} %get-tuple-element.78.weight_ref, ...), custom_call_target="tpu_custom_call" | custom-call | tf_op jit(solution)/shard_map/smooth1/pallas_call | solution.py:110
  50.5 10.1 %all_to_all.47.refs_0_ = f32[32,8,128]{2,1,0:T(8,128)S(1)} all-to-all(f32[32,8,128]{2,1,0:T(8,128)S(1)} %get-tuple-element.79), channel_id=1, replica_groups=mesh['sub'=8,'coarse'=4] {'sub','coarse'}, dimensions={0} | all-to-all | bytes 262144 | tf_op jit(solution)/shard_map/all_to_all | solution.py:766
  60.6 0.7 advance1.1
  61.3 7.4 %all_to_all.48.arrived_ref = f32[8,16,128]{2,1,0:T(8,128)S(1)} all-to-all(f32[8,16,128]{2,1,0:T(8,128)S(1)} %get-tuple-element.83.stat_ref), channel_id=1, replica_groups=mesh['sub'=8,'coarse'=4] {'sub'}, dimensions={0} | all-to-all | bytes 131072 | tf_op jit(solution)/shard_map/all_to_all | solution.py:696
  68.7 1.6 %smooth2.1 = (f32[128,128]{1,0:T(8,128)S(1)}, f32[32,8,128]{2,1,0:T(8,128)S(1)}, f32[8,128]{1,0:T(8,128)S(1)}) custom-call(f32[8,16,128]{2,1,0:T(8,128)S(1)} %all_to_all.48.arrived_ref, f32[128,128]{1,0:T(8,128)S(1)} %get-tuple-element.84.vector_ref.refs_3_, bf16[64,256,256]{2,1,0:T(8,128)(2,1)S(1)} %get-tuple-element.78.weight_ref, ...), custom_call_target="tpu_custom_call" | custom-call | tf_op jit(solution)/shard_map/smooth2/pallas_call | solution.py:110
  70.3 10.1 %all_to_all.49.refs_0_ = f32[32,8,128]{2,1,0:T(8,128)S(1)} all-to-all(f32[32,8,128]{2,1,0:T(8,128)S(1)} %get-tuple-element.85), channel_id=1, replica_groups=mesh['sub'=8,'coarse'=4] {'sub','coarse'}, dimensions={0} | all-to-all | bytes 262144 | tf_op jit(solution)/shard_map/all_to_all | solution.py:766
  80.4 0.7 advance2.1
  81.1 7.4 %all_to_all.50.arrived_ref = f32[8,16,128]{2,1,0:T(8,128)S(1)} all-to-all(f32[8,16,128]{2,1,0:T(8,128)S(1)} %get-tuple-element.89.stat_ref), channel_id=1, replica_groups=mesh['sub'=8,'coarse'=4] {'sub'}, dimensions={0} | all-to-all | bytes 131072 | tf_op jit(solution)/shard_map/all_to_all | solution.py:696
  88.5 1.6 %smooth3.1 = (f32[128,128]{1,0:T(8,128)S(1)}, f32[32,8,128]{2,1,0:T(8,128)S(1)}, f32[8,128]{1,0:T(8,128)S(1)}) custom-call(f32[8,16,128]{2,1,0:T(8,128)S(1)} %all_to_all.50.arrived_ref, f32[128,128]{1,0:T(8,128)S(1)} %get-tuple-element.90.vector_ref.refs_3_, bf16[64,256,256]{2,1,0:T(8,128)(2,1)S(1)} %get-tuple-element.78.weight_ref, ...), custom_call_target="tpu_custom_call" | custom-call | tf_op jit(solution)/shard_map/smooth3/pallas_call | solution.py:110
  90.1 10.1 %all_to_all.51.refs_0_ = f32[32,8,128]{2,1,0:T(8,128)S(1)} all-to-all(f32[32,8,128]{2,1,0:T(8,128)S(1)} %get-tuple-element.91), channel_id=1, replica_groups=mesh['sub'=8,'coarse'=4] {'sub','coarse'}, dimensions={0} | all-to-all | bytes 262144 | tf_op jit(solution)/shard_map/all_to_all | solution.py:766
  100.2 0.6 advance3.1
  100.8 10.1 %all_to_all.52.arrived_ref = f32[32,8,128]{2,1,0:T(8,128)S(1)} all-to-all(f32[32,8,128]{2,1,0:T(8,128)S(1)} %get-tuple-element.95), channel_id=1, replica_groups=mesh['sub'=8,'coarse'=4] {'sub','coarse'}, dimensions={0} | all-to-all | bytes 262144 | tf_op jit(solution)/shard_map/all_to_all | solution.py:801
  110.9 0.8 finish.1
  (2 shorter events, 0.2 us)
Async XLA Ops:
  2.5 14.7 %all-to-all-start = ((f32[8,32,128]{2,1,0:T(8,128)}), f32[8,32,128]{2,1,0:T(8,128)S(1)}, u32[]{:S(2)}, u32[]{:S(2)}) async-start(f32[8,32,128]{2,1,0:T(8,128)} %get-tuple-element.51.stat_ref), calls=%async_computation | async-start | bytes 262144 | tf_op jit(solution)/shard_map/all_to_all | solution.py:696
  7.7 6.5 %collective-permute-start = (f32[32,512]{1,0:T(8,128)S(1)}, f32[32,512]{1,0:T(8,128)S(1)}, u32[]{:S(2)}, u32[]{:S(2)}) collective-permute-start(f32[32,512]{1,0:T(8,128)S(1)} %get-tuple-element.58), channel_id=1, source_target_pairs={{0,1},{1,2},{2,3},{3,0},{4,5},{5,6},{6,7},{7,4},{8,9},{9,10},{10,1... | collective-permute-start | bytes 196616 | tf_op jit(solution)/shard_map/ppermute | solution.py:339
  9.3 7.7 %collective-permute-start.1 = (f32[32,512]{1,0:T(8,128)S(1)}, f32[32,512]{1,0:T(8,128)S(1)}, u32[]{:S(2)}, u32[]{:S(2)}) collective-permute-start(f32[32,512]{1,0:T(8,128)S(1)} %get-tuple-element.59), channel_id=1, source_target_pairs={{0,2},{1,3},{2,0},{3,1},{4,6},{5,7},{6,4},{7,5},{8,10},{9,11},{10,... | collective-permute-start | bytes 196616 | tf_op jit(solution)/shard_map/ppermute | solution.py:339
  11.9 5.4 %collective-permute-start.2 = (f32[32,512]{1,0:T(8,128)S(1)}, f32[32,512]{1,0:T(8,128)S(1)}, u32[]{:S(2)}, u32[]{:S(2)}) collective-permute-start(f32[32,512]{1,0:T(8,128)S(1)} %get-tuple-element.60), channel_id=1, source_target_pairs={{0,3},{1,0},{2,1},{3,2},{4,7},{5,4},{6,5},{7,6},{8,11},{9,8},{10,9... | collective-permute-start | bytes 196616 | tf_op jit(solution)/shard_map/ppermute | solution.py:339

commit v5 on v4

--- a/solution.py
+++ b/solution.py
@@ -11,6 +11,7 @@
 ITERS = 4
 LANES = 128
 ROWS = 8
+INVERSE_PARTS = 4
 BF16 = jnp.bfloat16
 F32 = jnp.float32
 
@@ -402,7 +403,6 @@
         link_hbm,
         *refs,
     ):
-        chunk_refs = refs[:parts]
         (
             out_ref,
             slot_ref,
@@ -416,13 +416,12 @@
             part_ref,
             diagonal_ref,
             link_ref,
-            coarse_ref,
             inverse_ref,
             coupling_ref,
             shifted_ref,
             semaphores,
-            group_semaphores,
-        ) = refs[parts:]
+            part_semaphores,
+        ) = refs
         copies = [
             pltpu.make_async_copy(source, to, semaphores.at[position])
             for position, (source, to) in enumerate(
@@ -434,16 +433,17 @@
             )
         ]
 
-        def group_copy(group):
-            rows = pl.ds(group * ROWS, ROWS)
-            return pltpu.make_async_copy(
-                inverse_hbm.at[rows], inverse_ref.at[rows], group_semaphores.at[group]
-            )
-
-        for copy in copies:
+        span = block_count // INVERSE_PARTS
+        part_copies = [
+            pltpu.make_async_copy(
+                inverse_hbm.at[pl.ds(number * span, span)],
+                inverse_ref.at[pl.ds(number * span, span)],
+                part_semaphores.at[number],
+            )
+            for number in range(INVERSE_PARTS)
+        ]
+        for copy in copies + part_copies:
             copy.start()
-        for group in range(block_count // ROWS):
-            group_copy(group).start()
         route = route_ref[...]
         table = selector_ref[:, 0:block_count].astype(F32)
         pieces = [table, table]
@@ -460,8 +460,6 @@
                 own_lane == iota((LANES, block_count), 0) + chunk * LANES
             ).T
         part_ref[...] = hot(((numbers >> own_bits) & (parts - 1)) == iota((ROWS, LANES), 0))
-        for turn, chunk_ref in enumerate(chunk_refs):
-            coarse_ref[turn * chunk_rows : (turn + 1) * chunk_rows, :] = chunk_ref[...]
         at = widest + stat_rows
         basis_rows_ref[...] = arrived_rows(arrived_ref, at, route)
         for chunk in range(sub_chunks):
@@ -476,7 +474,6 @@
         shifted_ref[...] = vector_ref[...] + put(target_ref[...], mapped)
 
         def step(group, carry):
-            group_copy(group).wait()
             left = block_rows(shifted_ref, group)
 
             def weight_of(offset):
@@ -498,7 +495,10 @@
             out_ref[rows, :] = block_product(left, weight_of)
             return carry
 
-        lax.fori_loop(0, block_count // ROWS, step, 0, unroll=2)
+        groups = span // ROWS
+        for number in range(INVERSE_PARTS):
+            part_copies[number].wait()
+            lax.fori_loop(number * groups, (number + 1) * groups, step, 0, unroll=2)
         for copy in copies[1:]:
             copy.wait()
         smooth_rest(
@@ -575,9 +575,9 @@
                 part_ref,
                 diagonal_ref,
                 link_ref,
-                coarse_ref,
-            ) = refs[:19]
-            outs = list(refs[19:])
+            ) = refs[:18]
+            coarse_refs = refs[18 : 18 + parts]
+            outs = list(refs[18 + parts :])
             if first:
                 state_ref = outs.pop()
             else:
@@ -609,11 +609,15 @@
                 remaining = remaining - head * head
             length = jnp.sqrt(jnp.maximum(remaining, square * 1e-12))
             scale = 1.0 / length
-            gathered = coarse_ref[:, 0:LANES] * total[0:1]
-            for chunk in range(1, coarse_rows):
-                gathered = gathered + (
-                    coarse_ref[:, chunk * LANES : (chunk + 1) * LANES] * total[chunk : chunk + 1]
-                )
+            gathered = []
+            for coarse_ref in coarse_refs:
+                piece = coarse_ref[:, 0:LANES] * total[0:1]
+                for chunk in range(1, coarse_rows):
+                    piece = piece + (
+                        coarse_ref[:, chunk * LANES : (chunk + 1) * LANES] * total[chunk : chunk + 1]
+                    )
+                gathered.append(piece)
+            gathered = jnp.concatenate(gathered, axis=0)
             column = jnp.sum(gathered, axis=1, keepdims=True)
             same = iota((LANES, LANES), 0) == iota((LANES, LANES), 1)
             lines = [
@@ -709,7 +713,6 @@
                 part_table,
                 diagonal_local,
                 link_local,
-                coarse_block,
             ) = call(
                 smooth_first,
                 outs
@@ -723,7 +726,6 @@
                     vmem((ROWS, LANES)),
                     vmem(full),
                     vmem(full),
-                    vmem((sub_aggregates, aggregates)),
                 ],
                 arrived,
                 vector,
@@ -736,7 +738,6 @@
                 coupling[0, 0],
                 diagonal[0, 0],
                 cell_link[0, 0],
-                *coarse_chunks,
                 name="smooth0",
                 places="vvvvvvvhhhh",
                 scratch=[
@@ -744,9 +745,10 @@
                     vmem((rounds, unknowns, unknowns)),
                     vmem(full),
                     pltpu.SemaphoreType.DMA((3,)),
-                    pltpu.SemaphoreType.DMA((block_count // ROWS,)),
+                    pltpu.SemaphoreType.DMA((INVERSE_PARTS,)),
                 ],
             )
+            slots, *coarse_chunks = lax.optimization_barrier((slots, *coarse_chunks))
         else:
             smoothed, slots, sums = call(
                 smooth,
@@ -789,10 +791,10 @@
             part_table,
             diagonal_local,
             link_local,
-            coarse_block,
+            *coarse_chunks,
             *([] if first else [state]),
             name=f"advance{step_id}",
-            aliases={} if first else {19: len(outs) - 1},
+            aliases={} if first else {18 + parts: len(outs) - 1},
         )
         if last:
             slots, state = made

time: 112 us -> 104 us (0.929)
  waiting for transfers between devices: 4.01 us -> 0.02 us
  Pallas kernels: 20.9 us -> 17.5 us
  blocking collectives: 76 us -> 74.8 us
    ppermute x3, waiting for transfers between devices: 4.01 us -> 0.01 us  [on_device(): lax.ppermute(coarse_chunks[turn], 'coarse', [(i, (i + turn) % parts) for...]
    pallas_call x10, Pallas kernels: 20.9 us -> 17.5 us  [call(): pl.pallas_call(kernel, out_shape=outs, in_specs=[pl.BlockSpec(memory_spac...]
    all_to_all x5, blocking collectives: 53.8 us -> 52.6 us  [on_device(): arrived = lax.all_to_all(slots, ('sub', 'coarse'), 0, 0)]
  transfers between devices with their start and end apart: 4 -> 4, of which waited for: 3 -> 0; matrix products, arithmetic and copies ran while one was open for 0% -> 0% of each run, Pallas kernels for 0% -> 7%
where the time goes in v5:
time: 104 us; the launch traced here: 103 us
  blocking collectives  74.8 us (72%)
  Pallas kernels  17.5 us (17%)
  starting transfers between devices  10.7 us (10%)
    all_to_all x5, blocking collectives, on_device(): arrived = lax.all_to_all(slots, ('sub', 'coarse'), 0, 0)  52.6 us
    all_to_all x3, blocking collectives, on_device(): arrived = lax.all_to_all(outgoing, 'sub', 0, 0)  22.2 us
    pallas_call x10, Pallas kernels, call(): pl.pallas_call(kernel, out_shape=outs, in_specs=[pl.BlockSpec(memory_spac...  17.5 us
    ppermute x3, starting transfers between devices, on_device(): lax.ppermute(coarse_chunks[turn], 'coarse', [(i, (i + turn) % parts) for...  5.51 us
    all_to_all x1, starting transfers between devices, on_device(): arrived = lax.all_to_all(outgoing, 'sub', 0, 0)  5.18 us
  transfers between devices with their start and end apart: 4, of which 0 were waited for; matrix products, arithmetic and copies ran while one was open for 0% of the time, Pallas kernels for 7%

profile of v5, /device:TPU:0, one launch (start us, length us, event | category | flops | bytes accessed | tf_op | source)
XLA Modules:
  0.0 103.1 jit_solution(7839301042571657221)
XLA Ops:
  0.0 2.5 %begin.1 = (f32[8,32,128]{2,1,0:T(8,128)}, bf16[32,256]{1,0:T(8,128)(2,1)S(1)}, f32[32,128]{1,0:T(8,128)S(1)}, f32[32,128]{1,0:T(8,128)S(1)}, f32[128,128]{1,0:T...) custom-call(s32[4,8]{1,0:T(4,128)} %bitcast.15, ...), custom_call_target="tpu_custom_call" | custom-call | tf_op jit(solution)/shard_map/begin/pallas_call | solution.py:111
  2.5 5.2 %all-to-all-start = ((f32[8,32,128]{2,1,0:T(8,128)}), f32[8,32,128]{2,1,0:T(8,128)S(1)}, u32[]{:S(2)}, u32[]{:S(2)}) async-start(f32[8,32,128]{2,1,0:T(8,128)} %get-tuple-element.55.stat_ref), calls=%async_computation | async-start | bytes 262144 | tf_op jit(solution)/shard_map/all_to_all | solution.py:700
  7.7 1.6 %collective-permute-start = (f32[32,512]{1,0:T(8,128)S(1)}, f32[32,512]{1,0:T(8,128)S(1)}, u32[]{:S(2)}, u32[]{:S(2)}) collective-permute-start(f32[32,512]{1,0:T(8,128)S(1)} %get-tuple-element.63), channel_id=1, source_target_pairs={{0,1},{1,2},{2,3},{3,0},{4,5},{5,6},{6,7},{7,4},{8,9},{9,10},{10,1... | collective-permute-start | bytes 196616 | tf_op jit(solution)/shard_map/ppermute | solution.py:340
  9.3 2.6 %collective-permute-start.1 = (f32[32,512]{1,0:T(8,128)S(1)}, f32[32,512]{1,0:T(8,128)S(1)}, u32[]{:S(2)}, u32[]{:S(2)}) collective-permute-start(f32[32,512]{1,0:T(8,128)S(1)} %get-tuple-element.64), channel_id=1, source_target_pairs={{0,2},{1,3},{2,0},{3,1},{4,6},{5,7},{6,4},{7,5},{8,10},{9,11},{10,... | collective-permute-start | bytes 196616 | tf_op jit(solution)/shard_map/ppermute | solution.py:340
  11.9 1.3 %collective-permute-start.2 = (f32[32,512]{1,0:T(8,128)S(1)}, f32[32,512]{1,0:T(8,128)S(1)}, u32[]{:S(2)}, u32[]{:S(2)}) collective-permute-start(f32[32,512]{1,0:T(8,128)S(1)} %get-tuple-element.65), channel_id=1, source_target_pairs={{0,3},{1,0},{2,1},{3,2},{4,7},{5,4},{6,5},{7,6},{8,11},{9,8},{10,9... | collective-permute-start | bytes 196616 | tf_op jit(solution)/shard_map/ppermute | solution.py:340
  13.2 0.0 all-to-all-done.arrived_ref
  13.2 6.7 %smooth0.1 = (f32[128,128]{1,0:T(8,128)S(1)}, f32[32,8,128]{2,1,0:T(8,128)S(1)}, f32[8,128]{1,0:T(8,128)S(1)}, f32[32,128]{1,0:T(8,128)S(1)}, f32[1,32,128]{2,1,...) custom-call(f32[8,32,128]{2,1,0:T(8,128)S(1)} %all-to-all-done.arriv, ...), custom_call_target="tpu_custom_call" | custom-call | tf_op jit(solution)/shard_map/smooth0/pallas_call | solution.py:111
  20.0 0.0 collective-permute-done.1.refs_20_
  20.0 12.2 %all_to_all.45.refs_0_ = f32[32,8,128]{2,1,0:T(8,128)S(1)} all-to-all(f32[32,8,128]{2,1,0:T(8,128)S(1)} %get-tuple-element.66), channel_id=1, replica_groups=mesh['sub'=8,'coarse'=4] {'sub','coarse'}, dimensions={0} | all-to-all | bytes 262144 | tf_op jit(solution)/shard_map/all_to_all | solution.py:768
  32.2 0.7 advance0.1
  32.8 7.4 %all_to_all.46.arrived_ref = f32[8,16,128]{2,1,0:T(8,128)S(1)} all-to-all(f32[8,16,128]{2,1,0:T(8,128)S(1)} %get-tuple-element.84.stat_ref), channel_id=1, replica_groups=mesh['sub'=8,'coarse'=4] {'sub'}, dimensions={0} | all-to-all | bytes 131072 | tf_op jit(solution)/shard_map/all_to_all | solution.py:700
  40.2 1.6 %smooth1.1 = (f32[128,128]{1,0:T(8,128)S(1)}, f32[32,8,128]{2,1,0:T(8,128)S(1)}, f32[8,128]{1,0:T(8,128)S(1)}) custom-call(f32[8,16,128]{2,1,0:T(8,128)S(1)} %all_to_all.46.arrived_ref, f32[128,128]{1,0:T(8,128)S(1)} %get-tuple-element.85.vector_ref.refs_3_, bf16[64,256,256]{2,1,0:T(8,128)(2,1)S(1)} %get-tuple-element.86.weight_ref, ...), custom_call_target="tpu_custom_call" | custom-call | tf_op jit(solution)/shard_map/smooth1/pallas_call | solution.py:111
  41.9 10.1 %all_to_all.47.refs_0_ = f32[32,8,128]{2,1,0:T(8,128)S(1)} all-to-all(f32[32,8,128]{2,1,0:T(8,128)S(1)} %get-tuple-element.87), channel_id=1, replica_groups=mesh['sub'=8,'coarse'=4] {'sub','coarse'}, dimensions={0} | all-to-all | bytes 262144 | tf_op jit(solution)/shard_map/all_to_all | solution.py:768
  52.0 0.7 advance1.1
  52.6 7.4 %all_to_all.48.arrived_ref = f32[8,16,128]{2,1,0:T(8,128)S(1)} all-to-all(f32[8,16,128]{2,1,0:T(8,128)S(1)} %get-tuple-element.91.stat_ref), channel_id=1, replica_groups=mesh['sub'=8,'coarse'=4] {'sub'}, dimensions={0} | all-to-all | bytes 131072 | tf_op jit(solution)/shard_map/all_to_all | solution.py:700
  60.0 1.6 %smooth2.1 = (f32[128,128]{1,0:T(8,128)S(1)}, f32[32,8,128]{2,1,0:T(8,128)S(1)}, f32[8,128]{1,0:T(8,128)S(1)}) custom-call(f32[8,16,128]{2,1,0:T(8,128)S(1)} %all_to_all.48.arrived_ref, f32[128,128]{1,0:T(8,128)S(1)} %get-tuple-element.92.vector_ref.refs_3_, bf16[64,256,256]{2,1,0:T(8,128)(2,1)S(1)} %get-tuple-element.86.weight_ref, ...), custom_call_target="tpu_custom_call" | custom-call | tf_op jit(solution)/shard_map/smooth2/pallas_call | solution.py:111
  61.7 10.1 %all_to_all.49.refs_0_ = f32[32,8,128]{2,1,0:T(8,128)S(1)} all-to-all(f32[32,8,128]{2,1,0:T(8,128)S(1)} %get-tuple-element.93), channel_id=1, replica_groups=mesh['sub'=8,'coarse'=4] {'sub','coarse'}, dimensions={0} | all-to-all | bytes 262144 | tf_op jit(solution)/shard_map/all_to_all | solution.py:768
  71.8 0.7 advance2.1
  72.5 7.4 %all_to_all.50.arrived_ref = f32[8,16,128]{2,1,0:T(8,128)S(1)} all-to-all(f32[8,16,128]{2,1,0:T(8,128)S(1)} %get-tuple-element.97.stat_ref), channel_id=1, replica_groups=mesh['sub'=8,'coarse'=4] {'sub'}, dimensions={0} | all-to-all | bytes 131072 | tf_op jit(solution)/shard_map/all_to_all | solution.py:700
  79.9 1.6 %smooth3.1 = (f32[128,128]{1,0:T(8,128)S(1)}, f32[32,8,128]{2,1,0:T(8,128)S(1)}, f32[8,128]{1,0:T(8,128)S(1)}) custom-call(f32[8,16,128]{2,1,0:T(8,128)S(1)} %all_to_all.50.arrived_ref, f32[128,128]{1,0:T(8,128)S(1)} %get-tuple-element.98.vector_ref.refs_3_, bf16[64,256,256]{2,1,0:T(8,128)(2,1)S(1)} %get-tuple-element.86.weight_ref, ...), custom_call_target="tpu_custom_call" | custom-call | tf_op jit(solution)/shard_map/smooth3/pallas_call | solution.py:111
  81.5 10.1 %all_to_all.51.refs_0_ = f32[32,8,128]{2,1,0:T(8,128)S(1)} all-to-all(f32[32,8,128]{2,1,0:T(8,128)S(1)} %get-tuple-element.99), channel_id=1, replica_groups=mesh['sub'=8,'coarse'=4] {'sub','coarse'}, dimensions={0} | all-to-all | bytes 262144 | tf_op jit(solution)/shard_map/all_to_all | solution.py:768
  91.6 0.6 advance3.1
  92.2 10.1 %all_to_all.52.arrived_ref = f32[32,8,128]{2,1,0:T(8,128)S(1)} all-to-all(f32[32,8,128]{2,1,0:T(8,128)S(1)} %get-tuple-element.103), channel_id=1, replica_groups=mesh['sub'=8,'coarse'=4] {'sub','coarse'}, dimensions={0} | all-to-all | bytes 262144 | tf_op jit(solution)/shard_map/all_to_all | solution.py:803
  102.3 0.8 finish.1
  (2 shorter events, 0.0 us)
Async XLA Ops:
  2.5 10.7 %all-to-all-start = ((f32[8,32,128]{2,1,0:T(8,128)}), f32[8,32,128]{2,1,0:T(8,128)S(1)}, u32[]{:S(2)}, u32[]{:S(2)}) async-start(f32[8,32,128]{2,1,0:T(8,128)} %get-tuple-element.55.stat_ref), calls=%async_computation | async-start | bytes 262144 | tf_op jit(solution)/shard_map/all_to_all | solution.py:700
  7.7 12.2 %collective-permute-start = (f32[32,512]{1,0:T(8,128)S(1)}, f32[32,512]{1,0:T(8,128)S(1)}, u32[]{:S(2)}, u32[]{:S(2)}) collective-permute-start(f32[32,512]{1,0:T(8,128)S(1)} %get-tuple-element.63), channel_id=1, source_target_pairs={{0,1},{1,2},{2,3},{3,0},{4,5},{5,6},{6,7},{7,4},{8,9},{9,10},{10,1... | collective-permute-start | bytes 196616 | tf_op jit(solution)/shard_map/ppermute | solution.py:340
  9.3 10.7 %collective-permute-start.1 = (f32[32,512]{1,0:T(8,128)S(1)}, f32[32,512]{1,0:T(8,128)S(1)}, u32[]{:S(2)}, u32[]{:S(2)}) collective-permute-start(f32[32,512]{1,0:T(8,128)S(1)} %get-tuple-element.64), channel_id=1, source_target_pairs={{0,2},{1,3},{2,0},{3,1},{4,6},{5,7},{6,4},{7,5},{8,10},{9,11},{10,... | collective-permute-start | bytes 196616 | tf_op jit(solution)/shard_map/ppermute | solution.py:340
  11.9 8.1 %collective-permute-start.2 = (f32[32,512]{1,0:T(8,128)S(1)}, f32[32,512]{1,0:T(8,128)S(1)}, u32[]{:S(2)}, u32[]{:S(2)}) collective-permute-start(f32[32,512]{1,0:T(8,128)S(1)} %get-tuple-element.65), channel_id=1, source_target_pairs={{0,3},{1,0},{2,1},{3,2},{4,7},{5,4},{6,5},{7,6},{8,11},{9,8},{10,9... | collective-permute-start | bytes 196616 | tf_op jit(solution)/shard_map/ppermute | solution.py:340

commit v6 on v5

--- a/solution.py
+++ b/solution.py
@@ -12,6 +12,7 @@
 LANES = 128
 ROWS = 8
 INVERSE_PARTS = 4
+DIRECT_GROUPS = 4
 BF16 = jnp.bfloat16
 F32 = jnp.float32
 
@@ -160,6 +161,8 @@
     margin_rows = rounds * widest
     table_rows = -(-2 * margin_rows // LANES) * LANES
     full = (block_count, unknowns)
+    direct_blocks = DIRECT_GROUPS * ROWS
+    paired_blocks = block_count - direct_blocks
 
     v_at = 0
     z_at = v_at + (ITERS - 1) * block_count
@@ -202,10 +205,9 @@
         return jnp.concatenate(lines, axis=0)
 
     def begin(
-        blocks_ref,
-        partner_ref,
-        width_ref,
-        number_ref,
+        blocks_hbm,
+        partner_hbm,
+        width_hbm,
         start_hbm,
         basis_hbm,
         member_of_hbm,
@@ -224,28 +226,48 @@
             member_of_ref,
         ) = refs[:9]
         chunk_refs = refs[9 : 9 + parts]
-        semaphores = refs[9 + parts]
+        (
+            blocks_ref,
+            partner_ref,
+            width_ref,
+            number_ref,
+            held_ref,
+            semaphores,
+            scalar_semaphores,
+        ) = refs[9 + parts :]
+        scalar_copies = [
+            pltpu.make_async_copy(source, to, scalar_semaphores.at[position])
+            for position, (source, to) in enumerate(
+                [
+                    (member_of_hbm, number_ref),
+                    (blocks_hbm, blocks_ref),
+                    (partner_hbm, partner_ref),
+                    (width_hbm, width_ref),
+                ]
+            )
+        ]
         copies = [
             pltpu.make_async_copy(source, to, semaphores.at[position])
             for position, (source, to) in enumerate(
                 [(start_hbm, start_ref), (basis_hbm, basis_ref), (member_of_hbm, member_of_ref)]
             )
         ]
+        held_copies = [
+            pltpu.make_async_copy(
+                coarse_hbm.at[
+                    pl.ds((span * parts + part_id) * own_aggregates, own_aggregates), :
+                ],
+                held_ref.at[part_id, pl.ds(span * own_aggregates, own_aggregates), :],
+                semaphores.at[3 + span * parts + part_id],
+            )
+            for span in range(sub_span)
+            for part_id in range(parts)
+        ]
+        for copy in scalar_copies + copies + held_copies:
+            copy.start()
+        for copy in scalar_copies:
+            copy.wait()
         own_part = (number_ref[0, 0] >> own_bits) & (parts - 1)
-        chunk_copies = []
-        for turn, chunk_ref in enumerate(chunk_refs):
-            to_part = (own_part + turn) & (parts - 1)
-            for span in range(sub_span):
-                first = pl.multiple_of((span * parts + to_part) * own_aggregates, own_aggregates)
-                chunk_copies.append(
-                    pltpu.make_async_copy(
-                        coarse_hbm.at[pl.ds(first, own_aggregates), :],
-                        chunk_ref.at[pl.ds(span * own_aggregates, own_aggregates), :],
-                        semaphores.at[3 + turn * sub_span + span],
-                    )
-                )
-        for copy in copies + chunk_copies:
-            copy.start()
         row = iota((widest, LANES), 0)
         lane = iota((widest, LANES), 1)
         tables = []
@@ -296,8 +318,10 @@
             for chunk in range(sub_chunks):
                 at = at + widest
                 slot_ref[sub_id, at : at + widest, :] = rows_lane[chunk][sub_id]
-        for copy in chunk_copies:
+        for copy in held_copies:
             copy.wait()
+        for turn, chunk_ref in enumerate(chunk_refs):
+            chunk_ref[...] = held_ref[(own_part + turn) & (parts - 1)]
 
     (
         outgoing,
@@ -327,14 +351,21 @@
         blocks,
         partner,
         margin_width,
-        aggregate[0],
         right_side[0, 0],
         coarse_basis[0, 0],
         aggregate[0],
         coarse_inverse,
         name="begin",
-        places="sssshhhh",
-        scratch=[pltpu.SemaphoreType.DMA((3 + parts * sub_span,))],
+        places="hhhhhhh",
+        scratch=[
+            pltpu.SMEM((rounds, widest), jnp.int32),
+            pltpu.SMEM((1, rounds), jnp.int32),
+            pltpu.SMEM((1, rounds), jnp.int32),
+            pltpu.SMEM((1, block_count), jnp.int32),
+            vmem((parts, chunk_rows, aggregates)),
+            pltpu.SemaphoreType.DMA((3 + parts * sub_span,)),
+            pltpu.SemaphoreType.DMA((4,)),
+        ],
     )
     for turn in range(1, parts):
         coarse_chunks[turn] = lax.ppermute(
@@ -378,6 +409,13 @@
     def block_rows(shifted_ref, group):
         rows = pl.ds(pl.multiple_of(group * ROWS, ROWS), ROWS)
         return paired_rows(shifted_ref[rows, :])
+
+    def direct_product(values, blocks_at):
+        lines = []
+        for offset in range(ROWS):
+            scaled = blocks_at(offset) * values[offset : offset + 1, :]
+            lines.append(jnp.sum(scaled, axis=1)[None, :])
+        return jnp.concatenate(lines, axis=0)
 
     def block_product(left, weight_of):
         row = iota((ROWS, unknowns), 0)
@@ -410,6 +448,7 @@
             basis_rows_ref,
             lane_rows_ref,
             weight_ref,
+            direct_ref,
             pair_ref,
             target_ref,
             sub_member_ref,
@@ -433,17 +472,29 @@
             )
         ]
 
-        span = block_count // INVERSE_PARTS
+        span = paired_blocks // INVERSE_PARTS
+        direct_span = direct_blocks // INVERSE_PARTS
+        direct_copies = [
+            pltpu.make_async_copy(
+                inverse_hbm.at[pl.ds(number * direct_span, direct_span)],
+                direct_ref.at[pl.ds(number * direct_span, direct_span)],
+                semaphores.at[3 + number],
+            )
+            for number in range(INVERSE_PARTS)
+        ]
         part_copies = [
             pltpu.make_async_copy(
-                inverse_hbm.at[pl.ds(number * span, span)],
+                inverse_hbm.at[pl.ds(direct_blocks + number * span, span)],
                 inverse_ref.at[pl.ds(number * span, span)],
                 part_semaphores.at[number],
             )
             for number in range(INVERSE_PARTS)
         ]
-        for copy in copies + part_copies:
+        for copy in copies:
             copy.start()
+        for number in range(INVERSE_PARTS):
+            direct_copies[number].start()
+            part_copies[number].start()
         route = route_ref[...]
         table = selector_ref[:, 0:block_count].astype(F32)
         pieces = [table, table]
@@ -473,11 +524,13 @@
         mapped = couple(arrived_rows(arrived_ref, 0, route), pair_ref, live_ref[...])
         shifted_ref[...] = vector_ref[...] + put(target_ref[...], mapped)
 
-        def step(group, carry):
+        paired_groups = (block_count // ROWS - DIRECT_GROUPS) // DIRECT_GROUPS
+
+        def paired_step(group):
             left = block_rows(shifted_ref, group)
 
             def weight_of(offset):
-                pair = group * (ROWS // 2) + offset
+                pair = (group - DIRECT_GROUPS) * (ROWS // 2) + offset
                 highs = []
                 lows = []
                 for position in range(2):
@@ -493,12 +546,21 @@
 
             rows = pl.ds(pl.multiple_of(group * ROWS, ROWS), ROWS)
             out_ref[rows, :] = block_product(left, weight_of)
+
+        def step(unit, carry):
+            rows = pl.ds(pl.multiple_of(unit * ROWS, ROWS), ROWS)
+            out_ref[rows, :] = direct_product(
+                shifted_ref[rows, :], lambda offset: direct_ref[unit * ROWS + offset]
+            )
+            for number in range(paired_groups):
+                paired_step(DIRECT_GROUPS + unit * paired_groups + number)
             return carry
 
-        groups = span // ROWS
+        units = DIRECT_GROUPS // INVERSE_PARTS
         for number in range(INVERSE_PARTS):
+            direct_copies[number].wait()
             part_copies[number].wait()
-            lax.fori_loop(number * groups, (number + 1) * groups, step, 0, unroll=2)
+            lax.fori_loop(number * units, (number + 1) * units, step, 0, unroll=1)
         for copy in copies[1:]:
             copy.wait()
         smooth_rest(
@@ -517,6 +579,7 @@
         arrived_ref,
         vector_ref,
         weight_ref,
+        direct_ref,
         pair_ref,
         target_ref,
         selector_ref,
@@ -533,10 +596,15 @@
         shifted = vector_ref[...] + put(target_ref[...], mapped)
         pieces = []
         for group in range(block_count // ROWS):
-            left = paired_rows(shifted[group * ROWS : (group + 1) * ROWS])
-            pieces.append(
-                block_product(left, lambda offset: weight_ref[group * (ROWS // 2) + offset])
-            )
+            values = shifted[group * ROWS : (group + 1) * ROWS]
+            if group < DIRECT_GROUPS:
+                piece = direct_product(values, lambda offset: direct_ref[group * ROWS + offset])
+            else:
+                at = (group - DIRECT_GROUPS) * (ROWS // 2)
+                piece = block_product(
+                    paired_rows(values), lambda offset: weight_ref[at + offset]
+                )
+            pieces.append(piece)
         out = jnp.concatenate(pieces, axis=0)
         out_ref[...] = out
         smooth_rest(
@@ -654,9 +722,11 @@
             against = earlier + [vector, product]
             if last:
                 (slot_ref,) = outs
-                block = statistics_block(
-                    product, basis_value, member_ref[...], home_ref[...], against, ROWS, 0
-                )
+                lane = iota((1, LANES), 1)
+                block = jnp.zeros((1, LANES), F32)
+                for position, other in enumerate(against):
+                    value = jnp.sum(column_sum(other * product), axis=1, keepdims=True)
+                    block = jnp.where(lane == position, value, block)
                 for slot in range(devices):
                     slot_ref[slot] = block
             else:
@@ -707,6 +777,7 @@
                 basis_rows,
                 lane_rows,
                 weights,
+                direct,
                 pairs,
                 target,
                 sub_member,
@@ -719,7 +790,8 @@
                 + [
                     vmem((margin_rows, unknowns)),
                     vmem((sub_chunks, margin_rows, LANES)),
-                    vmem((block_count // 2, 2 * unknowns, 2 * unknowns), BF16),
+                    vmem((paired_blocks // 2, 2 * unknowns, 2 * unknowns), BF16),
+                    vmem((direct_blocks, unknowns, unknowns)),
                     vmem((rounds, unknowns, 2 * unknowns), BF16),
                     vmem((block_count, table_rows), BF16),
                     vmem((block_count, sub_aggregates)),
@@ -741,10 +813,10 @@
                 name="smooth0",
                 places="vvvvvvvhhhh",
                 scratch=[
-                    vmem((block_count, unknowns, unknowns)),
+                    vmem((paired_blocks, unknowns, unknowns)),
                     vmem((rounds, unknowns, unknowns)),
                     vmem(full),
-                    pltpu.SemaphoreType.DMA((3,)),
+                    pltpu.SemaphoreType.DMA((3 + INVERSE_PARTS,)),
                     pltpu.SemaphoreType.DMA((INVERSE_PARTS,)),
                 ],
             )
@@ -756,6 +828,7 @@
                 arrived,
                 vector,
                 weights,
+                direct,
                 pairs,
                 target,
                 selector,
@@ -767,7 +840,7 @@
             )
         arrived = lax.all_to_all(slots, ("sub", "coarse"), 0, 0)
         if last:
-            outs = [vmem((devices, ROWS, LANES)), state_shape]
+            outs = [vmem((devices, 1, LANES)), state_shape]
         else:
             outs = [vmem(full), vmem((subs, widest + stat_rows, unknowns)), state_shape]
         made = call(
@@ -803,12 +876,9 @@
     arrived = lax.all_to_all(slots, ("sub", "coarse"), 0, 0)
 
     def finish(arrived_ref, state_ref, out_ref):
-        total = arrived_ref[0]
-        for slot in range(1, devices):
-            total = total + arrived_ref[slot]
-        products = jnp.sum(total, axis=1, keepdims=True)
-        heads = [products[i : i + 1] for i in range(ITERS)]
-        square = products[ITERS : ITERS + 1]
+        total = column_sum(arrived_ref[...].reshape(devices, LANES))
+        heads = [total[:, i : i + 1] for i in range(ITERS)]
+        square = total[:, ITERS : ITERS + 1]
         remaining = square
         for head in heads:
             remaining = remaining - head * head

time: 104 us -> 100 us (0.962)
  Pallas kernels: 17.5 us -> 15.5 us
  blocking collectives: 74.8 us -> 73.6 us
    pallas_call x10, Pallas kernels: 17.5 us -> 15.5 us  [call(): pl.pallas_call(kernel, out_shape=outs, in_specs=[pl.BlockSpec(memory_spac...]
    all_to_all x5, blocking collectives: 52.6 us -> 51.4 us  [on_device(): arrived = lax.all_to_all(slots, ('sub', 'coarse'), 0, 0)]
  transfers between devices with their start and end apart: 4 -> 4, of which waited for: 0 -> 0; matrix products, arithmetic and copies ran while one was open for 0% -> 0% of each run, Pallas kernels for 7% -> 6%
where the time goes in v6:
time: 100 us; the launch traced here: 99.9 us
  blocking collectives  73.6 us (74%)
  Pallas kernels  15.5 us (16%)
  starting transfers between devices  10.7 us (11%)
    all_to_all x5, blocking collectives, on_device(): arrived = lax.all_to_all(slots, ('sub', 'coarse'), 0, 0)  51.4 us
    all_to_all x3, blocking collectives, on_device(): arrived = lax.all_to_all(outgoing, 'sub', 0, 0)  22.2 us
    pallas_call x10, Pallas kernels, call(): pl.pallas_call(kernel, out_shape=outs, in_specs=[pl.BlockSpec(memory_spac...  15.5 us
    ppermute x3, starting transfers between devices, on_device(): lax.ppermute(coarse_chunks[turn], 'coarse', [(i, (i + turn) % parts) for...  5.51 us
    all_to_all x1, starting transfers between devices, on_device(): arrived = lax.all_to_all(outgoing, 'sub', 0, 0)  5.18 us
  transfers between devices with their start and end apart: 4, of which 0 were waited for; matrix products, arithmetic and copies ran while one was open for 0% of the time, Pallas kernels for 6%

profile of v6, /device:TPU:0, one launch (start us, length us, event | category | flops | bytes accessed | tf_op | source)
XLA Modules:
  0.0 99.9 jit_solution(11164896062198777750)
XLA Ops:
  0.0 1.9 %begin.1 = (f32[8,32,128]{2,1,0:T(8,128)}, bf16[32,256]{1,0:T(8,128)(2,1)S(1)}, f32[32,128]{1,0:T(8,128)S(1)}, f32[32,128]{1,0:T(8,128)S(1)}, f32[128,128]{1,0:T...) custom-call(s32[4,8]{1,0:T(4,128)} %bitcast.15, ...), custom_call_target="tpu_custom_call" | custom-call | tf_op jit(solution)/shard_map/begin/pallas_call | solution.py:112
  1.9 5.2 %all-to-all-start = ((f32[8,32,128]{2,1,0:T(8,128)}), f32[8,32,128]{2,1,0:T(8,128)S(1)}, u32[]{:S(2)}, u32[]{:S(2)}) async-start(f32[8,32,128]{2,1,0:T(8,128)} %get-tuple-element.56.stat_ref), calls=%async_computation | async-start | bytes 262144 | tf_op jit(solution)/shard_map/all_to_all | solution.py:770
  7.0 1.6 %collective-permute-start = (f32[32,512]{1,0:T(8,128)S(1)}, f32[32,512]{1,0:T(8,128)S(1)}, u32[]{:S(2)}, u32[]{:S(2)}) collective-permute-start(f32[32,512]{1,0:T(8,128)S(1)} %get-tuple-element.64), channel_id=1, source_target_pairs={{0,1},{1,2},{2,3},{3,0},{4,5},{5,6},{6,7},{7,4},{8,9},{9,10},{10,1... | collective-permute-start | bytes 196616 | tf_op jit(solution)/shard_map/ppermute | solution.py:371
  8.6 2.6 %collective-permute-start.1 = (f32[32,512]{1,0:T(8,128)S(1)}, f32[32,512]{1,0:T(8,128)S(1)}, u32[]{:S(2)}, u32[]{:S(2)}) collective-permute-start(f32[32,512]{1,0:T(8,128)S(1)} %get-tuple-element.65), channel_id=1, source_target_pairs={{0,2},{1,3},{2,0},{3,1},{4,6},{5,7},{6,4},{7,5},{8,10},{9,11},{10,... | collective-permute-start | bytes 196616 | tf_op jit(solution)/shard_map/ppermute | solution.py:371
  11.2 1.3 %collective-permute-start.2 = (f32[32,512]{1,0:T(8,128)S(1)}, f32[32,512]{1,0:T(8,128)S(1)}, u32[]{:S(2)}, u32[]{:S(2)}) collective-permute-start(f32[32,512]{1,0:T(8,128)S(1)} %get-tuple-element.66), channel_id=1, source_target_pairs={{0,3},{1,0},{2,1},{3,2},{4,7},{5,4},{6,5},{7,6},{8,11},{9,8},{10,9... | collective-permute-start | bytes 196616 | tf_op jit(solution)/shard_map/ppermute | solution.py:371
  12.6 0.0 all-to-all-done.arrived_ref
  12.6 6.0 %smooth0.1 = (f32[128,128]{1,0:T(8,128)S(1)}, f32[32,8,128]{2,1,0:T(8,128)S(1)}, f32[8,128]{1,0:T(8,128)S(1)}, f32[32,128]{1,0:T(8,128)S(1)}, f32[1,32,128]{2,1,...) custom-call(f32[8,32,128]{2,1,0:T(8,128)S(1)} %all-to-all-done.arriv, ...), custom_call_target="tpu_custom_call" | custom-call | tf_op jit(solution)/shard_map/smooth0/pallas_call | solution.py:112
  18.6 0.0 collective-permute-done.refs_19_
  18.6 12.2 %all_to_all.45.refs_0_ = f32[32,8,128]{2,1,0:T(8,128)S(1)} all-to-all(f32[32,8,128]{2,1,0:T(8,128)S(1)} %get-tuple-element.67), channel_id=1, replica_groups=mesh['sub'=8,'coarse'=4] {'sub','coarse'}, dimensions={0} | all-to-all | bytes 262144 | tf_op jit(solution)/shard_map/all_to_all | solution.py:841
  30.8 0.7 advance0.1
  31.5 7.4 %all_to_all.46.arrived_ref = f32[8,16,128]{2,1,0:T(8,128)S(1)} all-to-all(f32[8,16,128]{2,1,0:T(8,128)S(1)} %get-tuple-element.85.stat_ref), channel_id=1, replica_groups=mesh['sub'=8,'coarse'=4] {'sub'}, dimensions={0} | all-to-all | bytes 131072 | tf_op jit(solution)/shard_map/all_to_all | solution.py:770
  38.9 1.4 %smooth1.1 = (f32[128,128]{1,0:T(8,128)S(1)}, f32[32,8,128]{2,1,0:T(8,128)S(1)}, f32[8,128]{1,0:T(8,128)S(1)}) custom-call(f32[8,16,128]{2,1,0:T(8,128)S(1)} %all_to_all.46.arrived_ref, f32[128,128]{1,0:T(8,128)S(1)} %get-tuple-element.86.vector_ref.refs_3_, bf16[48,256,256]{2,1,0:T(8,128)(2,1)S(1)} %get-tuple-element.87.weight_ref, ...), custom_call_target="tpu_custom_call" | custom-call | tf_op jit(solution)/shard_map/smooth1/pallas_call | solution.py:112
  40.2 10.1 %all_to_all.47.refs_0_ = f32[32,8,128]{2,1,0:T(8,128)S(1)} all-to-all(f32[32,8,128]{2,1,0:T(8,128)S(1)} %get-tuple-element.89), channel_id=1, replica_groups=mesh['sub'=8,'coarse'=4] {'sub','coarse'}, dimensions={0} | all-to-all | bytes 262144 | tf_op jit(solution)/shard_map/all_to_all | solution.py:841
  50.4 0.7 advance1.1
  51.0 7.4 %all_to_all.48.arrived_ref = f32[8,16,128]{2,1,0:T(8,128)S(1)} all-to-all(f32[8,16,128]{2,1,0:T(8,128)S(1)} %get-tuple-element.93.stat_ref), channel_id=1, replica_groups=mesh['sub'=8,'coarse'=4] {'sub'}, dimensions={0} | all-to-all | bytes 131072 | tf_op jit(solution)/shard_map/all_to_all | solution.py:770
  58.4 1.4 %smooth2.1 = (f32[128,128]{1,0:T(8,128)S(1)}, f32[32,8,128]{2,1,0:T(8,128)S(1)}, f32[8,128]{1,0:T(8,128)S(1)}) custom-call(f32[8,16,128]{2,1,0:T(8,128)S(1)} %all_to_all.48.arrived_ref, f32[128,128]{1,0:T(8,128)S(1)} %get-tuple-element.94.vector_ref.refs_3_, bf16[48,256,256]{2,1,0:T(8,128)(2,1)S(1)} %get-tuple-element.87.weight_ref, ...), custom_call_target="tpu_custom_call" | custom-call | tf_op jit(solution)/shard_map/smooth2/pallas_call | solution.py:112
  59.8 10.1 %all_to_all.49.refs_0_ = f32[32,8,128]{2,1,0:T(8,128)S(1)} all-to-all(f32[32,8,128]{2,1,0:T(8,128)S(1)} %get-tuple-element.95), channel_id=1, replica_groups=mesh['sub'=8,'coarse'=4] {'sub','coarse'}, dimensions={0} | all-to-all | bytes 262144 | tf_op jit(solution)/shard_map/all_to_all | solution.py:841
  69.9 0.7 advance2.1
  70.6 7.4 %all_to_all.50.arrived_ref = f32[8,16,128]{2,1,0:T(8,128)S(1)} all-to-all(f32[8,16,128]{2,1,0:T(8,128)S(1)} %get-tuple-element.99.stat_ref), channel_id=1, replica_groups=mesh['sub'=8,'coarse'=4] {'sub'}, dimensions={0} | all-to-all | bytes 131072 | tf_op jit(solution)/shard_map/all_to_all | solution.py:770
  78.0 1.4 %smooth3.1 = (f32[128,128]{1,0:T(8,128)S(1)}, f32[32,8,128]{2,1,0:T(8,128)S(1)}, f32[8,128]{1,0:T(8,128)S(1)}) custom-call(f32[8,16,128]{2,1,0:T(8,128)S(1)} %all_to_all.50.arrived_ref, f32[128,128]{1,0:T(8,128)S(1)} %get-tuple-element.100.vector_ref.refs_3_, bf16[48,256,256]{2,1,0:T(8,128)(2,1)S(1)} %get-tuple-element.87.weight_ref, ...), custom_call_target="tpu_custom_call" | custom-call | tf_op jit(solution)/shard_map/smooth3/pallas_call | solution.py:112
  79.4 10.1 %all_to_all.51.refs_0_ = f32[32,8,128]{2,1,0:T(8,128)S(1)} all-to-all(f32[32,8,128]{2,1,0:T(8,128)S(1)} %get-tuple-element.101), channel_id=1, replica_groups=mesh['sub'=8,'coarse'=4] {'sub','coarse'}, dimensions={0} | all-to-all | bytes 262144 | tf_op jit(solution)/shard_map/all_to_all | solution.py:841
  89.5 0.6 advance3.1
  90.1 8.9 %all_to_all.52.arrived_ref = f32[32,1,128]{2,1,0:T(1,128)S(1)} all-to-all(f32[32,1,128]{2,1,0:T(1,128)S(1)} %get-tuple-element.105), channel_id=1, replica_groups=mesh['sub'=8,'coarse'=4] {'sub','coarse'}, dimensions={0} | all-to-all | bytes 32768 | tf_op jit(solution)/shard_map/all_to_all | solution.py:876
  99.0 0.9 finish.1
  (2 shorter events, 0.0 us)
Async XLA Ops:
  1.9 10.7 %all-to-all-start = ((f32[8,32,128]{2,1,0:T(8,128)}), f32[8,32,128]{2,1,0:T(8,128)S(1)}, u32[]{:S(2)}, u32[]{:S(2)}) async-start(f32[8,32,128]{2,1,0:T(8,128)} %get-tuple-element.56.stat_ref), calls=%async_computation | async-start | bytes 262144 | tf_op jit(solution)/shard_map/all_to_all | solution.py:770
  7.0 11.6 %collective-permute-start = (f32[32,512]{1,0:T(8,128)S(1)}, f32[32,512]{1,0:T(8,128)S(1)}, u32[]{:S(2)}, u32[]{:S(2)}) collective-permute-start(f32[32,512]{1,0:T(8,128)S(1)} %get-tuple-element.64), channel_id=1, source_target_pairs={{0,1},{1,2},{2,3},{3,0},{4,5},{5,6},{6,7},{7,4},{8,9},{9,10},{10,1... | collective-permute-start | bytes 196616 | tf_op jit(solution)/shard_map/ppermute | solution.py:371
  8.6 10.0 %collective-permute-start.1 = (f32[32,512]{1,0:T(8,128)S(1)}, f32[32,512]{1,0:T(8,128)S(1)}, u32[]{:S(2)}, u32[]{:S(2)}) collective-permute-start(f32[32,512]{1,0:T(8,128)S(1)} %get-tuple-element.65), channel_id=1, source_target_pairs={{0,2},{1,3},{2,0},{3,1},{4,6},{5,7},{6,4},{7,5},{8,10},{9,11},{10,... | collective-permute-start | bytes 196616 | tf_op jit(solution)/shard_map/ppermute | solution.py:371
  11.2 7.4 %collective-permute-start.2 = (f32[32,512]{1,0:T(8,128)S(1)}, f32[32,512]{1,0:T(8,128)S(1)}, u32[]{:S(2)}, u32[]{:S(2)}) collective-permute-start(f32[32,512]{1,0:T(8,128)S(1)} %get-tuple-element.66), channel_id=1, source_target_pairs={{0,3},{1,0},{2,1},{3,2},{4,7},{5,4},{6,5},{7,6},{8,11},{9,8},{10,9... | collective-permute-start | bytes 196616 | tf_op jit(solution)/shard_map/ppermute | solution.py:371

commit v7 on v6

--- a/solution.py
+++ b/solution.py
@@ -212,6 +212,7 @@
         basis_hbm,
         member_of_hbm,
         coarse_hbm,
+        coupling_hbm,
         *refs,
     ):
         (
@@ -224,8 +225,9 @@
             start_ref,
             basis_ref,
             member_of_ref,
-        ) = refs[:9]
-        chunk_refs = refs[9 : 9 + parts]
+            coupling_ref,
+        ) = refs[:10]
+        chunk_refs = refs[10 : 10 + parts]
         (
             blocks_ref,
             partner_ref,
@@ -234,7 +236,7 @@
             held_ref,
             semaphores,
             scalar_semaphores,
-        ) = refs[9 + parts :]
+        ) = refs[10 + parts :]
         scalar_copies = [
             pltpu.make_async_copy(source, to, scalar_semaphores.at[position])
             for position, (source, to) in enumerate(
@@ -263,7 +265,10 @@
             for span in range(sub_span)
             for part_id in range(parts)
         ]
-        for copy in scalar_copies + copies + held_copies:
+        coupling_copy = pltpu.make_async_copy(
+            coupling_hbm, coupling_ref, scalar_semaphores.at[4]
+        )
+        for copy in scalar_copies + copies + held_copies + [coupling_copy]:
             copy.start()
         for copy in scalar_copies:
             copy.wait()
@@ -322,6 +327,7 @@
             copy.wait()
         for turn, chunk_ref in enumerate(chunk_refs):
             chunk_ref[...] = held_ref[(own_part + turn) & (parts - 1)]
+        coupling_copy.wait()
 
     (
         outgoing,
@@ -333,6 +339,7 @@
         start_vector,
         basis,
         member_of,
+        couplings,
         *coarse_chunks,
     ) = call(
         begin,
@@ -346,6 +353,7 @@
             vmem(full),
             vmem(full),
             vmem((1, block_count), jnp.int32),
+            vmem((rounds, unknowns, unknowns)),
         ]
         + [vmem((chunk_rows, aggregates))] * parts,
         blocks,
@@ -355,8 +363,9 @@
         coarse_basis[0, 0],
         aggregate[0],
         coarse_inverse,
+        coupling[0, 0],
         name="begin",
-        places="hhhhhhh",
+        places="hhhhhhhh",
         scratch=[
             pltpu.SMEM((rounds, widest), jnp.int32),
             pltpu.SMEM((1, rounds), jnp.int32),
@@ -364,7 +373,7 @@
             pltpu.SMEM((1, block_count), jnp.int32),
             vmem((parts, chunk_rows, aggregates)),
             pltpu.SemaphoreType.DMA((3 + parts * sub_span,)),
-            pltpu.SemaphoreType.DMA((4,)),
+            pltpu.SemaphoreType.DMA((5,)),
         ],
     )
     for turn in range(1, parts):
@@ -435,8 +444,8 @@
         live_ref,
         member_of_ref,
         stat_ref,
+        coupling_ref,
         inverse_hbm,
-        coupling_hbm,
         diagonal_hbm,
         link_hbm,
         *refs,
@@ -456,7 +465,6 @@
             diagonal_ref,
             link_ref,
             inverse_ref,
-            coupling_ref,
             shifted_ref,
             semaphores,
             part_semaphores,
@@ -465,7 +473,6 @@
             pltpu.make_async_copy(source, to, semaphores.at[position])
             for position, (source, to) in enumerate(
                 [
-                    (coupling_hbm, coupling_ref),
                     (diagonal_hbm, diagonal_ref),
                     (link_hbm, link_ref),
                 ]
@@ -512,16 +519,16 @@
             ).T
         part_ref[...] = hot(((numbers >> own_bits) & (parts - 1)) == iota((ROWS, LANES), 0))
         at = widest + stat_rows
-        basis_rows_ref[...] = arrived_rows(arrived_ref, at, route)
+        basis_rows = arrived_rows(arrived_ref, at, route)
         for chunk in range(sub_chunks):
             at = at + widest
             lane_rows_ref[chunk] = arrived_rows(arrived_ref, at, route)
-        copies[0].wait()
         for round_id in range(rounds):
             high, low = split(coupling_ref[round_id])
             pair_ref[round_id, :, 0:unknowns] = high
             pair_ref[round_id, :, unknowns : 2 * unknowns] = low
         mapped = couple(arrived_rows(arrived_ref, 0, route), pair_ref, live_ref[...])
+        basis_rows_ref[...] = couple(basis_rows, pair_ref, live_ref[...])
         shifted_ref[...] = vector_ref[...] + put(target_ref[...], mapped)
 
         paired_groups = (block_count // ROWS - DIRECT_GROUPS) // DIRECT_GROUPS
@@ -534,7 +541,8 @@
                 highs = []
                 lows = []
                 for position in range(2):
-                    high, low = split(inverse_ref[pair * 2 + position].T)
+                    high, low = split(inverse_ref[pair * 2 + position])
+                    high, low = high.T, low.T
                     lanes = slice(position * unknowns, (position + 1) * unknowns)
                     weight_ref[pair, 0:unknowns, lanes] = high
                     weight_ref[pair, unknowns : 2 * unknowns, lanes] = low
@@ -561,7 +569,7 @@
             direct_copies[number].wait()
             part_copies[number].wait()
             lax.fori_loop(number * units, (number + 1) * units, step, 0, unroll=1)
-        for copy in copies[1:]:
+        for copy in copies:
             copy.wait()
         smooth_rest(
             arrived_ref,
@@ -707,7 +715,8 @@
                 direction = direction - head * held(z_at, number, block_count)
             direction = direction * scale
             route = route_ref[...]
-            rows = gather_rounds(pieces, route, rounds) + row_coarse * basis_rows_ref[...]
+            rows = couple(gather_rounds(pieces, route, rounds), pair_ref, live_ref[...])
+            rows = rows + row_coarse * basis_rows_ref[...]
             for number, head in enumerate(heads):
                 rows = rows - head * held(m_at, number, margin_rows)
             rows = rows * scale
@@ -717,7 +726,7 @@
                 vector = vector - head * other
             vector = vector * scale
             product = line_product(direction, diagonal_ref[...], link_ref[...]) - put(
-                target_ref[...], couple(rows, pair_ref, live_ref[...])
+                target_ref[...], rows
             )
             against = earlier + [vector, product]
             if last:
@@ -806,15 +815,14 @@
                 live,
                 member_of,
                 outgoing,
+                couplings,
                 block_inverse[0, 0],
-                coupling[0, 0],
                 diagonal[0, 0],
                 cell_link[0, 0],
                 name="smooth0",
-                places="vvvvvvvhhhh",
+                places="vvvvvvvvhhh",
                 scratch=[
                     vmem((paired_blocks, unknowns, unknowns)),
-                    vmem((rounds, unknowns, unknowns)),
                     vmem(full),
                     pltpu.SemaphoreType.DMA((3 + INVERSE_PARTS,)),
                     pltpu.SemaphoreType.DMA((INVERSE_PARTS,)),

time: 100 us -> 99.7 us (level)
  no operation moved by 1% of the time
where the time goes in v7:
time: 99.7 us; the launch traced here: 99.3 us
  blocking collectives  73.6 us (74%)
  Pallas kernels  14.9 us (15%)
  starting transfers between devices  10.7 us (11%)
    all_to_all x5, blocking collectives, on_device(): arrived = lax.all_to_all(slots, ('sub', 'coarse'), 0, 0)  51.4 us
    all_to_all x3, blocking collectives, on_device(): arrived = lax.all_to_all(outgoing, 'sub', 0, 0)  22.2 us
    pallas_call x10, Pallas kernels, call(): pl.pallas_call(kernel, out_shape=outs, in_specs=[pl.BlockSpec(memory_spac...  14.9 us
    ppermute x3, starting transfers between devices, on_device(): lax.ppermute(coarse_chunks[turn], 'coarse', [(i, (i + turn) % parts) for...  5.51 us
    all_to_all x1, starting transfers between devices, on_device(): arrived = lax.all_to_all(outgoing, 'sub', 0, 0)  5.18 us
  transfers between devices with their start and end apart: 4, of which 0 were waited for; matrix products, arithmetic and copies ran while one was open for 0% of the time, Pallas kernels for 6%

profile of v7, /device:TPU:0, one launch (start us, length us, event | category | flops | bytes accessed | tf_op | source)
XLA Modules:
  0.0 99.3 jit_solution(11074814433404213546)
XLA Ops:
  0.0 2.0 %begin.1 = (f32[8,32,128]{2,1,0:T(8,128)}, bf16[32,256]{1,0:T(8,128)(2,1)S(1)}, f32[32,128]{1,0:T(8,128)S(1)}, f32[32,128]{1,0:T(8,128)S(1)}, f32[128,128]{1,0:T...) custom-call(s32[4,8]{1,0:T(4,128)} %bitcast.15, ...), custom_call_target="tpu_custom_call" | custom-call | tf_op jit(solution)/shard_map/begin/pallas_call | solution.py:112
  2.0 5.2 %all-to-all-start = ((f32[8,32,128]{2,1,0:T(8,128)}), f32[8,32,128]{2,1,0:T(8,128)S(1)}, u32[]{:S(2)}, u32[]{:S(2)}) async-start(f32[8,32,128]{2,1,0:T(8,128)} %get-tuple-element.57.stat_ref), calls=%async_computation | async-start | bytes 262144 | tf_op jit(solution)/shard_map/all_to_all | solution.py:779
  7.2 1.6 %collective-permute-start = (f32[32,512]{1,0:T(8,128)S(1)}, f32[32,512]{1,0:T(8,128)S(1)}, u32[]{:S(2)}, u32[]{:S(2)}) collective-permute-start(f32[32,512]{1,0:T(8,128)S(1)} %get-tuple-element.66), channel_id=1, source_target_pairs={{0,1},{1,2},{2,3},{3,0},{4,5},{5,6},{6,7},{7,4},{8,9},{9,10},{10,1... | collective-permute-start | bytes 196616 | tf_op jit(solution)/shard_map/ppermute | solution.py:380
  8.7 2.6 %collective-permute-start.1 = (f32[32,512]{1,0:T(8,128)S(1)}, f32[32,512]{1,0:T(8,128)S(1)}, u32[]{:S(2)}, u32[]{:S(2)}) collective-permute-start(f32[32,512]{1,0:T(8,128)S(1)} %get-tuple-element.67), channel_id=1, source_target_pairs={{0,2},{1,3},{2,0},{3,1},{4,6},{5,7},{6,4},{7,5},{8,10},{9,11},{10,... | collective-permute-start | bytes 196616 | tf_op jit(solution)/shard_map/ppermute | solution.py:380
  11.3 1.3 %collective-permute-start.2 = (f32[32,512]{1,0:T(8,128)S(1)}, f32[32,512]{1,0:T(8,128)S(1)}, u32[]{:S(2)}, u32[]{:S(2)}) collective-permute-start(f32[32,512]{1,0:T(8,128)S(1)} %get-tuple-element.68), channel_id=1, source_target_pairs={{0,3},{1,0},{2,1},{3,2},{4,7},{5,4},{6,5},{7,6},{8,11},{9,8},{10,9... | collective-permute-start | bytes 196616 | tf_op jit(solution)/shard_map/ppermute | solution.py:380
  12.7 0.0 all-to-all-done.arrived_ref
  12.7 5.9 %smooth0.1 = (f32[128,128]{1,0:T(8,128)S(1)}, f32[32,8,128]{2,1,0:T(8,128)S(1)}, f32[8,128]{1,0:T(8,128)S(1)}, f32[32,128]{1,0:T(8,128)S(1)}, f32[1,32,128]{2,1,...) custom-call(f32[8,32,128]{2,1,0:T(8,128)S(1)} %all-to-all-done.arriv, ...), custom_call_target="tpu_custom_call" | custom-call | tf_op jit(solution)/shard_map/smooth0/pallas_call | solution.py:112
  18.6 0.0 collective-permute-done.refs_19_
  18.6 12.2 %all_to_all.45.refs_0_ = f32[32,8,128]{2,1,0:T(8,128)S(1)} all-to-all(f32[32,8,128]{2,1,0:T(8,128)S(1)} %get-tuple-element.69), channel_id=1, replica_groups=mesh['sub'=8,'coarse'=4] {'sub','coarse'}, dimensions={0} | all-to-all | bytes 262144 | tf_op jit(solution)/shard_map/all_to_all | solution.py:849
  30.8 0.5 advance0.1
  31.3 7.4 %all_to_all.46.arrived_ref = f32[8,16,128]{2,1,0:T(8,128)S(1)} all-to-all(f32[8,16,128]{2,1,0:T(8,128)S(1)} %get-tuple-element.87.stat_ref), channel_id=1, replica_groups=mesh['sub'=8,'coarse'=4] {'sub'}, dimensions={0} | all-to-all | bytes 131072 | tf_op jit(solution)/shard_map/all_to_all | solution.py:779
  38.7 1.4 %smooth1.1 = (f32[128,128]{1,0:T(8,128)S(1)}, f32[32,8,128]{2,1,0:T(8,128)S(1)}, f32[8,128]{1,0:T(8,128)S(1)}) custom-call(f32[8,16,128]{2,1,0:T(8,128)S(1)} %all_to_all.46.arrived_ref, f32[128,128]{1,0:T(8,128)S(1)} %get-tuple-element.88.vector_ref.refs_3_, bf16[48,256,256]{2,1,0:T(8,128)(2,1)S(1)} %get-tuple-element.89.weight_ref, ...), custom_call_target="tpu_custom_call" | custom-call | tf_op jit(solution)/shard_map/smooth1/pallas_call | solution.py:112
  40.1 10.1 %all_to_all.47.refs_0_ = f32[32,8,128]{2,1,0:T(8,128)S(1)} all-to-all(f32[32,8,128]{2,1,0:T(8,128)S(1)} %get-tuple-element.91), channel_id=1, replica_groups=mesh['sub'=8,'coarse'=4] {'sub','coarse'}, dimensions={0} | all-to-all | bytes 262144 | tf_op jit(solution)/shard_map/all_to_all | solution.py:849
  50.2 0.5 advance1.1
  50.7 7.4 %all_to_all.48.arrived_ref = f32[8,16,128]{2,1,0:T(8,128)S(1)} all-to-all(f32[8,16,128]{2,1,0:T(8,128)S(1)} %get-tuple-element.95.stat_ref), channel_id=1, replica_groups=mesh['sub'=8,'coarse'=4] {'sub'}, dimensions={0} | all-to-all | bytes 131072 | tf_op jit(solution)/shard_map/all_to_all | solution.py:779
  58.1 1.4 %smooth2.1 = (f32[128,128]{1,0:T(8,128)S(1)}, f32[32,8,128]{2,1,0:T(8,128)S(1)}, f32[8,128]{1,0:T(8,128)S(1)}) custom-call(f32[8,16,128]{2,1,0:T(8,128)S(1)} %all_to_all.48.arrived_ref, f32[128,128]{1,0:T(8,128)S(1)} %get-tuple-element.96.vector_ref.refs_3_, bf16[48,256,256]{2,1,0:T(8,128)(2,1)S(1)} %get-tuple-element.89.weight_ref, ...), custom_call_target="tpu_custom_call" | custom-call | tf_op jit(solution)/shard_map/smooth2/pallas_call | solution.py:112
  59.5 10.1 %all_to_all.49.refs_0_ = f32[32,8,128]{2,1,0:T(8,128)S(1)} all-to-all(f32[32,8,128]{2,1,0:T(8,128)S(1)} %get-tuple-element.97), channel_id=1, replica_groups=mesh['sub'=8,'coarse'=4] {'sub','coarse'}, dimensions={0} | all-to-all | bytes 262144 | tf_op jit(solution)/shard_map/all_to_all | solution.py:849
  69.6 0.5 advance2.1
  70.1 7.4 %all_to_all.50.arrived_ref = f32[8,16,128]{2,1,0:T(8,128)S(1)} all-to-all(f32[8,16,128]{2,1,0:T(8,128)S(1)} %get-tuple-element.101.stat_ref), channel_id=1, replica_groups=mesh['sub'=8,'coarse'=4] {'sub'}, dimensions={0} | all-to-all | bytes 131072 | tf_op jit(solution)/shard_map/all_to_all | solution.py:779
  77.5 1.4 %smooth3.1 = (f32[128,128]{1,0:T(8,128)S(1)}, f32[32,8,128]{2,1,0:T(8,128)S(1)}, f32[8,128]{1,0:T(8,128)S(1)}) custom-call(f32[8,16,128]{2,1,0:T(8,128)S(1)} %all_to_all.50.arrived_ref, f32[128,128]{1,0:T(8,128)S(1)} %get-tuple-element.102.vector_ref.refs_3_, bf16[48,256,256]{2,1,0:T(8,128)(2,1)S(1)} %get-tuple-element.89.weight_ref, ...), custom_call_target="tpu_custom_call" | custom-call | tf_op jit(solution)/shard_map/smooth3/pallas_call | solution.py:112
  78.9 10.1 %all_to_all.51.refs_0_ = f32[32,8,128]{2,1,0:T(8,128)S(1)} all-to-all(f32[32,8,128]{2,1,0:T(8,128)S(1)} %get-tuple-element.103), channel_id=1, replica_groups=mesh['sub'=8,'coarse'=4] {'sub','coarse'}, dimensions={0} | all-to-all | bytes 262144 | tf_op jit(solution)/shard_map/all_to_all | solution.py:849
  89.0 0.5 advance3.1
  89.5 8.9 %all_to_all.52.arrived_ref = f32[32,1,128]{2,1,0:T(1,128)S(1)} all-to-all(f32[32,1,128]{2,1,0:T(1,128)S(1)} %get-tuple-element.107), channel_id=1, replica_groups=mesh['sub'=8,'coarse'=4] {'sub','coarse'}, dimensions={0} | all-to-all | bytes 32768 | tf_op jit(solution)/shard_map/all_to_all | solution.py:884
  98.4 0.9 finish.1
  (2 shorter events, 0.0 us)
Async XLA Ops:
  2.0 10.7 %all-to-all-start = ((f32[8,32,128]{2,1,0:T(8,128)}), f32[8,32,128]{2,1,0:T(8,128)S(1)}, u32[]{:S(2)}, u32[]{:S(2)}) async-start(f32[8,32,128]{2,1,0:T(8,128)} %get-tuple-element.57.stat_ref), calls=%async_computation | async-start | bytes 262144 | tf_op jit(solution)/shard_map/all_to_all | solution.py:779
  7.2 11.5 %collective-permute-start = (f32[32,512]{1,0:T(8,128)S(1)}, f32[32,512]{1,0:T(8,128)S(1)}, u32[]{:S(2)}, u32[]{:S(2)}) collective-permute-start(f32[32,512]{1,0:T(8,128)S(1)} %get-tuple-element.66), channel_id=1, source_target_pairs={{0,1},{1,2},{2,3},{3,0},{4,5},{5,6},{6,7},{7,4},{8,9},{9,10},{10,1... | collective-permute-start | bytes 196616 | tf_op jit(solution)/shard_map/ppermute | solution.py:380
  8.7 9.9 %collective-permute-start.1 = (f32[32,512]{1,0:T(8,128)S(1)}, f32[32,512]{1,0:T(8,128)S(1)}, u32[]{:S(2)}, u32[]{:S(2)}) collective-permute-start(f32[32,512]{1,0:T(8,128)S(1)} %get-tuple-element.67), channel_id=1, source_target_pairs={{0,2},{1,3},{2,0},{3,1},{4,6},{5,7},{6,4},{7,5},{8,10},{9,11},{10,... | collective-permute-start | bytes 196616 | tf_op jit(solution)/shard_map/ppermute | solution.py:380
  11.3 7.3 %collective-permute-start.2 = (f32[32,512]{1,0:T(8,128)S(1)}, f32[32,512]{1,0:T(8,128)S(1)}, u32[]{:S(2)}, u32[]{:S(2)}) collective-permute-start(f32[32,512]{1,0:T(8,128)S(1)} %get-tuple-element.68), channel_id=1, source_target_pairs={{0,3},{1,0},{2,1},{3,2},{4,7},{5,4},{6,5},{7,6},{8,11},{9,8},{10,9... | collective-permute-start | bytes 196616 | tf_op jit(solution)/shard_map/ppermute | solution.py:380

commit v8 on v7

--- a/solution.py
+++ b/solution.py
@@ -45,6 +45,13 @@
 def pick(selector, values):
     high, low = split(values)
     return dot_plain(selector, jnp.concatenate([high, low], axis=0))
+
+
+def tree_sum(values):
+    while len(values) > 1:
+        pairs = [left + right for left, right in zip(values[::2], values[1::2])]
+        values = pairs + ([values[-1]] if len(values) % 2 else [])
+    return values[0]
 
 
 def column_sum(values):
@@ -667,16 +674,17 @@
                 rows = values.shape[0]
                 state_ref[at + number * rows : at + (number + 1) * rows, :] = values
 
-            total = sum_ref[...]
+            parts_of_total = [sum_ref[...]]
             pieces = []
             for sub_id in range(subs):
                 piece = jnp.zeros((widest, unknowns), F32)
                 for part_id in range(parts):
                     slot = sub_id * parts + part_id
                     own = part_ref[part_id : part_id + 1, :] > 0.5
-                    total = total + jnp.where(own, 0.0, arrived_ref[slot, 0:stat_rows, :])
+                    parts_of_total.append(jnp.where(own, 0.0, arrived_ref[slot, 0:stat_rows, :]))
                     piece = piece + jnp.where(own, arrived_ref[slot, 0:widest, :], 0.0)
                 pieces.append(piece)
+            total = tree_sum(parts_of_total)
             products = jnp.sum(total[coarse_rows : coarse_rows + step_id + 1], axis=1, keepdims=True)
             heads = [products[i : i + 1] for i in range(step_id)]
             square = products[step_id : step_id + 1]

time: 99.7 us -> 99.7 us (level)
  no operation moved by 1% of the time
where the time goes in v8:
time: 99.7 us; the launch traced here: 99.2 us
  blocking collectives  73.6 us (74%)
  Pallas kernels  14.8 us (15%)
  starting transfers between devices  10.7 us (11%)
    all_to_all x5, blocking collectives, on_device(): arrived = lax.all_to_all(slots, ('sub', 'coarse'), 0, 0)  51.4 us
    all_to_all x3, blocking collectives, on_device(): arrived = lax.all_to_all(outgoing, 'sub', 0, 0)  22.2 us
    pallas_call x10, Pallas kernels, call(): pl.pallas_call(kernel, out_shape=outs, in_specs=[pl.BlockSpec(memory_spac...  14.8 us
    ppermute x3, starting transfers between devices, on_device(): lax.ppermute(coarse_chunks[turn], 'coarse', [(i, (i + turn) % parts) for...  5.51 us
    all_to_all x1, starting transfers between devices, on_device(): arrived = lax.all_to_all(outgoing, 'sub', 0, 0)  5.18 us
  transfers between devices with their start and end apart: 4, of which 0 were waited for; matrix products, arithmetic and copies ran while one was open for 0% of the time, Pallas kernels for 6%

profile of v8, /device:TPU:0, one launch (start us, length us, event | category | flops | bytes accessed | tf_op | source)
XLA Modules:
  0.0 99.2 jit_solution(16017767460741465265)
XLA Ops:
  0.0 2.0 %begin.1 = (f32[8,32,128]{2,1,0:T(8,128)}, bf16[32,256]{1,0:T(8,128)(2,1)S(1)}, f32[32,128]{1,0:T(8,128)S(1)}, f32[32,128]{1,0:T(8,128)S(1)}, f32[128,128]{1,0:T...) custom-call(s32[4,8]{1,0:T(4,128)} %bitcast.15, ...), custom_call_target="tpu_custom_call" | custom-call | tf_op jit(solution)/shard_map/begin/pallas_call | solution.py:119
  2.0 5.2 %all-to-all-start = ((f32[8,32,128]{2,1,0:T(8,128)}), f32[8,32,128]{2,1,0:T(8,128)S(1)}, u32[]{:S(2)}, u32[]{:S(2)}) async-start(f32[8,32,128]{2,1,0:T(8,128)} %get-tuple-element.57.stat_ref), calls=%async_computation | async-start | bytes 262144 | tf_op jit(solution)/shard_map/all_to_all | solution.py:787
  7.2 1.6 %collective-permute-start = (f32[32,512]{1,0:T(8,128)S(1)}, f32[32,512]{1,0:T(8,128)S(1)}, u32[]{:S(2)}, u32[]{:S(2)}) collective-permute-start(f32[32,512]{1,0:T(8,128)S(1)} %get-tuple-element.66), channel_id=1, source_target_pairs={{0,1},{1,2},{2,3},{3,0},{4,5},{5,6},{6,7},{7,4},{8,9},{9,10},{10,1... | collective-permute-start | bytes 196616 | tf_op jit(solution)/shard_map/ppermute | solution.py:387
  8.7 2.6 %collective-permute-start.1 = (f32[32,512]{1,0:T(8,128)S(1)}, f32[32,512]{1,0:T(8,128)S(1)}, u32[]{:S(2)}, u32[]{:S(2)}) collective-permute-start(f32[32,512]{1,0:T(8,128)S(1)} %get-tuple-element.67), channel_id=1, source_target_pairs={{0,2},{1,3},{2,0},{3,1},{4,6},{5,7},{6,4},{7,5},{8,10},{9,11},{10,... | collective-permute-start | bytes 196616 | tf_op jit(solution)/shard_map/ppermute | solution.py:387
  11.3 1.3 %collective-permute-start.2 = (f32[32,512]{1,0:T(8,128)S(1)}, f32[32,512]{1,0:T(8,128)S(1)}, u32[]{:S(2)}, u32[]{:S(2)}) collective-permute-start(f32[32,512]{1,0:T(8,128)S(1)} %get-tuple-element.68), channel_id=1, source_target_pairs={{0,3},{1,0},{2,1},{3,2},{4,7},{5,4},{6,5},{7,6},{8,11},{9,8},{10,9... | collective-permute-start | bytes 196616 | tf_op jit(solution)/shard_map/ppermute | solution.py:387
  12.7 0.0 all-to-all-done.arrived_ref
  12.7 5.9 %smooth0.1 = (f32[128,128]{1,0:T(8,128)S(1)}, f32[32,8,128]{2,1,0:T(8,128)S(1)}, f32[8,128]{1,0:T(8,128)S(1)}, f32[32,128]{1,0:T(8,128)S(1)}, f32[1,32,128]{2,1,...) custom-call(f32[8,32,128]{2,1,0:T(8,128)S(1)} %all-to-all-done.arriv, ...), custom_call_target="tpu_custom_call" | custom-call | tf_op jit(solution)/shard_map/smooth0/pallas_call | solution.py:119
  18.6 0.0 collective-permute-done.refs_19_
  18.6 12.2 %all_to_all.45.refs_0_ = f32[32,8,128]{2,1,0:T(8,128)S(1)} all-to-all(f32[32,8,128]{2,1,0:T(8,128)S(1)} %get-tuple-element.69), channel_id=1, replica_groups=mesh['sub'=8,'coarse'=4] {'sub','coarse'}, dimensions={0} | all-to-all | bytes 262144 | tf_op jit(solution)/shard_map/all_to_all | solution.py:857
  30.8 0.5 advance0.1
  31.3 7.4 %all_to_all.46.arrived_ref = f32[8,16,128]{2,1,0:T(8,128)S(1)} all-to-all(f32[8,16,128]{2,1,0:T(8,128)S(1)} %get-tuple-element.87.stat_ref), channel_id=1, replica_groups=mesh['sub'=8,'coarse'=4] {'sub'}, dimensions={0} | all-to-all | bytes 131072 | tf_op jit(solution)/shard_map/all_to_all | solution.py:787
  38.7 1.4 %smooth1.1 = (f32[128,128]{1,0:T(8,128)S(1)}, f32[32,8,128]{2,1,0:T(8,128)S(1)}, f32[8,128]{1,0:T(8,128)S(1)}) custom-call(f32[8,16,128]{2,1,0:T(8,128)S(1)} %all_to_all.46.arrived_ref, f32[128,128]{1,0:T(8,128)S(1)} %get-tuple-element.88.vector_ref.refs_3_, bf16[48,256,256]{2,1,0:T(8,128)(2,1)S(1)} %get-tuple-element.89.weight_ref, ...), custom_call_target="tpu_custom_call" | custom-call | tf_op jit(solution)/shard_map/smooth1/pallas_call | solution.py:119
  40.1 10.1 %all_to_all.47.refs_0_ = f32[32,8,128]{2,1,0:T(8,128)S(1)} all-to-all(f32[32,8,128]{2,1,0:T(8,128)S(1)} %get-tuple-element.91), channel_id=1, replica_groups=mesh['sub'=8,'coarse'=4] {'sub','coarse'}, dimensions={0} | all-to-all | bytes 262144 | tf_op jit(solution)/shard_map/all_to_all | solution.py:857
  50.2 0.5 advance1.1
  50.7 7.4 %all_to_all.48.arrived_ref = f32[8,16,128]{2,1,0:T(8,128)S(1)} all-to-all(f32[8,16,128]{2,1,0:T(8,128)S(1)} %get-tuple-element.95.stat_ref), channel_id=1, replica_groups=mesh['sub'=8,'coarse'=4] {'sub'}, dimensions={0} | all-to-all | bytes 131072 | tf_op jit(solution)/shard_map/all_to_all | solution.py:787
  58.1 1.4 %smooth2.1 = (f32[128,128]{1,0:T(8,128)S(1)}, f32[32,8,128]{2,1,0:T(8,128)S(1)}, f32[8,128]{1,0:T(8,128)S(1)}) custom-call(f32[8,16,128]{2,1,0:T(8,128)S(1)} %all_to_all.48.arrived_ref, f32[128,128]{1,0:T(8,128)S(1)} %get-tuple-element.96.vector_ref.refs_3_, bf16[48,256,256]{2,1,0:T(8,128)(2,1)S(1)} %get-tuple-element.89.weight_ref, ...), custom_call_target="tpu_custom_call" | custom-call | tf_op jit(solution)/shard_map/smooth2/pallas_call | solution.py:119
  59.5 10.1 %all_to_all.49.refs_0_ = f32[32,8,128]{2,1,0:T(8,128)S(1)} all-to-all(f32[32,8,128]{2,1,0:T(8,128)S(1)} %get-tuple-element.97), channel_id=1, replica_groups=mesh['sub'=8,'coarse'=4] {'sub','coarse'}, dimensions={0} | all-to-all | bytes 262144 | tf_op jit(solution)/shard_map/all_to_all | solution.py:857
  69.6 0.5 advance2.1
  70.1 7.4 %all_to_all.50.arrived_ref = f32[8,16,128]{2,1,0:T(8,128)S(1)} all-to-all(f32[8,16,128]{2,1,0:T(8,128)S(1)} %get-tuple-element.101.stat_ref), channel_id=1, replica_groups=mesh['sub'=8,'coarse'=4] {'sub'}, dimensions={0} | all-to-all | bytes 131072 | tf_op jit(solution)/shard_map/all_to_all | solution.py:787
  77.5 1.4 %smooth3.1 = (f32[128,128]{1,0:T(8,128)S(1)}, f32[32,8,128]{2,1,0:T(8,128)S(1)}, f32[8,128]{1,0:T(8,128)S(1)}) custom-call(f32[8,16,128]{2,1,0:T(8,128)S(1)} %all_to_all.50.arrived_ref, f32[128,128]{1,0:T(8,128)S(1)} %get-tuple-element.102.vector_ref.refs_3_, bf16[48,256,256]{2,1,0:T(8,128)(2,1)S(1)} %get-tuple-element.89.weight_ref, ...), custom_call_target="tpu_custom_call" | custom-call | tf_op jit(solution)/shard_map/smooth3/pallas_call | solution.py:119
  78.9 10.1 %all_to_all.51.refs_0_ = f32[32,8,128]{2,1,0:T(8,128)S(1)} all-to-all(f32[32,8,128]{2,1,0:T(8,128)S(1)} %get-tuple-element.103), channel_id=1, replica_groups=mesh['sub'=8,'coarse'=4] {'sub','coarse'}, dimensions={0} | all-to-all | bytes 262144 | tf_op jit(solution)/shard_map/all_to_all | solution.py:857
  89.0 0.5 advance3.1
  89.5 8.9 %all_to_all.52.arrived_ref = f32[32,1,128]{2,1,0:T(1,128)S(1)} all-to-all(f32[32,1,128]{2,1,0:T(1,128)S(1)} %get-tuple-element.107), channel_id=1, replica_groups=mesh['sub'=8,'coarse'=4] {'sub','coarse'}, dimensions={0} | all-to-all | bytes 32768 | tf_op jit(solution)/shard_map/all_to_all | solution.py:892
  98.3 0.9 finish.1
  (2 shorter events, 0.0 us)
Async XLA Ops:
  2.0 10.7 %all-to-all-start = ((f32[8,32,128]{2,1,0:T(8,128)}), f32[8,32,128]{2,1,0:T(8,128)S(1)}, u32[]{:S(2)}, u32[]{:S(2)}) async-start(f32[8,32,128]{2,1,0:T(8,128)} %get-tuple-element.57.stat_ref), calls=%async_computation | async-start | bytes 262144 | tf_op jit(solution)/shard_map/all_to_all | solution.py:787
  7.2 11.5 %collective-permute-start = (f32[32,512]{1,0:T(8,128)S(1)}, f32[32,512]{1,0:T(8,128)S(1)}, u32[]{:S(2)}, u32[]{:S(2)}) collective-permute-start(f32[32,512]{1,0:T(8,128)S(1)} %get-tuple-element.66), channel_id=1, source_target_pairs={{0,1},{1,2},{2,3},{3,0},{4,5},{5,6},{6,7},{7,4},{8,9},{9,10},{10,1... | collective-permute-start | bytes 196616 | tf_op jit(solution)/shard_map/ppermute | solution.py:387
  8.7 9.9 %collective-permute-start.1 = (f32[32,512]{1,0:T(8,128)S(1)}, f32[32,512]{1,0:T(8,128)S(1)}, u32[]{:S(2)}, u32[]{:S(2)}) collective-permute-start(f32[32,512]{1,0:T(8,128)S(1)} %get-tuple-element.67), channel_id=1, source_target_pairs={{0,2},{1,3},{2,0},{3,1},{4,6},{5,7},{6,4},{7,5},{8,10},{9,11},{10,... | collective-permute-start | bytes 196616 | tf_op jit(solution)/shard_map/ppermute | solution.py:387
  11.3 7.3 %collective-permute-start.2 = (f32[32,512]{1,0:T(8,128)S(1)}, f32[32,512]{1,0:T(8,128)S(1)}, u32[]{:S(2)}, u32[]{:S(2)}) collective-permute-start(f32[32,512]{1,0:T(8,128)S(1)} %get-tuple-element.68), channel_id=1, source_target_pairs={{0,3},{1,0},{2,1},{3,2},{4,7},{5,4},{6,5},{7,6},{8,11},{9,8},{10,9... | collective-permute-start | bytes 196616 | tf_op jit(solution)/shard_map/ppermute | solution.py:387

commit v9 on v8

--- a/solution.py
+++ b/solution.py
@@ -87,12 +87,12 @@
 def gather_rounds(slots, route, rounds):
     pieces = []
     for round_id in range(rounds):
-        total = None
-        for sub_id, piece in enumerate(slots):
-            at = round_id * len(slots) + sub_id
-            term = route[at : at + 1] * piece
-            total = term if total is None else total + term
-        pieces.append(total)
+        at = round_id * len(slots)
+        pieces.append(
+            tree_sum(
+                [route[at + sub_id : at + sub_id + 1] * piece for sub_id, piece in enumerate(slots)]
+            )
+        )
     return jnp.concatenate(pieces, axis=0)
 
 
@@ -390,10 +390,9 @@
 
     def put(target_value, values):
         high, low = split(values)
-        pieces = [high, low]
-        if table_rows > 2 * margin_rows:
-            pieces.append(jnp.zeros((table_rows - 2 * margin_rows, unknowns), BF16))
-        return dot_plain(target_value, jnp.concatenate(pieces, axis=0))
+        return dot_plain(
+            target_value[:, : 2 * margin_rows], jnp.concatenate([high, low], axis=0)
+        )
 
     def smooth_rest(arrived_ref, out, target, selector, route, part_ref, stat_ref, slot_ref, sum_ref):
         slots = spread_rounds(pick(selector, out), route, subs, rounds)

time: 99.7 us -> 99.8 us (level)
  no operation moved by 1% of the time
where the time goes in v9:
time: 99.8 us; the launch traced here: 99.3 us
  blocking collectives  73.6 us (74%)
  Pallas kernels  14.9 us (15%)
  starting transfers between devices  10.7 us (11%)
    all_to_all x5, blocking collectives, on_device(): arrived = lax.all_to_all(slots, ('sub', 'coarse'), 0, 0)  51.4 us
    all_to_all x3, blocking collectives, on_device(): arrived = lax.all_to_all(outgoing, 'sub', 0, 0)  22.2 us
    pallas_call x10, Pallas kernels, call(): pl.pallas_call(kernel, out_shape=outs, in_specs=[pl.BlockSpec(memory_spac...  14.9 us
    ppermute x3, starting transfers between devices, on_device(): lax.ppermute(coarse_chunks[turn], 'coarse', [(i, (i + turn) % parts) for...  5.51 us
    all_to_all x1, starting transfers between devices, on_device(): arrived = lax.all_to_all(outgoing, 'sub', 0, 0)  5.18 us
  transfers between devices with their start and end apart: 4, of which 0 were waited for; matrix products, arithmetic and copies ran while one was open for 0% of the time, Pallas kernels for 6%

profile of v9, /device:TPU:0, one launch (start us, length us, event | category | flops | bytes accessed | tf_op | source)
XLA Modules:
  0.0 99.3 jit_solution(12978214635204519987)
XLA Ops:
  0.0 2.0 %begin.1 = (f32[8,32,128]{2,1,0:T(8,128)}, bf16[32,256]{1,0:T(8,128)(2,1)S(1)}, f32[32,128]{1,0:T(8,128)S(1)}, f32[32,128]{1,0:T(8,128)S(1)}, f32[128,128]{1,0:T...) custom-call(s32[4,8]{1,0:T(4,128)} %bitcast.15, ...), custom_call_target="tpu_custom_call" | custom-call | tf_op jit(solution)/shard_map/begin/pallas_call | solution.py:119
  2.0 5.2 %all-to-all-start = ((f32[8,32,128]{2,1,0:T(8,128)}), f32[8,32,128]{2,1,0:T(8,128)S(1)}, u32[]{:S(2)}, u32[]{:S(2)}) async-start(f32[8,32,128]{2,1,0:T(8,128)} %get-tuple-element.57.stat_ref), calls=%async_computation | async-start | bytes 262144 | tf_op jit(solution)/shard_map/all_to_all | solution.py:786
  7.2 1.6 %collective-permute-start = (f32[32,512]{1,0:T(8,128)S(1)}, f32[32,512]{1,0:T(8,128)S(1)}, u32[]{:S(2)}, u32[]{:S(2)}) collective-permute-start(f32[32,512]{1,0:T(8,128)S(1)} %get-tuple-element.66), channel_id=1, source_target_pairs={{0,1},{1,2},{2,3},{3,0},{4,5},{5,6},{6,7},{7,4},{8,9},{9,10},{10,1... | collective-permute-start | bytes 196616 | tf_op jit(solution)/shard_map/ppermute | solution.py:387
  8.7 2.6 %collective-permute-start.1 = (f32[32,512]{1,0:T(8,128)S(1)}, f32[32,512]{1,0:T(8,128)S(1)}, u32[]{:S(2)}, u32[]{:S(2)}) collective-permute-start(f32[32,512]{1,0:T(8,128)S(1)} %get-tuple-element.67), channel_id=1, source_target_pairs={{0,2},{1,3},{2,0},{3,1},{4,6},{5,7},{6,4},{7,5},{8,10},{9,11},{10,... | collective-permute-start | bytes 196616 | tf_op jit(solution)/shard_map/ppermute | solution.py:387
  11.3 1.3 %collective-permute-start.2 = (f32[32,512]{1,0:T(8,128)S(1)}, f32[32,512]{1,0:T(8,128)S(1)}, u32[]{:S(2)}, u32[]{:S(2)}) collective-permute-start(f32[32,512]{1,0:T(8,128)S(1)} %get-tuple-element.68), channel_id=1, source_target_pairs={{0,3},{1,0},{2,1},{3,2},{4,7},{5,4},{6,5},{7,6},{8,11},{9,8},{10,9... | collective-permute-start | bytes 196616 | tf_op jit(solution)/shard_map/ppermute | solution.py:387
  12.7 0.0 all-to-all-done.arrived_ref
  12.7 6.0 %smooth0.1 = (f32[128,128]{1,0:T(8,128)S(1)}, f32[32,8,128]{2,1,0:T(8,128)S(1)}, f32[8,128]{1,0:T(8,128)S(1)}, f32[32,128]{1,0:T(8,128)S(1)}, f32[1,32,128]{2,1,...) custom-call(f32[8,32,128]{2,1,0:T(8,128)S(1)} %all-to-all-done.arriv, ...), custom_call_target="tpu_custom_call" | custom-call | tf_op jit(solution)/shard_map/smooth0/pallas_call | solution.py:119
  18.7 0.0 collective-permute-done.refs_19_
  18.7 12.2 %all_to_all.45.refs_0_ = f32[32,8,128]{2,1,0:T(8,128)S(1)} all-to-all(f32[32,8,128]{2,1,0:T(8,128)S(1)} %get-tuple-element.69), channel_id=1, replica_groups=mesh['sub'=8,'coarse'=4] {'sub','coarse'}, dimensions={0} | all-to-all | bytes 262144 | tf_op jit(solution)/shard_map/all_to_all | solution.py:856
  30.9 0.5 advance0.1
  31.4 7.4 %all_to_all.46.arrived_ref = f32[8,16,128]{2,1,0:T(8,128)S(1)} all-to-all(f32[8,16,128]{2,1,0:T(8,128)S(1)} %get-tuple-element.87.stat_ref), channel_id=1, replica_groups=mesh['sub'=8,'coarse'=4] {'sub'}, dimensions={0} | all-to-all | bytes 131072 | tf_op jit(solution)/shard_map/all_to_all | solution.py:786
  38.8 1.4 %smooth1.1 = (f32[128,128]{1,0:T(8,128)S(1)}, f32[32,8,128]{2,1,0:T(8,128)S(1)}, f32[8,128]{1,0:T(8,128)S(1)}) custom-call(f32[8,16,128]{2,1,0:T(8,128)S(1)} %all_to_all.46.arrived_ref, f32[128,128]{1,0:T(8,128)S(1)} %get-tuple-element.88.vector_ref.refs_3_, bf16[48,256,256]{2,1,0:T(8,128)(2,1)S(1)} %get-tuple-element.89.weight_ref, ...), custom_call_target="tpu_custom_call" | custom-call | tf_op jit(solution)/shard_map/smooth1/pallas_call | solution.py:119
  40.2 10.1 %all_to_all.47.refs_0_ = f32[32,8,128]{2,1,0:T(8,128)S(1)} all-to-all(f32[32,8,128]{2,1,0:T(8,128)S(1)} %get-tuple-element.91), channel_id=1, replica_groups=mesh['sub'=8,'coarse'=4] {'sub','coarse'}, dimensions={0} | all-to-all | bytes 262144 | tf_op jit(solution)/shard_map/all_to_all | solution.py:856
  50.3 0.5 advance1.1
  50.8 7.4 %all_to_all.48.arrived_ref = f32[8,16,128]{2,1,0:T(8,128)S(1)} all-to-all(f32[8,16,128]{2,1,0:T(8,128)S(1)} %get-tuple-element.95.stat_ref), channel_id=1, replica_groups=mesh['sub'=8,'coarse'=4] {'sub'}, dimensions={0} | all-to-all | bytes 131072 | tf_op jit(solution)/shard_map/all_to_all | solution.py:786
  58.2 1.4 %smooth2.1 = (f32[128,128]{1,0:T(8,128)S(1)}, f32[32,8,128]{2,1,0:T(8,128)S(1)}, f32[8,128]{1,0:T(8,128)S(1)}) custom-call(f32[8,16,128]{2,1,0:T(8,128)S(1)} %all_to_all.48.arrived_ref, f32[128,128]{1,0:T(8,128)S(1)} %get-tuple-element.96.vector_ref.refs_3_, bf16[48,256,256]{2,1,0:T(8,128)(2,1)S(1)} %get-tuple-element.89.weight_ref, ...), custom_call_target="tpu_custom_call" | custom-call | tf_op jit(solution)/shard_map/smooth2/pallas_call | solution.py:119
  59.6 10.1 %all_to_all.49.refs_0_ = f32[32,8,128]{2,1,0:T(8,128)S(1)} all-to-all(f32[32,8,128]{2,1,0:T(8,128)S(1)} %get-tuple-element.97), channel_id=1, replica_groups=mesh['sub'=8,'coarse'=4] {'sub','coarse'}, dimensions={0} | all-to-all | bytes 262144 | tf_op jit(solution)/shard_map/all_to_all | solution.py:856
  69.7 0.5 advance2.1
  70.2 7.4 %all_to_all.50.arrived_ref = f32[8,16,128]{2,1,0:T(8,128)S(1)} all-to-all(f32[8,16,128]{2,1,0:T(8,128)S(1)} %get-tuple-element.101.stat_ref), channel_id=1, replica_groups=mesh['sub'=8,'coarse'=4] {'sub'}, dimensions={0} | all-to-all | bytes 131072 | tf_op jit(solution)/shard_map/all_to_all | solution.py:786
  77.6 1.4 %smooth3.1 = (f32[128,128]{1,0:T(8,128)S(1)}, f32[32,8,128]{2,1,0:T(8,128)S(1)}, f32[8,128]{1,0:T(8,128)S(1)}) custom-call(f32[8,16,128]{2,1,0:T(8,128)S(1)} %all_to_all.50.arrived_ref, f32[128,128]{1,0:T(8,128)S(1)} %get-tuple-element.102.vector_ref.refs_3_, bf16[48,256,256]{2,1,0:T(8,128)(2,1)S(1)} %get-tuple-element.89.weight_ref, ...), custom_call_target="tpu_custom_call" | custom-call | tf_op jit(solution)/shard_map/smooth3/pallas_call | solution.py:119
  79.0 10.1 %all_to_all.51.refs_0_ = f32[32,8,128]{2,1,0:T(8,128)S(1)} all-to-all(f32[32,8,128]{2,1,0:T(8,128)S(1)} %get-tuple-element.103), channel_id=1, replica_groups=mesh['sub'=8,'coarse'=4] {'sub','coarse'}, dimensions={0} | all-to-all | bytes 262144 | tf_op jit(solution)/shard_map/all_to_all | solution.py:856
  89.1 0.5 advance3.1
  89.6 8.9 %all_to_all.52.arrived_ref = f32[32,1,128]{2,1,0:T(1,128)S(1)} all-to-all(f32[32,1,128]{2,1,0:T(1,128)S(1)} %get-tuple-element.107), channel_id=1, replica_groups=mesh['sub'=8,'coarse'=4] {'sub','coarse'}, dimensions={0} | all-to-all | bytes 32768 | tf_op jit(solution)/shard_map/all_to_all | solution.py:891
  98.4 0.9 finish.1
  (2 shorter events, 0.0 us)
Async XLA Ops:
  2.0 10.7 %all-to-all-start = ((f32[8,32,128]{2,1,0:T(8,128)}), f32[8,32,128]{2,1,0:T(8,128)S(1)}, u32[]{:S(2)}, u32[]{:S(2)}) async-start(f32[8,32,128]{2,1,0:T(8,128)} %get-tuple-element.57.stat_ref), calls=%async_computation | async-start | bytes 262144 | tf_op jit(solution)/shard_map/all_to_all | solution.py:786
  7.2 11.5 %collective-permute-start = (f32[32,512]{1,0:T(8,128)S(1)}, f32[32,512]{1,0:T(8,128)S(1)}, u32[]{:S(2)}, u32[]{:S(2)}) collective-permute-start(f32[32,512]{1,0:T(8,128)S(1)} %get-tuple-element.66), channel_id=1, source_target_pairs={{0,1},{1,2},{2,3},{3,0},{4,5},{5,6},{6,7},{7,4},{8,9},{9,10},{10,1... | collective-permute-start | bytes 196616 | tf_op jit(solution)/shard_map/ppermute | solution.py:387
  8.7 10.0 %collective-permute-start.1 = (f32[32,512]{1,0:T(8,128)S(1)}, f32[32,512]{1,0:T(8,128)S(1)}, u32[]{:S(2)}, u32[]{:S(2)}) collective-permute-start(f32[32,512]{1,0:T(8,128)S(1)} %get-tuple-element.67), channel_id=1, source_target_pairs={{0,2},{1,3},{2,0},{3,1},{4,6},{5,7},{6,4},{7,5},{8,10},{9,11},{10,... | collective-permute-start | bytes 196616 | tf_op jit(solution)/shard_map/ppermute | solution.py:387
  11.3 7.4 %collective-permute-start.2 = (f32[32,512]{1,0:T(8,128)S(1)}, f32[32,512]{1,0:T(8,128)S(1)}, u32[]{:S(2)}, u32[]{:S(2)}) collective-permute-start(f32[32,512]{1,0:T(8,128)S(1)} %get-tuple-element.68), channel_id=1, source_target_pairs={{0,3},{1,0},{2,1},{3,2},{4,7},{5,4},{6,5},{7,6},{8,11},{9,8},{10,9... | collective-permute-start | bytes 196616 | tf_op jit(solution)/shard_map/ppermute | solution.py:387
